TPU v7x, 128 devices: a whole 4x4x4 slice. The times are simulated.
128 devices in a mesh: row: 16 (over z, y), col: 8 (over x, core).
Axes of the slice: x: 4, y: 4, z: 4, core: 2. Of those that a mesh axis runs over, the one named last changes fastest.
Arguments:
- queries: bfloat16 [2048, 8192], P('row', 'col'), may hold values from -42 to 42
- new_keys: bfloat16 [2048, 1024], P('row', 'col'), may hold values from -12 to 12
- new_values: bfloat16 [2048, 1024], P('row', 'col'), may hold values from -8 to 8
- key_cache: bfloat16 [2048, 256, 1024], P('row', None, 'col'), may hold values from -4 to 4
- value_cache: bfloat16 [2048, 256, 1024], P('row', None, 'col'), may hold values from -4 to 4
- residual: bfloat16 [2048, 8192], P('row', 'col'), may hold values from -3 to 3
- out_weight: bfloat16 [8192, 8192], P('row', 'col'), may hold values from -0.0625 to 0.0625
- tenant: int32 [2048], P('row'), may hold values from 0 to 127, as said below
- tenant_slot_index: int32 [128], replicated, may hold values from 0 to 127, each once
- read_bank: bfloat16 [2, 128, 64, 8192], P(None, 'row', None, 'col'), may hold values from -0.0625 to 0.0625
- write_bank: bfloat16 [2, 128, 64, 8192], P(None, 'row', None, 'col'), may hold values from -0.375 to 0.375
- mean_bank: bfloat16 [2, 128, 8192], P(None, 'row', 'col'), may hold values from -1.25 to 1.25
Outputs:
- erased_out: bfloat16 [2048, 8192], P('row', 'col')
Inputs may be any that keep to these rules, and one draw needn't show every extreme that they name: In each aligned block of 128 rows (the rows of one index of row) no tenant appears more than 3 times, and some tenant appears exactly 3 times in every block. `tenant_slot_index`: each bank slot belongs to exactly one tenant.
All inputs are finite; a program needn't handle non-finite values.
Results may differ from a plain program's by a relative error of at most 0.012.
Values may be sent and summed in bfloat16 or wider, within the bound.
No kernel may reach another device: no remote copies, remote signals or barrier semaphores. Data moves between devices by JAX's collectives and lax.ppermute only.
A program may use at most 128 MiB of HBM per device.

v0:
```python
import math

import jax
import jax.numpy as jnp
from jax import lax
from jax.sharding import PartitionSpec as P

HEADS = 64
KVH = 8
HD = 128
MOST = 3


def rounded(values):
    return lax.optimization_barrier(values.astype(jnp.bfloat16))


def attention(queries, new_keys, new_values, key_cache, value_cache):
    row_count = queries.shape[0]
    kv_local = new_keys.shape[1] // HD
    group_size = HEADS // KVH
    history = key_cache.shape[1]
    logit_scale = 1.0 / math.sqrt(HD)
    heads_of_query = queries.reshape(row_count, kv_local, group_size, HD)
    past_keys = key_cache.reshape(row_count, history, kv_local, HD)
    past_values = value_cache.reshape(row_count, history, kv_local, HD)
    current_keys = new_keys.reshape(row_count, kv_local, HD)
    own_values = new_values.reshape(row_count, kv_local, HD)
    past_scores = (
        jnp.einsum("bkgd,blkd->bkgl", heads_of_query, past_keys, preferred_element_type=jnp.float32)
        * logit_scale
    )
    current_scores = (
        jnp.einsum(
            "qivl,qil->qiv", heads_of_query, current_keys, preferred_element_type=jnp.float32
        )
        * logit_scale
    )
    highest = jnp.maximum(jnp.max(past_scores, axis=-1), current_scores)
    past_exp = jnp.exp(past_scores - highest[..., None])
    own_exp = jnp.exp(current_scores - highest)
    denominator = jnp.sum(past_exp, axis=-1) + own_exp
    past_weights = (past_exp / denominator[..., None]).astype(jnp.bfloat16)
    own_weights = rounded(own_exp / denominator)
    mixed_output = jnp.einsum(
        "bkgl,blkd->bkgd", past_weights, past_values, preferred_element_type=jnp.float32
    )
    mixed_output = (
        mixed_output
        + own_weights.astype(jnp.float32)[..., None] * own_values.astype(jnp.float32)[:, :, None, :]
    )
    return mixed_output.reshape(row_count, kv_local * group_size * HD).astype(jnp.bfloat16)


def placement_table(tenant, tenant_slot_index):
    row_count = tenant.shape[0]
    slot_total = tenant_slot_index.shape[0]
    tenant_ids = jnp.arange(slot_total, dtype=jnp.int32)
    slot_of = jnp.sum(
        jnp.where(tenant[:, None] == tenant_ids[None, :], tenant_slot_index[None, :], 0), axis=1
    )
    positions = jnp.arange(row_count, dtype=jnp.int32)
    same_tenant = (tenant[:, None] == tenant[None, :]) & (positions[None, :] < positions[:, None])
    rank_within = jnp.sum(same_tenant.astype(jnp.int32), axis=1)
    target = slot_of * MOST + rank_within
    buffer_ids = jnp.arange(slot_total * MOST, dtype=jnp.int32)
    return (buffer_ids[:, None] == target[None, :]).astype(jnp.bfloat16)


def erase(values, slot_table, read_bank, write_bank, mean_bank, site_index):
    feat_width = values.shape[1]
    owners = lax.axis_size("row")
    slot_local = read_bank.shape[1]
    reader = read_bank[site_index]
    writer = write_bank[site_index]
    centre = mean_bank[site_index].astype(jnp.float32)
    packed = jnp.dot(slot_table, values, preferred_element_type=jnp.float32).astype(jnp.bfloat16)
    packed = packed.reshape(owners, slot_local, MOST, feat_width)
    centered = (
        lax.all_to_all(packed, "row", split_axis=0, concat_axis=0, tiled=True).astype(jnp.float32)
        - centre[None, :, None, :]
    ).astype(jnp.bfloat16)
    partial_value = jnp.einsum(
        "stmw,tkw->stmk", centered, reader, preferred_element_type=jnp.float32
    )
    coefficients = lax.psum(partial_value, "col").astype(jnp.bfloat16)
    deltas = jnp.einsum(
        "stmk,tkw->stmw", coefficients, writer, preferred_element_type=jnp.float32
    ).astype(jnp.bfloat16)
    result_rows = lax.all_to_all(deltas, "row", split_axis=0, concat_axis=0, tiled=True)
    result_rows = result_rows.reshape(owners * slot_local * MOST, feat_width)
    delta_rows = lax.dot_general(
        slot_table, result_rows, (((0,), (0,)), ((), ())), preferred_element_type=jnp.float32
    )
    return (values.astype(jnp.float32) - delta_rows).astype(jnp.bfloat16)


def local(
    queries,
    new_keys,
    new_values,
    key_cache,
    value_cache,
    residual,
    out_weight,
    tenant,
    tenant_slot_index,
    read_bank,
    write_bank,
    mean_bank,
):
    slot_table = placement_table(tenant, tenant_slot_index)
    attended = attention(queries, new_keys, new_values, key_cache, value_cache)
    cleaned = erase(attended, slot_table, read_bank, write_bank, mean_bank, 0)
    full_rows = lax.all_gather(cleaned, "col", axis=1, tiled=True)
    regrouped = lax.all_to_all(full_rows, "row", split_axis=1, concat_axis=0, tiled=True)
    projected = lax.psum_scatter(
        jnp.dot(regrouped, out_weight, preferred_element_type=jnp.float32),
        "row",
        scatter_dimension=0,
        tiled=True,
    )
    hidden = (residual.astype(jnp.float32) + projected).astype(jnp.bfloat16)
    return erase(hidden, slot_table, read_bank, write_bank, mean_bank, 1)


def solution(mesh):
    return jax.shard_map(
        local,
        mesh=mesh,
        in_specs=(
            P("row", "col"),
            P("row", "col"),
            P("row", "col"),
            P("row", None, "col"),
            P("row", None, "col"),
            P("row", "col"),
            P("row", "col"),
            P("row"),
            P(),
            P(None, "row", None, "col"),
            P(None, "row", None, "col"),
            P(None, "row", "col"),
        ),
        out_specs=P("row", "col"),
        check_vma=False,
    )
```

profile of v0, /device:TPU:0, one launch (start us, length us, event | category | flops | bytes accessed | tf_op | source)
XLA Modules:
  0.0 310.5 jit_solution(9428337877540961581)
XLA Ops:
  6.5 0.9 convert_element_type.103
  7.4 1.0 copy.48
  8.4 1.0 fusion.26
  9.5 5.9 %fusion.31 = (f32[128,8]{1,0:T(8,128)S(1)}, f32[128,8,256]{2,1,0:T(8,128)S(1)}) fusion(bf16[128,8,128]{2,1,0:T(8,128)(2,1)S(1)} %bitcast.74, bf16[128,256,128]{2,1,0:T(8,128)(2,1)} %param.15), kind=kOutput, calls=%fused_computation.59 | convolution fusion | flops 67632128 | bytes 9703424 | tf_op jit(solution)/shard_map/bkgd,blkd->bkgl/dot_general | solution.py:30
  16.0 1.4 fusion.4
  18.3 1.2 copy.32
  19.5 8.1 %all-to-all-start = ((bf16[16,8,3,1024]{3,1,2,0:T(8,128)(2,1)}), bf16[16,8,3,1024]{3,1,2,0:T(8,128)(2,1)S(1)}, u32[]{:S(2)}, u32[]{:S(2)}) async-start(bf16[16,8,3,1024]{3,1,2,0:T(8,128)(2,1)} %copy.32), calls=%async_computation | async-start | bytes 1572864 | tf_op jit(solution)/shard_map/all_to_all | solution.py:80
  27.8 14.4 %all-to-all-done = bf16[16,8,3,1024]{3,1,2,0:T(8,128)(2,1)S(1)} async-done(((bf16[16,8,3,1024]{3,1,2,0:T(8,128)(2,1)}), bf16[16,8,3,1024]{3,1,2,0:T(8,128)(2,1)S(1)}, u32[]{:S(2)}, u32[]{:S(2)}) %all-to-all-start) | async-done | bytes 786464 | tf_op jit(solution)/shard_map/all_to_all | solution.py:80
  42.4 2.7 convolution_bitcast_fusion.1
  45.1 26.5 %psum.14 = bf16[16,8,3,64]{3,0,2,1:T(8,128)(2,1)S(1)} all-reduce(f32[16,8,3,64]{3,0,2,1:T(8,128)} %convolution_bitcast_fusion.1), channel_id=1, replica_groups=mesh['row'=16,'col'=8] {'col'}, use_global_device_ids=true, to_apply=%region_4.5 | all-reduce | flops 24576 | bytes 147456 | tf_op jit(solution)/shard_map/psum | solution.py:86
  72.4 15.4 %all_to_all.39 = bf16[16,8,3,1024]{3,1,2,0:T(8,128)(2,1)S(1)} all-to-all(bf16[16,8,3,1024]{3,1,2,0:T(8,128)(2,1)S(1)} %copy.34), channel_id=1, replica_groups=mesh['row'=16,'col'=8] {'row'}, dimensions={0} | all-to-all | bytes 1572864 | tf_op jit(solution)/shard_map/all_to_all | solution.py:90
  88.5 0.7 reshape.102
  89.2 1.1 fusion.2
  90.3 23.1 %all-gather.2.cloned.1.call-done = bf16[128,8192]{1,0:T(8,128)(2,1)} async-done(((bf16[128,1024]{1,0:T(8,128)(2,1)}), bf16[128,8192]{1,0:T(8,128)(2,1)}) %all-gather.2.cloned.1.call-update) | async-done | bytes 2097168 | tf_op jit(solution)/shard_map/all_gather | solution.py:115
  113.4 1.8 copy.62
  115.2 35.6 %all_to_all.40 = bf16[128,16,512]{2,0,1:T(8,128)(2,1)S(1)} all-to-all(bf16[128,16,512]{2,0,1:T(8,128)(2,1)S(1)} %bitcast.70), channel_id=1, replica_groups=mesh['row'=16,'col'=8] {'row'}, dimensions={1} | all-to-all | bytes 4194304 | tf_op jit(solution)/shard_map/all_to_all | solution.py:116
  150.8 5.6 %fusion.32 = f32[2048,1024]{1,0:T(8,128)} fusion(bf16[2048,512]{1,0:T(8,128)(2,1)S(1)} %bitcast.72, bf16[512,1024]{1,0:T(8,128)(2,1)S(1)} %copy-done), kind=kOutput, calls=%fused_computation.60 | convolution fusion | flops 2147483648 | bytes 11534336 | tf_op jit(solution)/shard_map/dot_general | solution.py:118
  156.5 81.5 %reduce-scatter.2.cloned.1.call-done = f32[128,1024]{1,0:T(8,128)} async-done(((f32[2048,1024]{1,0:T(8,128)}), f32[128,1024]{1,0:T(8,128)}) %reduce-scatter.2.cloned.1.call-update) | async-done | bytes 524304 | tf_op jit(solution)/shard_map/reduce_scatter | solution.py:117
  238.0 1.4 convolution_convert_fusion.1
  240.3 18.2 %all_to_all.41 = bf16[16,8,3,1024]{3,1,2,0:T(8,128)(2,1)S(1)} all-to-all(bf16[16,8,3,1024]{3,1,2,0:T(8,128)(2,1)S(1)} %copy.37), channel_id=1, replica_groups=mesh['row'=16,'col'=8] {'row'}, dimensions={0} | all-to-all | bytes 1572864 | tf_op jit(solution)/shard_map/all_to_all | solution.py:80
  259.3 25.4 %psum.15 = bf16[16,8,3,64]{3,0,2,1:T(8,128)(2,1)S(1)} all-reduce(f32[16,8,3,64]{3,0,2,1:T(8,128)S(1)} %convolution_bitcast_fusion), channel_id=1, replica_groups=mesh['row'=16,'col'=8] {'col'}, use_global_device_ids=true, to_apply=%region_6.7 | all-reduce | flops 24576 | bytes 147456 | tf_op jit(solution)/shard_map/psum | solution.py:86
  285.6 14.6 %all_to_all.42 = bf16[16,8,3,1024]{3,1,2,0:T(8,128)(2,1)S(1)} all-to-all(bf16[16,8,3,1024]{3,1,2,0:T(8,128)(2,1)S(1)} %copy.39), channel_id=1, replica_groups=mesh['row'=16,'col'=8] {'row'}, dimensions={0} | all-to-all | bytes 1572864 | tf_op jit(solution)/shard_map/all_to_all | solution.py:90
  300.9 0.7 reshape.104
  301.7 2.0 fusion.3
  (44 shorter events, 6.5 us)
Async XLA Ops:
  6.5 144.3 %copy-start = (bf16[512,1024]{1,0:T(8,128)(2,1)S(1)}, bf16[512,1024]{1,0:T(8,128)(2,1)}, u32[]{:S(2)}) copy-start(bf16[512,1024]{1,0:T(8,128)(2,1)} %param.18) | copy-start | bytes 3145732
  9.4 6.4 %copy-start.6 = (s32[128]{0:T(128)S(1)}, s32[128]{0:T(128)}, u32[]{:S(2)}) copy-start(s32[128]{0:T(128)} %param.19) | copy-start | bytes 1540
  9.4 6.4 %copy-start.7 = (s32[128]{0:T(128)S(1)}, s32[128]{0:T(128)}, u32[]{:S(2)}) copy-start(s32[128]{0:T(128)} %param.20) | copy-start | bytes 1540
  9.5 6.6 %copy-start.8 = (bf16[128,256,128]{2,1,0:T(8,128)(2,1)S(1)}, bf16[128,256,128]{2,1,0:T(8,128)(2,1)}, u32[]{:S(2)}) copy-start(bf16[128,256,128]{2,1,0:T(8,128)(2,1)} %param.16) | copy-start | bytes 25165828
  18.3 9.4 %copy-start.5 = (bf16[2,8,1024]{2,1,0:T(8,128)(2,1)S(1)}, bf16[2,8,1024]{2,1,0:T(8,128)(2,1)}, u32[]{:S(2)}) copy-start(bf16[2,8,1024]{2,1,0:T(8,128)(2,1)} %param.23) | copy-start | bytes 98308
  19.5 22.6 %all-to-all-start = ((bf16[16,8,3,1024]{3,1,2,0:T(8,128)(2,1)}), bf16[16,8,3,1024]{3,1,2,0:T(8,128)(2,1)S(1)}, u32[]{:S(2)}, u32[]{:S(2)}) async-start(bf16[16,8,3,1024]{3,1,2,0:T(8,128)(2,1)} %copy.32), calls=%async_computation | async-start | bytes 1572864 | tf_op jit(solution)/shard_map/all_to_all | solution.py:80
  27.7 85.7 %all-gather.2.cloned.1.call-start = ((), (), s32[]{:S(2)}) async-start(), calls=%async_computation.6 | async-start | bytes 2359296 | tf_op jit(solution)/shard_map/all_gather | solution.py:115
  42.4 29.2 %copy-start.1 = (bf16[2,8,64,1024]{3,2,1,0:T(8,128)(2,1)S(1)}, bf16[2,8,64,1024]{3,2,1,0:T(8,128)(2,1)}, u32[]{:S(2)}) copy-start(bf16[2,8,64,1024]{3,2,1,0:T(8,128)(2,1)} %param.22) | copy-start | bytes 6291460
  90.3 147.7 %reduce-scatter.2.cloned.1.call-start = ((), (), s32[]{:S(2)}) async-start(), calls=%async_computation.7 | async-start | bytes 8912896 | tf_op jit(solution)/shard_map/reduce_scatter | solution.py:117
  156.4 81.6 %copy-start.4 = (bf16[128,1024]{1,0:T(8,128)(2,1)S(1)}, bf16[128,1024]{1,0:T(8,128)(2,1)}, u32[]{:S(2)}) copy-start(bf16[128,1024]{1,0:T(8,128)(2,1)} %param.17) | copy-start | bytes 786436
  239.9 18.8 %copy-start.9 = (bf16[2,8,64,1024]{3,2,1,0:T(8,128)(2,1)S(1)}, bf16[2,8,64,1024]{3,2,1,0:T(8,128)(2,1)}, u32[]{:S(2)}) copy-start(bf16[2,8,64,1024]{3,2,1,0:T(8,128)(2,1)} %param.21) | copy-start | bytes 6291460
  258.5 26.3 %copy-start.2 = (bf16[2,8,64,1024]{3,2,1,0:T(8,128)(2,1)S(1)}, bf16[2,8,64,1024]{3,2,1,0:T(8,128)(2,1)}, u32[]{:S(2)}) copy-start(bf16[2,8,64,1024]{3,2,1,0:T(8,128)(2,1)} %param.22) | copy-start | bytes 6291460
  300.2 1.4 copy-start.3
Sparse Core Ops, SparseCore 0:
  90.4 22.9 all-gather.1
  156.6 81.3 reduce-scatter.1
where the time goes:
time: 311 us
  blocking collectives  136 us (44%)
  waiting for transfers between devices  119 us (38%)
  matrix products  22.9 us (7%)
  between operations  13.7 us (4%)
  local copies, waits for them, and re-layouts  9.09 us (3%)
  starting transfers between devices  8.21 us (3%)
    reduce_scatter x1, waiting for transfers between devices, local(): lax.psum_scatter(jnp.dot(regrouped, out_weight, preferred_element_type=jn...  81.5 us
    psum x2, blocking collectives, erase(): coefficients = lax.psum(partial_value, 'col').astype(jnp.bfloat16)  51.9 us
    all_to_all x1, blocking collectives, local(): lax.all_to_all(full_rows, 'row', split_axis=1, concat_axis=0, tiled=True)  35.6 us
    all_to_all x2, blocking collectives, erase(): lax.all_to_all(deltas, 'row', split_axis=0, concat_axis=0, tiled=True)  30 us
    all_gather x1, waiting for transfers between devices, local(): full_rows = lax.all_gather(cleaned, 'col', axis=1, tiled=True)  23.1 us
    all_to_all x1, blocking collectives, erase(): lax.all_to_all(packed, 'row', split_axis=0, concat_axis=0, tiled=True)  18.2 us
    all_to_all x1, waiting for transfers between devices, erase(): lax.all_to_all(packed, 'row', split_axis=0, concat_axis=0, tiled=True)  14.4 us
    all_to_all x1, starting transfers between devices, erase(): lax.all_to_all(packed, 'row', split_axis=0, concat_axis=0, tiled=True)  8.13 us
  transfers between devices with their start and end apart: 3, of which 3 were waited for; matrix products, arithmetic and copies ran while one was open for 0% of the time, Pallas kernels for 0%

commit v1 on v0

v1 whole, which is shorter than its diff:
```python
import functools
import math

import jax
import jax.numpy as jnp
from jax import lax
from jax.experimental import pallas as pl
from jax.experimental.pallas import tpu as pltpu
from jax.sharding import PartitionSpec as P

HEADS = 64
KVH = 8
HD = 128
MOST = 3
ROWS = 16
RING = 4
SLOTS = 8
RANK = 64
PART = SLOTS * MOST
PACKED = ROWS * PART
BLOCK = 128
WIDTH = 1024
QUARTER = WIDTH // RING

ALONG_Z = [[z * RING + y for z in range(RING)] for y in range(RING)]
ALONG_Y = [[z * RING + y for y in range(RING)] for z in range(RING)]
BF = jnp.bfloat16
F32 = jnp.float32


def whole(shape):
    return pl.BlockSpec(shape, lambda *_: (0,) * len(shape))


def params(mib):
    return pltpu.CompilerParams(vmem_limit_bytes=mib << 20)


def attention(queries, new_keys, new_values, key_cache, value_cache):
    row_count = queries.shape[0]
    kv_local = new_keys.shape[1] // HD
    group_size = HEADS // KVH
    history = key_cache.shape[1]
    logit_scale = 1.0 / math.sqrt(HD)
    heads_of_query = queries.reshape(row_count, kv_local, group_size, HD)
    past_keys = key_cache.reshape(row_count, history, kv_local, HD)
    past_values = value_cache.reshape(row_count, history, kv_local, HD)
    current_keys = new_keys.reshape(row_count, kv_local, HD)
    own_values = new_values.reshape(row_count, kv_local, HD)
    past_scores = (
        jnp.einsum("bkgd,blkd->bkgl", heads_of_query, past_keys, preferred_element_type=F32)
        * logit_scale
    )
    current_scores = (
        jnp.einsum("qivl,qil->qiv", heads_of_query, current_keys, preferred_element_type=F32)
        * logit_scale
    )
    highest = jnp.maximum(jnp.max(past_scores, axis=-1), current_scores)
    past_exp = jnp.exp(past_scores - highest[..., None])
    own_exp = jnp.exp(current_scores - highest)
    denominator = jnp.sum(past_exp, axis=-1) + own_exp
    past_weights = (past_exp / denominator[..., None]).astype(BF)
    own_weights = (own_exp / denominator).astype(BF)
    mixed = jnp.einsum("bkgl,blkd->bkgd", past_weights, past_values, preferred_element_type=F32)
    mixed = mixed + own_weights.astype(F32)[..., None] * own_values.astype(F32)[:, :, None, :]
    return mixed.reshape(row_count, kv_local * group_size * HD).astype(BF)


def packed_position(tenant, tenant_slot_index):
    tenants = jnp.arange(tenant_slot_index.shape[0], dtype=jnp.int32)
    slot = jnp.sum(
        jnp.where(tenant[:, None] == tenants[None, :], tenant_slot_index[None, :], 0), axis=1
    )
    order = jnp.arange(tenant.shape[0], dtype=jnp.int32)
    earlier = (tenant[:, None] == tenant[None, :]) & (order[None, :] < order[:, None])
    rank = jnp.sum(earlier.astype(jnp.int32), axis=1)
    return slot // SLOTS * PART + rank * SLOTS + slot % SLOTS


def slot_mask(rows):
    shape = (rows, SLOTS * RANK)
    return lax.broadcasted_iota(jnp.int32, shape, 0) % SLOTS == (
        lax.broadcasted_iota(jnp.int32, shape, 1) // RANK
    )


def coef_body(rows_ref, mean_ref, read_ref, out_ref):
    rows = rows_ref[...].astype(F32).reshape(PACKED // SLOTS, SLOTS, WIDTH)
    centered = (rows - mean_ref[...].astype(F32)).astype(BF).reshape(PACKED, WIDTH)
    full = lax.dot_general(
        centered, read_ref[...], (((1,), (1,)), ((), ())), preferred_element_type=F32
    )
    full = jnp.where(slot_mask(PACKED), full, 0.0)
    lanes = full[:, :128] + full[:, 128:256] + full[:, 256:384] + full[:, 384:]
    half = PACKED // 2
    out_ref[...] = lanes[:half] + pltpu.roll(lanes[half:], RANK, 1)


def partial_coefs(rows, mean_bank, read_bank, site):
    return pl.pallas_call(
        coef_body,
        grid=(1,),
        in_specs=[
            whole((PACKED, WIDTH)),
            pl.BlockSpec((None, SLOTS, WIDTH), lambda i: (site, 0, 0)),
            pl.BlockSpec((None, SLOTS * RANK, WIDTH), lambda i: (site, 0, 0)),
        ],
        out_specs=whole((PACKED // 2, 128)),
        out_shape=jax.ShapeDtypeStruct((PACKED // 2, 128), F32),
        compiler_params=params(32),
        cost_estimate=pl.CostEstimate(
            flops=2 * PACKED * WIDTH * SLOTS * RANK, bytes_accessed=2 << 20, transcendentals=0
        ),
        name="coefs",
    )(rows, mean_bank, read_bank.reshape(2, SLOTS * RANK, WIDTH))


def erased_rows(rows_ref, sum_ref, last_ref, write_ref):
    total = sum_ref[...] + last_ref[...].astype(F32)
    both = jnp.concatenate([total, pltpu.roll(total, RANK, 1)], axis=0)
    wide = jnp.concatenate([both] * (SLOTS * RANK // 128), axis=1)
    wide = jnp.where(slot_mask(PACKED), wide, 0.0).astype(BF)
    delta = jnp.dot(wide, write_ref[...], preferred_element_type=F32).astype(BF)
    return rows_ref[...].astype(F32) - delta.astype(F32)


def spread_body(rows_ref, sum_ref, last_ref, write_ref, out_ref):
    erased = erased_rows(rows_ref, sum_ref, last_ref, write_ref)
    for z in range(RING):
        for y in range(RING):
            first = QUARTER * quarter_of(y)
            pieces = []
            for step in range(RING):
                start = PART * (z * RING + (y + step) % RING)
                pieces.append(erased[start : start + PART, first : first + QUARTER])
            out_ref[z * RING + y] = jnp.concatenate(pieces, axis=0).astype(BF)


def home_body(rows_ref, sum_ref, last_ref, write_ref, out_ref):
    out_ref[...] = erased_rows(rows_ref, sum_ref, last_ref, write_ref).astype(BF)


def apply_eraser(body, rows, summed, last, write_bank, site, shape):
    return pl.pallas_call(
        body,
        grid=(1,),
        in_specs=[
            whole((PACKED, WIDTH)),
            whole((PACKED // 2, 128)),
            whole((PACKED // 2, 128)),
            pl.BlockSpec((None, SLOTS * RANK, WIDTH), lambda i: (site, 0, 0)),
        ],
        out_specs=whole(shape),
        out_shape=jax.ShapeDtypeStruct(shape, BF),
        compiler_params=params(32),
        cost_estimate=pl.CostEstimate(
            flops=2 * PACKED * WIDTH * SLOTS * RANK, bytes_accessed=3 << 20, transcendentals=0
        ),
        name="erase",
    )(rows, summed, last, write_bank.reshape(2, SLOTS * RANK, WIDTH))


def quarter_of(y):
    return 2 * (y % 2) + y // 2


def along_col(values, move):
    return lax.ppermute(values, "col", [(i, move(i)) for i in range(8)])


def along_y(values, step):
    return lax.ppermute(
        values, "row", [(i, i // RING * RING + (i + step) % RING) for i in range(ROWS)]
    )


def sum_but_last(partial):
    for bit in (1, 2):
        partial = partial + along_col(partial.astype(BF), lambda i: i ^ bit).astype(F32)
    return partial, along_col(partial.astype(BF), lambda i: i ^ 4)


def compact_body(y_ref, target_ref, rows_ref, out_ref):
    rows = rows_ref[...].astype(F32)
    for step in range(RING):
        target = target_ref[pl.ds((y_ref[0] + step) % RING, 1), :]
        table = (lax.broadcasted_iota(jnp.int32, (PACKED, BLOCK), 0) == target).astype(BF)
        part = rows[:, PART * step : PART * (step + 1), :].reshape(PACKED, QUARTER).astype(BF)
        picked = lax.dot_general(
            table, part, (((0,), (0,)), ((), ())), preferred_element_type=F32
        )
        out_ref[BLOCK * step : BLOCK * (step + 1), :] = picked.astype(BF)


def compact(y, targets, rows):
    return pl.pallas_call(
        compact_body,
        grid_spec=pltpu.PrefetchScalarGridSpec(
            num_scalar_prefetch=1,
            grid=(1,),
            in_specs=[whole((RING, BLOCK)), whole((ROWS, RING * PART, QUARTER))],
            out_specs=whole((RING * BLOCK, QUARTER)),
        ),
        out_shape=jax.ShapeDtypeStruct((RING * BLOCK, QUARTER), BF),
        compiler_params=params(32),
        cost_estimate=pl.CostEstimate(
            flops=2 * RING * BLOCK * PACKED * QUARTER, bytes_accessed=1 << 20, transcendentals=0
        ),
        name="compact",
    )(y, targets, rows)


def project_body(scalar_ref, *refs):
    same, other = refs[0:4], refs[4:8]
    kept_ref, swapped_ref, own_ref, up_ref, far_ref, down_ref, sum_ref = refs[8:]
    step = pl.program_id(0)
    for which in range(RING):

        @pl.when(step == which)
        def _():
            a, b = same[which][...], other[which][...]
            straight = scalar_ref[RING] == 0
            first, second = jnp.where(straight, a, b), jnp.where(straight, b, a)
            product = jnp.dot(first, kept_ref[...], preferred_element_type=F32)
            product += jnp.dot(second, swapped_ref[...], preferred_element_type=F32)
            if which == 0:
                sum_ref[...] = product
            elif which < RING - 1:
                sum_ref[...] += product
            else:
                product += sum_ref[...]
                own_ref[...] = product[:BLOCK]
                up_ref[...] = product[BLOCK : 2 * BLOCK].astype(BF)
                far_ref[...] = product[2 * BLOCK : 3 * BLOCK].astype(BF)
                down_ref[...] = product[3 * BLOCK :].astype(BF)


def project(scalars, same, other, kept, swapped):
    act = whole((RING * BLOCK, QUARTER))
    weight = pl.BlockSpec((None, QUARTER, WIDTH), lambda i, s: (s[i], 0, 0))
    out = whole((BLOCK, WIDTH))
    sent = jax.ShapeDtypeStruct((BLOCK, WIDTH), BF)
    return pl.pallas_call(
        project_body,
        grid_spec=pltpu.PrefetchScalarGridSpec(
            num_scalar_prefetch=1,
            grid=(RING,),
            in_specs=[act] * 8 + [weight] * 2,
            out_specs=[out] * 4,
            scratch_shapes=[pltpu.VMEM((RING * BLOCK, WIDTH), F32)],
        ),
        out_shape=[jax.ShapeDtypeStruct((BLOCK, WIDTH), F32), sent, sent, sent],
        compiler_params=params(40),
        cost_estimate=pl.CostEstimate(
            flops=2 * RING * BLOCK * 8 * QUARTER * WIDTH, bytes_accessed=7 << 20, transcendentals=0
        ),
        name="project",
    )(scalars, *same, *other, kept, swapped)


def local(
    queries,
    new_keys,
    new_values,
    key_cache,
    value_cache,
    residual,
    out_weight,
    tenant,
    tenant_slot_index,
    read_bank,
    write_bank,
    mean_bank,
):
    row, col = lax.axis_index("row"), lax.axis_index("col")
    y = row % RING
    upper = y // 2
    half = out_weight.shape[0] // 2
    kept = lax.dynamic_slice_in_dim(out_weight, upper * half, half)
    swapped = lax.dynamic_slice_in_dim(out_weight, (1 - upper) * half, half)
    swapped = lax.ppermute(swapped, "row", [(i, i ^ 2) for i in range(ROWS)])
    kept = lax.all_gather(kept, "row", axis_index_groups=ALONG_Z)
    swapped = lax.all_gather(swapped, "row", axis_index_groups=ALONG_Z)

    target = packed_position(tenant, tenant_slot_index)
    targets = lax.all_gather(target, "row", axis_index_groups=ALONG_Y)
    table = (jnp.arange(PACKED, dtype=jnp.int32)[:, None] == target[None, :]).astype(BF)

    def dispatch(values):
        packed = jnp.dot(table, values, preferred_element_type=F32).astype(BF)
        packed = packed.reshape(ROWS, PART, WIDTH)
        return lax.all_to_all(packed, "row", 0, 0, tiled=True).reshape(PACKED, WIDTH)

    attended = attention(queries, new_keys, new_values, key_cache, value_cache)
    rows = dispatch(attended)
    summed, last = sum_but_last(partial_coefs(rows, mean_bank, read_bank, 0))
    cleaned = apply_eraser(
        spread_body, rows, summed, last, write_bank, 0, (ROWS, RING * PART, QUARTER)
    )
    cleaned = lax.all_to_all(cleaned, "row", 0, 0, tiled=True)
    here = compact(y[None], targets, cleaned)

    after = along_col(here, lambda i: (i + 2) % 8)
    before = along_col(here, lambda i: (i - 2) % 8)
    across = along_col(here, lambda i: (i + 4) % 8)
    same = [here, after, before, across]
    other = [along_col(part, lambda i: i ^ 1) for part in same]
    x = col // 2
    scalars = jnp.stack([x, (x + 3) % RING, (x + 1) % RING, (x + 2) % RING, (col % 2) ^ upper])
    own, up, far, down = project(scalars.astype(jnp.int32), same, other, kept, swapped)
    projected = own + along_y(up, 1).astype(F32) + along_y(down, 3).astype(F32)
    projected = projected + along_y(far, 2).astype(F32)
    hidden = (residual.astype(F32) + projected).astype(BF)

    rows = dispatch(hidden)
    summed, last = sum_but_last(partial_coefs(rows, mean_bank, read_bank, 1))
    erased = apply_eraser(home_body, rows, summed, last, write_bank, 1, (PACKED, WIDTH))
    erased = lax.all_to_all(erased.reshape(ROWS, PART, WIDTH), "row", 0, 0, tiled=True)
    return lax.dot_general(
        table,
        erased.reshape(PACKED, WIDTH),
        (((0,), (0,)), ((), ())),
        preferred_element_type=F32,
    ).astype(BF)


def solution(mesh):
    return jax.shard_map(
        local,
        mesh=mesh,
        in_specs=(
            P("row", "col"),
            P("row", "col"),
            P("row", "col"),
            P("row", None, "col"),
            P("row", None, "col"),
            P("row", "col"),
            P("row", "col"),
            P("row"),
            P(),
            P(None, "row", None, "col"),
            P(None, "row", None, "col"),
            P(None, "row", "col"),
        ),
        out_specs=P("row", "col"),
        check_vma=False,
    )
```

time: 311 us -> 177 us (0.57)
  waiting for transfers between devices: 119 us -> 35.3 us
  blocking collectives: 136 us -> 65.5 us
  starting transfers between devices: 8.21 us -> 28.1 us
  matrix products: 22.9 us -> 12.6 us
  Pallas kernels: 0 us -> 7.64 us
    reduce_scatter x1 -> x0, waiting for transfers between devices: 81.5 us -> none  [local(): lax.psum_scatter(jnp.dot(regrouped, out_weight, preferred_element_type=jn...]
    psum x2 -> x0, blocking collectives: 51.9 us -> none  [erase(): coefficients = lax.psum(partial_value, 'col').astype(jnp.bfloat16)]
    ppermute x0 -> x17, waiting for transfers between devices: none -> 33.9 us  [the longest x13 22.7 us: along_col(): return lax.ppermute(values, 'col', [(i, move(i)) for i in range(8)])]
    all_to_all x4 -> x3, blocking collectives: 83.8 us -> 53.1 us  [the longest x2 37.9 us: dispatch(): lax.all_to_all(packed, 'row', 0, 0, tiled=True).reshape(PACKED, WIDTH)]
    ppermute x0 -> x17, starting transfers between devices: none -> 23.7 us  [the longest x13 14.1 us: along_col(): return lax.ppermute(values, 'col', [(i, move(i)) for i in range(8)])]
    all_gather x1 -> x2, waiting for transfers between devices: 23.1 us -> 0.01 us  [the longest x1 0.01 us: local(): kept = lax.all_gather(kept, 'row', axis_index_groups=ALONG_Z)]
    all_to_all x1, waiting for transfers between devices: 14.4 us -> 1.39 us  [local(): cleaned = lax.all_to_all(cleaned, 'row', 0, 0, tiled=True)]
    dot_general x9 -> x3, matrix products: 14.6 us -> 1.84 us  [the longest x1 1.06 us: local(): lax.dot_general(table, erased.reshape(PACKED, WIDTH), (((0,), (0,)), ((),...]
  transfers between devices with their start and end apart: 3 -> 20, of which waited for: 3 -> 15; matrix products, arithmetic and copies ran while one was open for 0% -> 9% of each run, Pallas kernels for 0% -> 1%
where the time goes in v1:
time: 177 us; the launch traced here: 176 us
  blocking collectives  65.5 us (37%)
  waiting for transfers between devices  35.3 us (20%)
  starting transfers between devices  28.1 us (16%)
  between operations  13.6 us (8%)
  matrix products  12.6 us (7%)
  local copies, waits for them, and re-layouts  11.1 us (6%)
  Pallas kernels  7.64 us (4%)
  other arithmetic  2.05 us (1%)
    all_to_all x2, blocking collectives, dispatch(): lax.all_to_all(packed, 'row', 0, 0, tiled=True).reshape(PACKED, WIDTH)  37.9 us
    ppermute x13, waiting for transfers between devices, along_col(): return lax.ppermute(values, 'col', [(i, move(i)) for i in range(8)])  22.7 us
    all_to_all x1, blocking collectives, local(): lax.all_to_all(erased.reshape(ROWS, PART, WIDTH), 'row', 0, 0, tiled=True)  15.3 us
    ppermute x13, starting transfers between devices, along_col(): return lax.ppermute(values, 'col', [(i, move(i)) for i in range(8)])  14.1 us
    all_gather x1, blocking collectives, local(): targets = lax.all_gather(target, 'row', axis_index_groups=ALONG_Y)  12.3 us
    ppermute x3, waiting for transfers between devices, along_y(): lax.ppermute(values, 'row', [(i, i // RING * RING + (i + step) % RING) fo...  11.2 us
    unnamed x23, local copies, waits for them, and re-layouts  6.96 us
    ppermute x3, starting transfers between devices, along_y(): lax.ppermute(values, 'row', [(i, i // RING * RING + (i + step) % RING) fo...  6.21 us
  transfers between devices with their start and end apart: 20, of which 15 were waited for; matrix products, arithmetic and copies ran while one was open for 9% of the time, Pallas kernels for 1%

profile of v1, /device:TPU:0, one launch (start us, length us, event | category | flops | bytes accessed | tf_op | source)
XLA Modules:
  0.0 176.0 jit_solution(1274875263211744170)
XLA Ops:
  6.6 2.3 %constant_dynamic-slice_fusion.1 = (bf16[256,1024]{1,0:T(8,128)(2,1)}, bf16[256,1024]{1,0:T(8,128)(2,1)}) fusion(bf16[512,1024]{1,0:T(8,128)(2,1)} %param.18, s32[]{:T(128)S(6)} %select_n.84, s32[]{:T(128)S(6)} %select_n.83), kind=kLoop, calls=%fused_computation.52 | loop fusion | bytes 2097160 | tf_op jit(solution)/shard_map/dynamic_slice | solution.py:280
  9.0 3.4 %collective-permute-start.10 = (bf16[256,1024]{1,0:T(8,128)(2,1)}, bf16[256,1024]{1,0:T(8,128)(2,1)}, u32[]{:S(2)}, u32[]{:S(2)}) collective-permute-start(bf16[256,1024]{1,0:T(8,128)(2,1)} %get-tuple-element.19), channel_id=1, source_target_pairs={{0,16},{8,24},{16,0},{24,8},{32,48},{40,56},{48,32},{56,40},{64,80... | collective-permute-start | bytes 1572872 | tf_op jit(solution)/shard_map/ppermute | solution.py:281
  15.0 5.8 %fusion.22 = (f32[128,8]{1,0:T(8,128)S(1)}, f32[128,8,256]{2,1,0:T(8,128)S(1)}) fusion(bf16[128,8,128]{2,1,0:T(8,128)(2,1)S(1)} %bitcast.85, bf16[128,256,128]{2,1,0:T(8,128)(2,1)} %param.15), kind=kOutput, calls=%fused_computation.56 | convolution fusion | flops 67632128 | bytes 9703424 | tf_op jit(solution)/shard_map/bkgd,blkd->bkgl/dot_general | solution.py:51
  23.1 4.7 %fusion = bf16[128,8,128]{2,1,0:T(8,128)(2,1)S(1)} fusion(bf16[128,256,128]{2,1,0:T(8,128)(2,1)} %param.16, f32[128,8,256]{2,1,0:T(8,128)S(1)} %get-tuple-element.24, f32[128,8]{1,0:T(8,128)} %copy.20, f32[128,8]{1,0:T(8,128)S(1)} %copy.18, f32[128,128]{1,0:T(8,128)} %convert_element_type.85, f32[128,8]{1,0:T(8,128)} %copy.21), kind=kOutput, calls=%fused_computation.4 | convolution fusion | flops 68288512 | bytes 9777152 | tf_op jit(solution)/shard_map/bkgl,blkd->bkgd/dot_general | solution.py:64
  28.2 20.9 %all_to_all.20 = bf16[16,24,1024]{2,1,0:T(8,128)(2,1)S(1)} all-to-all(bf16[16,24,1024]{2,1,0:T(8,128)(2,1)S(1)} %bitcast.83), channel_id=1, replica_groups=mesh['row'=16,'col'=8] {'row'}, dimensions={0} | all-to-all | bytes 1572864 | tf_op jit(solution)/shard_map/all_to_all | solution.py:292
  52.7 2.6 %collective-permute-done.1 = bf16[192,128]{1,0:T(8,128)(2,1)S(1)} collective-permute-done((bf16[192,128]{1,0:T(8,128)(2,1)S(1)}, bf16[192,128]{1,0:T(8,128)(2,1)S(1)}, u32[]{:S(2)}, u32[]{:S(2)}) %collective-permute-start.1) | collective-permute-done | bytes 49184 | tf_op jit(solution)/shard_map/ppermute | solution.py:168
  55.3 3.1 %collective-permute-start.2 = (bf16[192,128]{1,0:T(8,128)(2,1)S(1)}, bf16[192,128]{1,0:T(8,128)(2,1)S(1)}, u32[]{:S(2)}, u32[]{:S(2)}) collective-permute-start(bf16[192,128]{1,0:T(8,128)(2,1)S(1)} %get-tuple-element.17), channel_id=1, source_target_pairs={{0,4},{1,5},{2,6},{3,7},{4,0},{5,1},{6,2},{7,3},{8,12},{9,13},{10,... | collective-permute-start | bytes 147464 | tf_op jit(solution)/shard_map/ppermute | solution.py:168
  58.4 2.6 %collective-permute-done.2.last_ref = bf16[192,128]{1,0:T(8,128)(2,1)S(1)} collective-permute-done((bf16[192,128]{1,0:T(8,128)(2,1)S(1)}, bf16[192,128]{1,0:T(8,128)(2,1)S(1)}, u32[]{:S(2)}, u32[]{:S(2)}) %collective-permute-start.2) | collective-permute-done | bytes 49184 | tf_op jit(solution)/shard_map/ppermute | solution.py:168
  64.2 4.4 %all-to-all-start.1 = ((bf16[16,96,256]{2,1,0:T(8,128)(2,1)}), bf16[16,96,256]{2,1,0:T(8,128)(2,1)S(1)}, u32[]{:S(2)}, u32[]{:S(2)}) async-start(bf16[16,96,256]{2,1,0:T(8,128)(2,1)} %copy-done.4), calls=%async_computation.1 | async-start | bytes 1572864 | tf_op jit(solution)/shard_map/all_to_all | solution.py:300
  68.6 12.3 %all-gather.2 = s32[4,1,128]{2,1,0:T(1,128)S(1)} all-gather(s32[1,1,128]{2,1,0:T(1,128)S(1)} %fusion.19), channel_id=1, replica_groups={{0,8,16,24},{32,40,48,56},{64,72,80,88},{96,104,112,120},{1,9,17,25},{3..., dimensions={0}, use_global_device_ids=true | all-gather | bytes 2560 | tf_op jit(solution)/shard_map/all_gather | solution.py:286
  82.7 3.1 %collective-permute-start.5 = (bf16[512,256]{1,0:T(8,128)(2,1)S(1)}, bf16[512,256]{1,0:T(8,128)(2,1)S(1)}, u32[]{:S(2)}, u32[]{:S(2)}) collective-permute-start(bf16[512,256]{1,0:T(8,128)(2,1)S(1)} %compact.1.refs_0_), channel_id=1, source_target_pairs={{0,4},{1,5},{2,6},{3,7},{4,0},{5,1},{6,2},{7,3},{8,12},{9,13},{10,... | collective-permute-start | bytes 786440 | tf_op jit(solution)/shard_map/ppermute | solution.py:168
  87.8 4.7 %collective-permute-done.5.refs_3_ = bf16[512,256]{1,0:T(8,128)(2,1)S(1)} collective-permute-done((bf16[512,256]{1,0:T(8,128)(2,1)S(1)}, bf16[512,256]{1,0:T(8,128)(2,1)S(1)}, u32[]{:S(2)}, u32[]{:S(2)}) %collective-permute-start.5) | collective-permute-done | bytes 262176 | tf_op jit(solution)/shard_map/ppermute | solution.py:168
  92.5 2.8 %collective-permute-done.4.refs_2_ = bf16[512,256]{1,0:T(8,128)(2,1)S(1)} collective-permute-done((bf16[512,256]{1,0:T(8,128)(2,1)S(1)}, bf16[512,256]{1,0:T(8,128)(2,1)S(1)}, u32[]{:S(2)}, u32[]{:S(2)}) %collective-permute-start.4) | collective-permute-done | bytes 262176 | tf_op jit(solution)/shard_map/ppermute | solution.py:168
  100.7 4.7 %project.1 = (f32[128,1024]{1,0:T(8,128)S(1)}, bf16[128,1024]{1,0:T(8,128)(2,1)S(1)}, bf16[128,1024]{1,0:T(8,128)(2,1)S(1)}, bf16[128,1024]{1,0:T(8,128)(2,1)S(1)}) custom-call(s32[5]{0:T(128)S(1)} %stack.23.scalar_ref, bf16[512,256]{1,0:T(8,128)(2,1)S(1)} %compact.1.refs_0_, bf16[512,256]{1,0:T(8,128)(2,1)S(1)} %collective-permute-done.3.refs_1_, ...), custom_call_target="tpu_custom_call" | custom-call | flops 2147483648 | bytes 7340032 | tf_op jit(solution)/shard_map/project/pallas_call | solution.py:243
  105.5 2.2 %collective-permute-start.11 = (bf16[128,1024]{1,0:T(8,128)(2,1)S(1)}, bf16[128,1024]{1,0:T(8,128)(2,1)S(1)}, u32[]{:S(2)}, u32[]{:S(2)}) collective-permute-start(bf16[128,1024]{1,0:T(8,128)(2,1)S(1)} %get-tuple-element.10), channel_id=1, source_target_pairs={{0,8},{8,16},{16,24},{24,0},{32,40},{40,48},{48,56},{56,32},{64,72... | collective-permute-start | bytes 786440 | tf_op jit(solution)/shard_map/ppermute | solution.py:172
  107.7 2.0 %collective-permute-start.12 = (bf16[128,1024]{1,0:T(8,128)(2,1)S(1)}, bf16[128,1024]{1,0:T(8,128)(2,1)S(1)}, u32[]{:S(2)}, u32[]{:S(2)}) collective-permute-start(bf16[128,1024]{1,0:T(8,128)(2,1)S(1)} %get-tuple-element.11), channel_id=1, source_target_pairs={{0,24},{8,0},{16,8},{24,16},{32,56},{40,32},{48,40},{56,48},{64,88... | collective-permute-start | bytes 786440 | tf_op jit(solution)/shard_map/ppermute | solution.py:172
  109.7 2.0 %collective-permute-start.13 = (bf16[128,1024]{1,0:T(8,128)(2,1)S(1)}, bf16[128,1024]{1,0:T(8,128)(2,1)S(1)}, u32[]{:S(2)}, u32[]{:S(2)}) collective-permute-start(bf16[128,1024]{1,0:T(8,128)(2,1)S(1)} %get-tuple-element.12), channel_id=1, source_target_pairs={{0,16},{8,24},{16,0},{24,8},{32,48},{40,56},{48,32},{56,40},{64,80... | collective-permute-start | bytes 786440 | tf_op jit(solution)/shard_map/ppermute | solution.py:172
  111.7 4.4 %collective-permute-done.11 = bf16[128,1024]{1,0:T(8,128)(2,1)S(1)} collective-permute-done((bf16[128,1024]{1,0:T(8,128)(2,1)S(1)}, bf16[128,1024]{1,0:T(8,128)(2,1)S(1)}, u32[]{:S(2)}, u32[]{:S(2)}) %collective-permute-start.11) | collective-permute-done | bytes 262176 | tf_op jit(solution)/shard_map/ppermute | solution.py:172
  116.0 5.2 %collective-permute-done.12 = bf16[128,1024]{1,0:T(8,128)(2,1)S(1)} collective-permute-done((bf16[128,1024]{1,0:T(8,128)(2,1)S(1)}, bf16[128,1024]{1,0:T(8,128)(2,1)S(1)}, u32[]{:S(2)}, u32[]{:S(2)}) %collective-permute-start.12) | collective-permute-done | bytes 262176 | tf_op jit(solution)/shard_map/ppermute | solution.py:172
  123.3 17.0 %all_to_all.21 = bf16[16,24,1024]{2,1,0:T(8,128)(2,1)S(1)} all-to-all(bf16[16,24,1024]{2,1,0:T(8,128)(2,1)S(1)} %bitcast.81), channel_id=1, replica_groups=mesh['row'=16,'col'=8] {'row'}, dimensions={0} | all-to-all | bytes 1572864 | tf_op jit(solution)/shard_map/all_to_all | solution.py:292
  143.8 2.7 %collective-permute-done.15 = bf16[192,128]{1,0:T(8,128)(2,1)S(1)} collective-permute-done((bf16[192,128]{1,0:T(8,128)(2,1)S(1)}, bf16[192,128]{1,0:T(8,128)(2,1)S(1)}, u32[]{:S(2)}, u32[]{:S(2)}) %collective-permute-start.15) | collective-permute-done | bytes 49184 | tf_op jit(solution)/shard_map/ppermute | solution.py:168
  146.5 2.6 %collective-permute-start.16 = (bf16[192,128]{1,0:T(8,128)(2,1)S(1)}, bf16[192,128]{1,0:T(8,128)(2,1)S(1)}, u32[]{:S(2)}, u32[]{:S(2)}) collective-permute-start(bf16[192,128]{1,0:T(8,128)(2,1)S(1)} %get-tuple-element.15), channel_id=1, source_target_pairs={{0,4},{1,5},{2,6},{3,7},{4,0},{5,1},{6,2},{7,3},{8,12},{9,13},{10,... | collective-permute-start | bytes 147464 | tf_op jit(solution)/shard_map/ppermute | solution.py:168
  149.1 3.1 %collective-permute-done.16.last_ref = bf16[192,128]{1,0:T(8,128)(2,1)S(1)} collective-permute-done((bf16[192,128]{1,0:T(8,128)(2,1)S(1)}, bf16[192,128]{1,0:T(8,128)(2,1)S(1)}, u32[]{:S(2)}, u32[]{:S(2)}) %collective-permute-start.16) | collective-permute-done | bytes 49184 | tf_op jit(solution)/shard_map/ppermute | solution.py:168
  152.8 15.3 %all_to_all.22 = bf16[16,24,1024]{2,1,0:T(8,128)(2,1)S(1)} all-to-all(bf16[16,24,1024]{2,1,0:T(8,128)(2,1)S(1)} %bitcast.77), channel_id=1, replica_groups=mesh['row'=16,'col'=8] {'row'}, dimensions={0} | all-to-all | bytes 1572864 | tf_op jit(solution)/shard_map/all_to_all | solution.py:318
  (78 shorter events, 28.6 us)
Async XLA Ops:
  6.5 90.8 %all-gather.6.cloned.1.call-start = ((), (), s32[]{:S(2)}) async-start(), calls=%async_computation.4 | async-start | bytes 2621440 | tf_op jit(solution)/shard_map/all_gather | solution.py:282
  8.9 88.5 %all-gather.8.cloned.1.call-start = ((), (), s32[]{:S(2)}) async-start(), calls=%async_computation.5 | async-start | bytes 2621440 | tf_op jit(solution)/shard_map/all_gather | solution.py:283
  9.0 18.8 %collective-permute-start.10 = (bf16[256,1024]{1,0:T(8,128)(2,1)}, bf16[256,1024]{1,0:T(8,128)(2,1)}, u32[]{:S(2)}, u32[]{:S(2)}) collective-permute-start(bf16[256,1024]{1,0:T(8,128)(2,1)} %get-tuple-element.19), channel_id=1, source_target_pairs={{0,16},{8,24},{16,0},{24,8},{32,48},{40,56},{48,32},{56,40},{64,80... | collective-permute-start | bytes 1572872 | tf_op jit(solution)/shard_map/ppermute | solution.py:281
  20.8 28.3 %copy-start.1 = (bf16[2,8,64,1024]{3,2,1,0:T(8,128)(2,1)S(1)}, bf16[2,8,64,1024]{3,2,1,0:T(8,128)(2,1)}, u32[]{:S(2)}) copy-start(bf16[2,8,64,1024]{3,2,1,0:T(8,128)(2,1)} %param.21) | copy-start | bytes 6291460
  20.8 28.3 %copy-start.5 = (bf16[2,8,1024]{2,1,0:T(8,128)(2,1)S(1)}, bf16[2,8,1024]{2,1,0:T(8,128)(2,1)}, u32[]{:S(2)}) copy-start(bf16[2,8,1024]{2,1,0:T(8,128)(2,1)} %mean_ref.3) | copy-start | bytes 98308
  49.1 73.7 %copy-start.8 = (bf16[128,1024]{1,0:T(8,128)(2,1)S(1)}, bf16[128,1024]{1,0:T(8,128)(2,1)}, u32[]{:S(2)}) copy-start(bf16[128,1024]{1,0:T(8,128)(2,1)} %param.17) | copy-start | bytes 786436
  49.8 1.3 collective-permute-start
  51.1 4.2 %collective-permute-start.1 = (bf16[192,128]{1,0:T(8,128)(2,1)S(1)}, bf16[192,128]{1,0:T(8,128)(2,1)S(1)}, u32[]{:S(2)}, u32[]{:S(2)}) collective-permute-start(bf16[192,128]{1,0:T(8,128)(2,1)S(1)} %fusion.9), channel_id=1, source_target_pairs={{0,2},{1,3},{2,0},{3,1},{4,6},{5,7},{6,4},{7,5},{8,10},{9,11},{10,... | collective-permute-start | bytes 147464 | tf_op jit(solution)/shard_map/ppermute | solution.py:168
  55.3 5.7 %collective-permute-start.2 = (bf16[192,128]{1,0:T(8,128)(2,1)S(1)}, bf16[192,128]{1,0:T(8,128)(2,1)S(1)}, u32[]{:S(2)}, u32[]{:S(2)}) collective-permute-start(bf16[192,128]{1,0:T(8,128)(2,1)S(1)} %get-tuple-element.17), channel_id=1, source_target_pairs={{0,4},{1,5},{2,6},{3,7},{4,0},{5,1},{6,2},{7,3},{8,12},{9,13},{10,... | collective-permute-start | bytes 147464 | tf_op jit(solution)/shard_map/ppermute | solution.py:168
  64.2 18.1 %all-to-all-start.1 = ((bf16[16,96,256]{2,1,0:T(8,128)(2,1)}), bf16[16,96,256]{2,1,0:T(8,128)(2,1)S(1)}, u32[]{:S(2)}, u32[]{:S(2)}) async-start(bf16[16,96,256]{2,1,0:T(8,128)(2,1)} %copy-done.4), calls=%async_computation.1 | async-start | bytes 1572864 | tf_op jit(solution)/shard_map/all_to_all | solution.py:300
  82.7 9.8 %collective-permute-start.5 = (bf16[512,256]{1,0:T(8,128)(2,1)S(1)}, bf16[512,256]{1,0:T(8,128)(2,1)S(1)}, u32[]{:S(2)}, u32[]{:S(2)}) collective-permute-start(bf16[512,256]{1,0:T(8,128)(2,1)S(1)} %compact.1.refs_0_), channel_id=1, source_target_pairs={{0,4},{1,5},{2,6},{3,7},{4,0},{5,1},{6,2},{7,3},{8,12},{9,13},{10,... | collective-permute-start | bytes 786440 | tf_op jit(solution)/shard_map/ppermute | solution.py:168
  85.8 9.5 %collective-permute-start.4 = (bf16[512,256]{1,0:T(8,128)(2,1)S(1)}, bf16[512,256]{1,0:T(8,128)(2,1)S(1)}, u32[]{:S(2)}, u32[]{:S(2)}) collective-permute-start(bf16[512,256]{1,0:T(8,128)(2,1)S(1)} %compact.1.refs_0_), channel_id=1, source_target_pairs={{0,6},{1,7},{2,0},{3,1},{4,2},{5,3},{6,4},{7,5},{8,14},{9,15},{10,... | collective-permute-start | bytes 786440 | tf_op jit(solution)/shard_map/ppermute | solution.py:168
  86.9 8.8 %collective-permute-start.3 = (bf16[512,256]{1,0:T(8,128)(2,1)S(1)}, bf16[512,256]{1,0:T(8,128)(2,1)S(1)}, u32[]{:S(2)}, u32[]{:S(2)}) collective-permute-start(bf16[512,256]{1,0:T(8,128)(2,1)S(1)} %compact.1.refs_0_), channel_id=1, source_target_pairs={{0,2},{1,3},{2,4},{3,5},{4,6},{5,7},{6,0},{7,1},{8,10},{9,11},{10,... | collective-permute-start | bytes 786440 | tf_op jit(solution)/shard_map/ppermute | solution.py:168
  87.8 8.1 %collective-permute-start.6 = (bf16[512,256]{1,0:T(8,128)(2,1)S(1)}, bf16[512,256]{1,0:T(8,128)(2,1)}, u32[]{:S(2)}, u32[]{:S(2)}) collective-permute-start(bf16[512,256]{1,0:T(8,128)(2,1)S(1)} %compact.1.refs_0_), channel_id=1, source_target_pairs={{0,1},{1,0},{2,3},{3,2},{4,5},{5,4},{6,7},{7,6},{8,9},{9,8},{10,11... | collective-permute-start | bytes 786440 | tf_op jit(solution)/shard_map/ppermute | solution.py:168
  92.5 3.4 %collective-permute-start.9 = (bf16[512,256]{1,0:T(8,128)(2,1)S(1)}, bf16[512,256]{1,0:T(8,128)(2,1)}, u32[]{:S(2)}, u32[]{:S(2)}) collective-permute-start(bf16[512,256]{1,0:T(8,128)(2,1)S(1)} %collective-permute-done.5.refs_3_), channel_id=1, source_target_pairs={{0,1},{1,0},{2,3},{3,2},{4,5},{5,4},{6,7},{7,6},{8,9},{9,8},{10,11... | collective-permute-start | bytes 786440 | tf_op jit(solution)/shard_map/ppermute | solution.py:168
  95.3 1.7 collective-permute-start.8
  95.7 1.7 collective-permute-start.7
  97.4 54.8 %copy-start.3 = (bf16[2,8,64,1024]{3,2,1,0:T(8,128)(2,1)S(1)}, bf16[2,8,64,1024]{3,2,1,0:T(8,128)(2,1)}, u32[]{:S(2)}) copy-start(bf16[2,8,64,1024]{3,2,1,0:T(8,128)(2,1)} %param.22) | copy-start | bytes 6291460
  105.5 10.6 %collective-permute-start.11 = (bf16[128,1024]{1,0:T(8,128)(2,1)S(1)}, bf16[128,1024]{1,0:T(8,128)(2,1)S(1)}, u32[]{:S(2)}, u32[]{:S(2)}) collective-permute-start(bf16[128,1024]{1,0:T(8,128)(2,1)S(1)} %get-tuple-element.10), channel_id=1, source_target_pairs={{0,8},{8,16},{16,24},{24,0},{32,40},{40,48},{48,56},{56,32},{64,72... | collective-permute-start | bytes 786440 | tf_op jit(solution)/shard_map/ppermute | solution.py:172
  107.7 13.5 %collective-permute-start.12 = (bf16[128,1024]{1,0:T(8,128)(2,1)S(1)}, bf16[128,1024]{1,0:T(8,128)(2,1)S(1)}, u32[]{:S(2)}, u32[]{:S(2)}) collective-permute-start(bf16[128,1024]{1,0:T(8,128)(2,1)S(1)} %get-tuple-element.11), channel_id=1, source_target_pairs={{0,24},{8,0},{16,8},{24,16},{32,56},{40,32},{48,40},{56,48},{64,88... | collective-permute-start | bytes 786440 | tf_op jit(solution)/shard_map/ppermute | solution.py:172
  109.7 13.1 %collective-permute-start.13 = (bf16[128,1024]{1,0:T(8,128)(2,1)S(1)}, bf16[128,1024]{1,0:T(8,128)(2,1)S(1)}, u32[]{:S(2)}, u32[]{:S(2)}) collective-permute-start(bf16[128,1024]{1,0:T(8,128)(2,1)S(1)} %get-tuple-element.12), channel_id=1, source_target_pairs={{0,16},{8,24},{16,0},{24,8},{32,48},{40,56},{48,32},{56,40},{64,80... | collective-permute-start | bytes 786440 | tf_op jit(solution)/shard_map/ppermute | solution.py:172
  141.0 1.3 collective-permute-start.14
  142.3 4.2 %collective-permute-start.15 = (bf16[192,128]{1,0:T(8,128)(2,1)S(1)}, bf16[192,128]{1,0:T(8,128)(2,1)S(1)}, u32[]{:S(2)}, u32[]{:S(2)}) collective-permute-start(bf16[192,128]{1,0:T(8,128)(2,1)S(1)} %fusion.10), channel_id=1, source_target_pairs={{0,2},{1,3},{2,0},{3,1},{4,6},{5,7},{6,4},{7,5},{8,10},{9,11},{10,... | collective-permute-start | bytes 147464 | tf_op jit(solution)/shard_map/ppermute | solution.py:168
  146.5 5.7 %collective-permute-start.16 = (bf16[192,128]{1,0:T(8,128)(2,1)S(1)}, bf16[192,128]{1,0:T(8,128)(2,1)S(1)}, u32[]{:S(2)}, u32[]{:S(2)}) collective-permute-start(bf16[192,128]{1,0:T(8,128)(2,1)S(1)} %get-tuple-element.15), channel_id=1, source_target_pairs={{0,4},{1,5},{2,6},{3,7},{4,0},{5,1},{6,2},{7,3},{8,12},{9,13},{10,... | collective-permute-start | bytes 147464 | tf_op jit(solution)/shard_map/ppermute | solution.py:168
  (7 other events, 46.9 us)
Sparse Core Ops, SparseCore 0:
  9.0 41.9 all-gather.5
  52.7 39.3 all-gather.7

commit v2 on v1

v2 whole, which is shorter than its diff:
```python
import functools
import math

import jax
import jax.numpy as jnp
from jax import lax
from jax.experimental import pallas as pl
from jax.experimental.pallas import tpu as pltpu
from jax.sharding import PartitionSpec as P

HEADS = 64
KVH = 8
HD = 128
MOST = 3
ROWS = 16
RING = 4
SLOTS = 8
RANK = 64
PART = SLOTS * MOST
PACKED = ROWS * PART
BLOCK = 128
TILE = 512
CHUNK = 32
WIDTH = 1024
QUARTER = WIDTH // RING

ALONG_Z = [[z * RING + y for z in range(RING)] for y in range(RING)]
ALONG_Y = [[z * RING + y for y in range(RING)] for z in range(RING)]
BF = jnp.bfloat16
F32 = jnp.float32


def whole(shape):
    return pl.BlockSpec(shape, lambda *_: (0,) * len(shape))


def params(mib):
    return pltpu.CompilerParams(vmem_limit_bytes=mib << 20)


def in_hbm(*arrays):
    return [pltpu.with_memory_space_constraint(array, pltpu.HBM) for array in arrays]


def attend_body(
    q_ref, key_ref, value_ref, target_ref, keys_ref, values_ref,
    out_ref, after_ref, heads_ref, mix_ref, all_ref
):
    step = pl.program_id(0)
    group = HEADS // KVH
    scale = 1.0 / math.sqrt(HD)
    q = q_ref[...].astype(F32)
    for head in range(group):
        heads_ref[pl.ds(head, CHUNK, stride=group), :] = q[:, HD * head : HD * (head + 1)]
    heads = heads_ref[...].reshape(CHUNK, group, HD)
    past = scale * jnp.einsum(
        "bhd,bld->bhl", heads.astype(BF), keys_ref[...], preferred_element_type=F32
    )
    key = key_ref[...].astype(F32)[:, None, :]
    own = scale * jnp.sum(heads * key, axis=-1, keepdims=True)
    top = jnp.maximum(jnp.max(past, axis=-1, keepdims=True), own)
    past, own = jnp.exp(past - top), jnp.exp(own - top)
    inverse = 1.0 / (jnp.sum(past, axis=-1, keepdims=True) + own)
    weights = (past * inverse).astype(BF)
    own = (own * inverse).astype(BF).astype(F32)
    mixed = jnp.einsum("bhl,bld->bhd", weights, values_ref[...], preferred_element_type=F32)
    mixed = mixed + own * value_ref[...].astype(F32)[:, None, :]
    mix_ref[...] = mixed.reshape(CHUNK * group, HD)
    rows = pl.ds(pl.multiple_of(step * CHUNK, CHUNK), CHUNK)
    for head in range(group):
        picked = mix_ref[pl.ds(head, CHUNK, stride=group), :]
        all_ref[rows, HD * head : HD * (head + 1)] = picked.astype(BF)

    @pl.when(step == pl.num_programs(0) - 1)
    def _():
        table = (
            lax.broadcasted_iota(jnp.int32, (PACKED, BLOCK), 0) == target_ref[...]
        ).astype(BF)
        packed = jnp.dot(table, all_ref[...], preferred_element_type=F32)
        out_ref[...] = packed.astype(BF)
        after_ref[...] = target_ref[...]


def attend_and_pack(queries, new_keys, new_values, key_cache, value_cache, target):
    history = key_cache.shape[1]
    group = HEADS // KVH
    by_row = lambda *tail: pl.BlockSpec((CHUNK,) + tail, lambda i: (i,) + (0,) * len(tail))
    queries, new_keys, new_values, key_cache, value_cache = in_hbm(
        queries, new_keys, new_values, key_cache, value_cache
    )
    return pl.pallas_call(
        attend_body,
        grid=(BLOCK // CHUNK,),
        in_specs=[
            by_row(WIDTH),
            by_row(HD),
            by_row(HD),
            whole((1, BLOCK)),
            by_row(history, HD),
            by_row(history, HD),
        ],
        out_specs=[whole((PACKED, WIDTH)), whole((1, BLOCK))],
        out_shape=[
            jax.ShapeDtypeStruct((PACKED, WIDTH), BF),
            jax.ShapeDtypeStruct((1, BLOCK), jnp.int32),
        ],
        scratch_shapes=[
            pltpu.VMEM((CHUNK * group, HD), F32),
            pltpu.VMEM((CHUNK * group, HD), F32),
            pltpu.VMEM((BLOCK, WIDTH), BF),
        ],
        compiler_params=params(20),
        cost_estimate=pl.CostEstimate(
            flops=4 * BLOCK * history * WIDTH, bytes_accessed=17 << 20, transcendentals=0
        ),
        name="attend",
    )(queries, new_keys, new_values, target, key_cache, value_cache)


def packed_position(tenant, tenant_slot_index):
    tenants = jnp.arange(tenant_slot_index.shape[0], dtype=jnp.int32)
    slot = jnp.sum(
        jnp.where(tenant[:, None] == tenants[None, :], tenant_slot_index[None, :], 0), axis=1
    )
    order = jnp.arange(tenant.shape[0], dtype=jnp.int32)
    earlier = (tenant[:, None] == tenant[None, :]) & (order[None, :] < order[:, None])
    rank = jnp.sum(earlier.astype(jnp.int32), axis=1)
    return slot // SLOTS * PART + rank * SLOTS + slot % SLOTS


def slot_mask(rows):
    shape = (rows, SLOTS * RANK)
    return lax.broadcasted_iota(jnp.int32, shape, 0) % SLOTS == (
        lax.broadcasted_iota(jnp.int32, shape, 1) // RANK
    )


def coef_body(rows_ref, mean_ref, read_ref, out_ref, short_ref):
    rows = rows_ref[...].astype(F32).reshape(PACKED // SLOTS, SLOTS, WIDTH)
    centered = (rows - mean_ref[...].astype(F32)).astype(BF).reshape(PACKED, WIDTH)
    full = lax.dot_general(
        centered, read_ref[...], (((1,), (1,)), ((), ())), preferred_element_type=F32
    )
    full = jnp.where(slot_mask(PACKED), full, 0.0)
    lanes = full[:, :128] + full[:, 128:256] + full[:, 256:384] + full[:, 384:]
    half = PACKED // 2
    packed = lanes[:half] + pltpu.roll(lanes[half:], RANK, 1)
    out_ref[...] = packed
    short_ref[...] = packed.astype(BF)


def partial_coefs(rows, mean_bank, read_bank, site):
    return pl.pallas_call(
        coef_body,
        grid=(1,),
        in_specs=[
            whole((PACKED, WIDTH)),
            pl.BlockSpec((None, SLOTS, WIDTH), lambda i: (site, 0, 0)),
            pl.BlockSpec((None, SLOTS * RANK, WIDTH), lambda i: (site, 0, 0)),
        ],
        out_specs=[whole((PACKED // 2, 128))] * 2,
        out_shape=[jax.ShapeDtypeStruct((PACKED // 2, 128), kind) for kind in (F32, BF)],
        compiler_params=params(16),
        cost_estimate=pl.CostEstimate(
            flops=2 * PACKED * WIDTH * SLOTS * RANK, bytes_accessed=2 << 20, transcendentals=0
        ),
        name="coefs",
    )(rows, mean_bank, read_bank.reshape(2, SLOTS * RANK, WIDTH))


def erased_rows(rows_ref, sum_ref, last_ref, write_ref):
    total = sum_ref[...] + last_ref[...].astype(F32)
    both = jnp.concatenate([total, pltpu.roll(total, RANK, 1)], axis=0)
    wide = jnp.concatenate([both] * (SLOTS * RANK // 128), axis=1)
    wide = jnp.where(slot_mask(PACKED), wide, 0.0).astype(BF)
    delta = jnp.dot(wide, write_ref[...], preferred_element_type=F32).astype(BF)
    return rows_ref[...].astype(F32) - delta.astype(F32)


def spread_body(core_ref, rows_ref, sum_ref, last_ref, write_ref, out_ref):
    erased = erased_rows(rows_ref, sum_ref, last_ref, write_ref).astype(BF).astype(F32)
    first_core = core_ref[0] == 0
    for y in range(RING):
        start = QUARTER * 2 * (y % 2)
        low = erased[:, start : start + QUARTER]
        high = erased[:, start + QUARTER : start + 2 * QUARTER]
        part = jnp.where(first_core, low, high) if y < 2 else jnp.where(first_core, high, low)
        for z in range(RING):
            pieces = []
            for step in range(RING):
                start = PART * (z * RING + (y + step) % RING)
                pieces.append(part[start : start + PART])
            out_ref[z * RING + y] = jnp.concatenate(pieces, axis=0).astype(BF)


def home_body(rows_ref, sum_ref, last_ref, write_ref, out_ref):
    out_ref[...] = erased_rows(rows_ref, sum_ref, last_ref, write_ref).astype(BF)


def apply_eraser(body, rows, summed, last, write_bank, site, shape, extra=()):
    write_bank = write_bank.reshape(2, SLOTS * RANK, WIDTH)
    if site == 0:
        write_bank = in_hbm(write_bank)[0]
    return pl.pallas_call(
        body,
        grid=(1,),
        in_specs=[pl.BlockSpec(memory_space=pltpu.SMEM)] * len(extra)
        + [
            whole((PACKED, WIDTH)),
            whole((PACKED // 2, 128)),
            whole((PACKED // 2, 128)),
            pl.BlockSpec((None, SLOTS * RANK, WIDTH), lambda i: (site, 0, 0)),
        ],
        out_specs=whole(shape),
        out_shape=jax.ShapeDtypeStruct(shape, BF),
        compiler_params=params(16),
        cost_estimate=pl.CostEstimate(
            flops=2 * PACKED * WIDTH * SLOTS * RANK, bytes_accessed=3 << 20, transcendentals=0
        ),
        name="erase",
    )(*extra, rows, summed, last, write_bank)


def along_col(values, move):
    return lax.ppermute(values, "col", [(i, move(i)) for i in range(8)])


def along_y(values, step):
    return lax.ppermute(
        values, "row", [(i, i // RING * RING + (i + step) % RING) for i in range(ROWS)]
    )


def sum_but_last(partial, short):
    for bit in (1, 2):
        partial = partial + along_col(short, lambda i: i ^ bit).astype(F32)
        short = partial.astype(BF)
    return partial, along_col(short, lambda i: i ^ 4)


def compact_body(y_ref, target_ref, rows_ref, out_ref):
    rows = rows_ref[...].astype(F32)
    for step in range(RING):
        target = target_ref[pl.ds((y_ref[0] + step) & 3, 1), :]
        table = (lax.broadcasted_iota(jnp.int32, (PACKED, BLOCK), 0) == target).astype(BF)
        part = rows[:, PART * step : PART * (step + 1), :].reshape(PACKED, QUARTER).astype(BF)
        picked = lax.dot_general(
            table, part, (((0,), (0,)), ((), ())), preferred_element_type=F32
        )
        out_ref[BLOCK * step : BLOCK * (step + 1), :] = picked.astype(BF)


def compact(y, targets, rows):
    return pl.pallas_call(
        compact_body,
        grid_spec=pltpu.PrefetchScalarGridSpec(
            num_scalar_prefetch=1,
            grid=(1,),
            in_specs=[whole((RING, BLOCK)), whole((ROWS, RING * PART, QUARTER))],
            out_specs=whole((RING * BLOCK, QUARTER)),
        ),
        out_shape=jax.ShapeDtypeStruct((RING * BLOCK, QUARTER), BF),
        compiler_params=params(16),
        cost_estimate=pl.CostEstimate(
            flops=2 * RING * BLOCK * PACKED * QUARTER, bytes_accessed=1 << 20, transcendentals=0
        ),
        name="compact",
    )(y, targets, rows)


def project_body(scalar_ref, *refs):
    same, other = refs[0:RING], refs[RING : 2 * RING]
    weight_ref, far_ref, up_ref, down_ref, own_ref = refs[2 * RING :]
    near = pl.multiple_of(scalar_ref[1] * QUARTER, QUARTER)
    away = pl.multiple_of(QUARTER - near, QUARTER)
    product = jnp.zeros((RING * BLOCK, TILE), F32)
    for step, offset in enumerate((0, 3, 1, 2)):
        z = (scalar_ref[0] + offset) & 3
        product += jnp.dot(
            same[step][...], weight_ref[z, pl.ds(near, QUARTER), :], preferred_element_type=F32
        )
        product += jnp.dot(
            other[step][...], weight_ref[z, pl.ds(away, QUARTER), :], preferred_element_type=F32
        )
    own_ref[...] = product[:BLOCK]
    up_ref[...] = product[BLOCK : 2 * BLOCK].astype(BF)
    far_ref[...] = product[2 * BLOCK : 3 * BLOCK].astype(BF)
    down_ref[...] = product[3 * BLOCK :].astype(BF)


def project(scalars, same, other, weight):
    act = whole((RING * BLOCK, QUARTER))
    out = pl.BlockSpec((BLOCK, TILE), lambda i, s: (0, i))
    sent = jax.ShapeDtypeStruct((BLOCK, WIDTH), BF)
    return pl.pallas_call(
        project_body,
        grid_spec=pltpu.PrefetchScalarGridSpec(
            num_scalar_prefetch=1,
            grid=(WIDTH // TILE,),
            in_specs=[act] * 8
            + [pl.BlockSpec((RING, 2 * QUARTER, TILE), lambda i, s: (0, 0, i))],
            out_specs=[out] * 4,
        ),
        out_shape=[sent, sent, sent, jax.ShapeDtypeStruct((BLOCK, WIDTH), F32)],
        compiler_params=params(20),
        cost_estimate=pl.CostEstimate(
            flops=2 * RING * BLOCK * 8 * QUARTER * WIDTH, bytes_accessed=7 << 20, transcendentals=0
        ),
        name="project",
    )(scalars, *same, *other, *in_hbm(weight))


def local(
    queries,
    new_keys,
    new_values,
    key_cache,
    value_cache,
    residual,
    out_weight,
    tenant,
    tenant_slot_index,
    read_bank,
    write_bank,
    mean_bank,
):
    row, col = lax.axis_index("row"), lax.axis_index("col")
    x, core, y, upper = col >> 1, col & 1, row & 3, (row & 3) >> 1
    half = out_weight.shape[0] // 2
    swapped = lax.ppermute(out_weight[half:], "row", [(i, i ^ 2) for i in range(ROWS)])
    target = packed_position(tenant, tenant_slot_index)

    def dispatch(packed):
        packed = packed.reshape(ROWS, PART, WIDTH)
        return lax.all_to_all(packed, "row", 0, 0, tiled=True).reshape(PACKED, WIDTH)

    packed, target = attend_and_pack(
        queries, new_keys, new_values, key_cache, value_cache, target[None]
    )
    swapped, target = lax.optimization_barrier((swapped, target))
    weight = jnp.concatenate([out_weight[:half], swapped], axis=0)
    weight = lax.all_gather(weight, "row", axis_index_groups=ALONG_Z)
    rows = dispatch(packed)
    targets = lax.all_gather(target[0], "row", axis_index_groups=ALONG_Y)
    table = (jnp.arange(PACKED, dtype=jnp.int32)[:, None] == target).astype(BF)
    summed, last = sum_but_last(*partial_coefs(rows, mean_bank, read_bank, 0))
    shape = (ROWS, RING * PART, QUARTER)
    cleaned = apply_eraser(spread_body, rows, summed, last, write_bank, 0, shape, (core[None],))
    cleaned = lax.all_to_all(cleaned, "row", 0, 0, tiled=True)
    here = compact(y[None], targets, cleaned)

    after = along_col(here, lambda i: (i + 2) % 8)
    before = along_col(here, lambda i: (i - 2) % 8)
    across = along_col(here, lambda i: (i + 4) % 8)
    same = [here, after, before, across]
    other = [along_col(part, lambda i: i ^ 1) for part in same]
    place = jnp.stack([x, core ^ upper])
    far, up, down, own = project(place, same, other, weight)
    far, up, down = along_y(far, 2), along_y(up, 1), along_y(down, 3)
    projected = own + up.astype(F32) + down.astype(F32) + far.astype(F32)
    hidden = (residual.astype(F32) + projected).astype(BF)

    rows = dispatch(jnp.dot(table, hidden, preferred_element_type=F32).astype(BF))
    summed, last = sum_but_last(*partial_coefs(rows, mean_bank, read_bank, 1))
    erased = apply_eraser(home_body, rows, summed, last, write_bank, 1, (PACKED, WIDTH))
    erased = lax.all_to_all(erased.reshape(ROWS, PART, WIDTH), "row", 0, 0, tiled=True)
    return lax.dot_general(
        table,
        erased.reshape(PACKED, WIDTH),
        (((0,), (0,)), ((), ())),
        preferred_element_type=F32,
    ).astype(BF)


def solution(mesh):
    return jax.shard_map(
        local,
        mesh=mesh,
        in_specs=(
            P("row", "col"),
            P("row", "col"),
            P("row", "col"),
            P("row", None, "col"),
            P("row", None, "col"),
            P("row", "col"),
            P("row", "col"),
            P("row"),
            P(),
            P(None, "row", None, "col"),
            P(None, "row", None, "col"),
            P(None, "row", "col"),
        ),
        out_specs=P("row", "col"),
        check_vma=False,
    )
```

time: 177 us -> 170 us (0.960)
  matrix products: 12.6 us -> 1.49 us
  Pallas kernels: 7.64 us -> 17.5 us
  local copies, waits for them, and re-layouts: 11.1 us -> 3.09 us
  waiting for transfers between devices: 35.3 us -> 37.2 us
    dot_general x5 -> x1, matrix products: 11.5 us -> 0.43 us  [local(): jnp.dot(table, hidden, preferred_element_type=F32).astype(BF)]
    pallas_call x2 -> x3, Pallas kernels: 1.2 us -> 10.9 us  [the longest x1 8.38 us: attend_and_pack(): pl.pallas_call(attend_body, grid=(BLOCK // CHUNK,), in_specs=[by_row(WIDT...]
    unnamed x23 -> x16, local copies, waits for them, and re-layouts: 6.96 us -> 1.8 us
    ppermute x1, waiting for transfers between devices: 0.01 us -> 2.44 us  [local(): lax.ppermute(out_weight[half:], 'row', [(i, i ^ 2) for i in range(ROWS)])]
    dynamic_slice x1 -> x0, local copies, waits for them, and re-layouts: 2.3 us -> none  [local(): swapped = lax.dynamic_slice_in_dim(out_weight, (1 - upper) * half, half)]
  transfers between devices with their start and end apart: 20 -> 19, of which waited for: 15 -> 16; matrix products, arithmetic and copies ran while one was open for 9% -> 0% of each run, Pallas kernels for 1% -> 7%
where the time goes in v2:
time: 170 us; the launch traced here: 169 us
  blocking collectives  66.9 us (39%)
  waiting for transfers between devices  37.2 us (22%)
  starting transfers between devices  27.9 us (16%)
  Pallas kernels  17.5 us (10%)
  between operations  13.5 us (8%)
  local copies, waits for them, and re-layouts  3.09 us (2%)
    all_to_all x2, blocking collectives, dispatch(): lax.all_to_all(packed, 'row', 0, 0, tiled=True).reshape(PACKED, WIDTH)  38.7 us
    ppermute x13, waiting for transfers between devices, along_col(): return lax.ppermute(values, 'col', [(i, move(i)) for i in range(8)])  22.2 us
    all_to_all x1, blocking collectives, local(): lax.all_to_all(erased.reshape(ROWS, PART, WIDTH), 'row', 0, 0, tiled=True)  15.3 us
    ppermute x13, starting transfers between devices, along_col(): return lax.ppermute(values, 'col', [(i, move(i)) for i in range(8)])  15.1 us
    all_gather x1, blocking collectives, local(): targets = lax.all_gather(target[0], 'row', axis_index_groups=ALONG_Y)  13 us
    ppermute x3, waiting for transfers between devices, along_y(): lax.ppermute(values, 'row', [(i, i // RING * RING + (i + step) % RING) fo...  11.2 us
    pallas_call x1, Pallas kernels, attend_and_pack(): pl.pallas_call(attend_body, grid=(BLOCK // CHUNK,), in_specs=[by_row(WIDT...  8.38 us
    ppermute x3, starting transfers between devices, along_y(): lax.ppermute(values, 'row', [(i, i // RING * RING + (i + step) % RING) fo...  5.8 us
  transfers between devices with their start and end apart: 19, of which 16 were waited for; matrix products, arithmetic and copies ran while one was open for 0% of the time, Pallas kernels for 7%

profile of v2, /device:TPU:0, one launch (start us, length us, event | category | flops | bytes accessed | tf_op | source)
XLA Modules:
  0.0 169.1 jit_solution(9299829275092782054)
XLA Ops:
  7.8 3.4 %collective-permute-start = (bf16[256,1024]{1,0:T(8,128)(2,1)S(1)}, bf16[256,1024]{1,0:T(8,128)(2,1)S(1)}, u32[]{:S(2)}, u32[]{:S(2)}) collective-permute-start(bf16[256,1024]{1,0:T(8,128)(2,1)S(1)} %get-tuple-element.36), channel_id=1, source_target_pairs={{0,16},{8,24},{16,0},{24,8},{32,48},{40,56},{48,32},{56,40},{64,80... | collective-permute-start | bytes 1572872 | tf_op jit(solution)/shard_map/ppermute | solution.py:330
  11.4 8.4 %attend.1 = (bf16[384,1024]{1,0:T(8,128)(2,1)S(1)}, s32[1,128]{1,0:T(1,128)S(1)}) custom-call(bf16[128,1024]{1,0:T(8,128)(2,1)} %q_ref.1, bf16[128,128]{1,0:T(8,128)(2,1)} %key_ref.1, bf16[128,128]{1,0:T(8,128)(2,1)} %value_ref.1, s32[1,128]{1,0:T(1,128)S(1)} %fusion.5.target_ref, bf16[128,256,128]{2,1,0:T(8,128)(2,1)} %keys_ref.1, ...), custom_call_target="tpu_custom_call" | custom-call | flops 134217728 | bytes 17825792 | tf_op jit(solution)/shard_map/attend/pallas_call | solution.py:91
  20.7 2.4 %collective-permute-done = bf16[256,1024]{1,0:T(8,128)(2,1)S(1)} collective-permute-done((bf16[256,1024]{1,0:T(8,128)(2,1)S(1)}, bf16[256,1024]{1,0:T(8,128)(2,1)S(1)}, u32[]{:S(2)}, u32[]{:S(2)}) %collective-permute-start) | collective-permute-done | bytes 524320 | tf_op jit(solution)/shard_map/ppermute | solution.py:330
  24.2 21.6 %all_to_all.20 = bf16[16,24,1024]{2,1,0:T(8,128)(2,1)S(1)} all-to-all(bf16[16,24,1024]{2,1,0:T(8,128)(2,1)} %bitcast.43), channel_id=1, replica_groups=mesh['row'=16,'col'=8] {'row'}, dimensions={0} | all-to-all | bytes 1572864 | tf_op jit(solution)/shard_map/all_to_all | solution.py:335
  49.5 2.6 %collective-permute-done.2 = bf16[192,128]{1,0:T(8,128)(2,1)S(1)} collective-permute-done((bf16[192,128]{1,0:T(8,128)(2,1)S(1)}, bf16[192,128]{1,0:T(8,128)(2,1)S(1)}, u32[]{:S(2)}, u32[]{:S(2)}) %collective-permute-start.2) | collective-permute-done | bytes 49184 | tf_op jit(solution)/shard_map/ppermute | solution.py:225
  52.1 3.1 %collective-permute-start.3 = (bf16[192,128]{1,0:T(8,128)(2,1)S(1)}, bf16[192,128]{1,0:T(8,128)(2,1)S(1)}, u32[]{:S(2)}, u32[]{:S(2)}) collective-permute-start(bf16[192,128]{1,0:T(8,128)(2,1)S(1)} %get-tuple-element.33), channel_id=1, source_target_pairs={{0,4},{1,5},{2,6},{3,7},{4,0},{5,1},{6,2},{7,3},{8,12},{9,13},{10,... | collective-permute-start | bytes 147464 | tf_op jit(solution)/shard_map/ppermute | solution.py:225
  55.2 2.6 %collective-permute-done.3.last_ref = bf16[192,128]{1,0:T(8,128)(2,1)S(1)} collective-permute-done((bf16[192,128]{1,0:T(8,128)(2,1)S(1)}, bf16[192,128]{1,0:T(8,128)(2,1)S(1)}, u32[]{:S(2)}, u32[]{:S(2)}) %collective-permute-start.3) | collective-permute-done | bytes 49184 | tf_op jit(solution)/shard_map/ppermute | solution.py:225
  57.8 1.9 %erase.2 = bf16[16,96,256]{2,1,0:T(8,128)(2,1)S(1)} custom-call(s32[1]{0:T(128)} %bitcast.8.core_ref, bf16[384,1024]{1,0:T(8,128)(2,1)S(1)} %bitcast.39, f32[192,128]{1,0:T(8,128)S(1)} %get-tuple-element.34.sum_ref, bf16[192,128]{1,0:T(8,128)(2,1)S(1)} %collective-permute-done.3.last_ref, bf16[2,512,1024]{2,1,0:T(8,128)(2,1)} %bitcast.36), custom_call_target="tpu_custom_call" | custom-call | flops 402653184 | bytes 3145728 | tf_op jit(solution)/shard_map/erase/pallas_call | solution.py:204
  60.5 3.6 %all-to-all-start.1 = ((bf16[16,96,256]{2,1,0:T(8,128)(2,1)}), bf16[16,96,256]{2,1,0:T(8,128)(2,1)S(1)}, u32[]{:S(2)}, u32[]{:S(2)}) async-start(bf16[16,96,256]{2,1,0:T(8,128)(2,1)} %copy-done.2), calls=%async_computation.1 | async-start | bytes 1572864 | tf_op jit(solution)/shard_map/all_to_all | solution.py:349
  64.2 13.0 %all-gather.1 = s32[4,1,128]{2,1,0:T(1,128)S(1)} all-gather(s32[1,1,128]{2,1,0:T(1,128)S(1)} %bitcast.45), channel_id=1, replica_groups={{0,8,16,24},{32,40,48,56},{64,72,80,88},{96,104,112,120},{1,9,17,25},{3..., dimensions={0}, use_global_device_ids=true | all-gather | bytes 2560 | tf_op jit(solution)/shard_map/all_gather | solution.py:344
  78.9 3.5 %collective-permute-start.6 = (bf16[512,256]{1,0:T(8,128)(2,1)S(1)}, bf16[512,256]{1,0:T(8,128)(2,1)S(1)}, u32[]{:S(2)}, u32[]{:S(2)}) collective-permute-start(bf16[512,256]{1,0:T(8,128)(2,1)S(1)} %compact.1.refs_0_), channel_id=1, source_target_pairs={{0,4},{1,5},{2,6},{3,7},{4,0},{5,1},{6,2},{7,3},{8,12},{9,13},{10,... | collective-permute-start | bytes 786440 | tf_op jit(solution)/shard_map/ppermute | solution.py:225
  84.4 4.5 %collective-permute-done.6.refs_3_ = bf16[512,256]{1,0:T(8,128)(2,1)S(1)} collective-permute-done((bf16[512,256]{1,0:T(8,128)(2,1)S(1)}, bf16[512,256]{1,0:T(8,128)(2,1)S(1)}, u32[]{:S(2)}, u32[]{:S(2)}) %collective-permute-start.6) | collective-permute-done | bytes 262176 | tf_op jit(solution)/shard_map/ppermute | solution.py:225
  88.9 2.6 %collective-permute-done.5.refs_2_ = bf16[512,256]{1,0:T(8,128)(2,1)S(1)} collective-permute-done((bf16[512,256]{1,0:T(8,128)(2,1)S(1)}, bf16[512,256]{1,0:T(8,128)(2,1)S(1)}, u32[]{:S(2)}, u32[]{:S(2)}) %collective-permute-start.5) | collective-permute-done | bytes 262176 | tf_op jit(solution)/shard_map/ppermute | solution.py:225
  94.0 4.9 %project.1 = (bf16[128,1024]{1,0:T(8,128)(2,1)S(1)}, bf16[128,1024]{1,0:T(8,128)(2,1)S(1)}, bf16[128,1024]{1,0:T(8,128)(2,1)S(1)}, f32[128,1024]{1,0:T(8,128)S(1)}) custom-call(s32[2]{0:T(128)S(1)} %pad_add_fusion.scalar_ref, bf16[512,256]{1,0:T(8,128)(2,1)S(1)} %compact.1.refs_0_, bf16[512,256]{1,0:T(8,128)(2,1)S(1)} %collective-permute-done.4.refs_1_, ...), custom_call_target="tpu_custom_call" | custom-call | flops 2147483648 | bytes 7340032 | tf_op jit(solution)/shard_map/project/pallas_call | solution.py:295
  99.0 2.0 %collective-permute-start.11 = (bf16[128,1024]{1,0:T(8,128)(2,1)S(1)}, bf16[128,1024]{1,0:T(8,128)(2,1)S(1)}, u32[]{:S(2)}, u32[]{:S(2)}) collective-permute-start(bf16[128,1024]{1,0:T(8,128)(2,1)S(1)} %get-tuple-element.24), channel_id=1, source_target_pairs={{0,8},{8,16},{16,24},{24,0},{32,40},{40,48},{48,56},{56,32},{64,72... | collective-permute-start | bytes 786440 | tf_op jit(solution)/shard_map/ppermute | solution.py:229
  102.6 2.1 %collective-permute-start.13 = (bf16[128,1024]{1,0:T(8,128)(2,1)S(1)}, bf16[128,1024]{1,0:T(8,128)(2,1)S(1)}, u32[]{:S(2)}, u32[]{:S(2)}) collective-permute-start(bf16[128,1024]{1,0:T(8,128)(2,1)S(1)} %get-tuple-element.26), channel_id=1, source_target_pairs={{0,16},{8,24},{16,0},{24,8},{32,48},{40,56},{48,32},{56,40},{64,80... | collective-permute-start | bytes 786440 | tf_op jit(solution)/shard_map/ppermute | solution.py:229
  104.8 4.4 %collective-permute-done.11 = bf16[128,1024]{1,0:T(8,128)(2,1)S(1)} collective-permute-done((bf16[128,1024]{1,0:T(8,128)(2,1)S(1)}, bf16[128,1024]{1,0:T(8,128)(2,1)S(1)}, u32[]{:S(2)}, u32[]{:S(2)}) %collective-permute-start.11) | collective-permute-done | bytes 262176 | tf_op jit(solution)/shard_map/ppermute | solution.py:229
  109.1 5.0 %collective-permute-done.12 = bf16[128,1024]{1,0:T(8,128)(2,1)S(1)} collective-permute-done((bf16[128,1024]{1,0:T(8,128)(2,1)S(1)}, bf16[128,1024]{1,0:T(8,128)(2,1)S(1)}, u32[]{:S(2)}, u32[]{:S(2)}) %collective-permute-start.12) | collective-permute-done | bytes 262176 | tf_op jit(solution)/shard_map/ppermute | solution.py:229
  114.1 1.8 %collective-permute-done.13 = bf16[128,1024]{1,0:T(8,128)(2,1)S(1)} collective-permute-done((bf16[128,1024]{1,0:T(8,128)(2,1)S(1)}, bf16[128,1024]{1,0:T(8,128)(2,1)S(1)}, u32[]{:S(2)}, u32[]{:S(2)}) %collective-permute-start.13) | collective-permute-done | bytes 262176 | tf_op jit(solution)/shard_map/ppermute | solution.py:229
  116.4 17.0 %all_to_all.21 = bf16[16,24,1024]{2,1,0:T(8,128)(2,1)S(1)} all-to-all(bf16[16,24,1024]{2,1,0:T(8,128)(2,1)S(1)} %bitcast.48), channel_id=1, replica_groups=mesh['row'=16,'col'=8] {'row'}, dimensions={0} | all-to-all | bytes 1572864 | tf_op jit(solution)/shard_map/all_to_all | solution.py:335
  137.2 2.4 %collective-permute-done.15 = bf16[192,128]{1,0:T(8,128)(2,1)S(1)} collective-permute-done((bf16[192,128]{1,0:T(8,128)(2,1)S(1)}, bf16[192,128]{1,0:T(8,128)(2,1)S(1)}, u32[]{:S(2)}, u32[]{:S(2)}) %collective-permute-start.15) | collective-permute-done | bytes 49184 | tf_op jit(solution)/shard_map/ppermute | solution.py:225
  139.6 3.0 %collective-permute-start.16 = (bf16[192,128]{1,0:T(8,128)(2,1)S(1)}, bf16[192,128]{1,0:T(8,128)(2,1)S(1)}, u32[]{:S(2)}, u32[]{:S(2)}) collective-permute-start(bf16[192,128]{1,0:T(8,128)(2,1)S(1)} %get-tuple-element.31), channel_id=1, source_target_pairs={{0,4},{1,5},{2,6},{3,7},{4,0},{5,1},{6,2},{7,3},{8,12},{9,13},{10,... | collective-permute-start | bytes 147464 | tf_op jit(solution)/shard_map/ppermute | solution.py:225
  142.6 2.7 %collective-permute-done.16.last_ref = bf16[192,128]{1,0:T(8,128)(2,1)S(1)} collective-permute-done((bf16[192,128]{1,0:T(8,128)(2,1)S(1)}, bf16[192,128]{1,0:T(8,128)(2,1)S(1)}, u32[]{:S(2)}, u32[]{:S(2)}) %collective-permute-start.16) | collective-permute-done | bytes 49184 | tf_op jit(solution)/shard_map/ppermute | solution.py:225
  145.9 15.3 %all_to_all.22 = bf16[16,24,1024]{2,1,0:T(8,128)(2,1)S(1)} all-to-all(bf16[16,24,1024]{2,1,0:T(8,128)(2,1)S(1)} %bitcast.42), channel_id=1, replica_groups=mesh['row'=16,'col'=8] {'row'}, dimensions={0} | all-to-all | bytes 1572864 | tf_op jit(solution)/shard_map/all_to_all | solution.py:366
  (53 shorter events, 21.8 us)
Async XLA Ops:
  6.5 4.7 %copy-start.6 = (s32[128]{0:T(128)S(1)}, s32[128]{0:T(128)}, u32[]{:S(2)}) copy-start(s32[128]{0:T(128)} %param.19) | copy-start | bytes 1540
  6.5 87.5 %all-gather.4.cloned.1.call-start = ((), (), s32[]{:S(2)}) async-start(), calls=%async_computation.4 | async-start | bytes 5242880 | tf_op jit(solution)/shard_map/all_gather | solution.py:342
  7.8 15.3 %collective-permute-start = (bf16[256,1024]{1,0:T(8,128)(2,1)S(1)}, bf16[256,1024]{1,0:T(8,128)(2,1)S(1)}, u32[]{:S(2)}, u32[]{:S(2)}) collective-permute-start(bf16[256,1024]{1,0:T(8,128)(2,1)S(1)} %get-tuple-element.36), channel_id=1, source_target_pairs={{0,16},{8,24},{16,0},{24,8},{32,48},{40,56},{48,32},{56,40},{64,80... | collective-permute-start | bytes 1572872 | tf_op jit(solution)/shard_map/ppermute | solution.py:330
  23.1 22.8 %copy-start = (bf16[2,8,64,1024]{3,2,1,0:T(8,128)(2,1)S(1)}, bf16[2,8,64,1024]{3,2,1,0:T(8,128)(2,1)}, u32[]{:S(2)}) copy-start(bf16[2,8,64,1024]{3,2,1,0:T(8,128)(2,1)} %param.21) | copy-start | bytes 6291460
  23.1 22.8 %copy-start.4 = (bf16[2,8,1024]{2,1,0:T(8,128)(2,1)S(1)}, bf16[2,8,1024]{2,1,0:T(8,128)(2,1)}, u32[]{:S(2)}) copy-start(bf16[2,8,1024]{2,1,0:T(8,128)(2,1)} %mean_ref.3) | copy-start | bytes 98308
  46.6 1.3 collective-permute-start.1
  47.9 4.2 %collective-permute-start.2 = (bf16[192,128]{1,0:T(8,128)(2,1)S(1)}, bf16[192,128]{1,0:T(8,128)(2,1)S(1)}, u32[]{:S(2)}, u32[]{:S(2)}) collective-permute-start(bf16[192,128]{1,0:T(8,128)(2,1)S(1)} %fusion.2), channel_id=1, source_target_pairs={{0,2},{1,3},{2,0},{3,1},{4,6},{5,7},{6,4},{7,5},{8,10},{9,11},{10,... | collective-permute-start | bytes 147464 | tf_op jit(solution)/shard_map/ppermute | solution.py:225
  52.1 5.7 %collective-permute-start.3 = (bf16[192,128]{1,0:T(8,128)(2,1)S(1)}, bf16[192,128]{1,0:T(8,128)(2,1)S(1)}, u32[]{:S(2)}, u32[]{:S(2)}) collective-permute-start(bf16[192,128]{1,0:T(8,128)(2,1)S(1)} %get-tuple-element.33), channel_id=1, source_target_pairs={{0,4},{1,5},{2,6},{3,7},{4,0},{5,1},{6,2},{7,3},{8,12},{9,13},{10,... | collective-permute-start | bytes 147464 | tf_op jit(solution)/shard_map/ppermute | solution.py:225
  60.5 18.0 %all-to-all-start.1 = ((bf16[16,96,256]{2,1,0:T(8,128)(2,1)}), bf16[16,96,256]{2,1,0:T(8,128)(2,1)S(1)}, u32[]{:S(2)}, u32[]{:S(2)}) async-start(bf16[16,96,256]{2,1,0:T(8,128)(2,1)} %copy-done.2), calls=%async_computation.1 | async-start | bytes 1572864 | tf_op jit(solution)/shard_map/all_to_all | solution.py:349
  78.9 10.0 %collective-permute-start.6 = (bf16[512,256]{1,0:T(8,128)(2,1)S(1)}, bf16[512,256]{1,0:T(8,128)(2,1)S(1)}, u32[]{:S(2)}, u32[]{:S(2)}) collective-permute-start(bf16[512,256]{1,0:T(8,128)(2,1)S(1)} %compact.1.refs_0_), channel_id=1, source_target_pairs={{0,4},{1,5},{2,6},{3,7},{4,0},{5,1},{6,2},{7,3},{8,12},{9,13},{10,... | collective-permute-start | bytes 786440 | tf_op jit(solution)/shard_map/ppermute | solution.py:225
  82.4 9.1 %collective-permute-start.5 = (bf16[512,256]{1,0:T(8,128)(2,1)S(1)}, bf16[512,256]{1,0:T(8,128)(2,1)S(1)}, u32[]{:S(2)}, u32[]{:S(2)}) collective-permute-start(bf16[512,256]{1,0:T(8,128)(2,1)S(1)} %compact.1.refs_0_), channel_id=1, source_target_pairs={{0,6},{1,7},{2,0},{3,1},{4,2},{5,3},{6,4},{7,5},{8,14},{9,15},{10,... | collective-permute-start | bytes 786440 | tf_op jit(solution)/shard_map/ppermute | solution.py:225
  83.6 8.8 %collective-permute-start.4 = (bf16[512,256]{1,0:T(8,128)(2,1)S(1)}, bf16[512,256]{1,0:T(8,128)(2,1)S(1)}, u32[]{:S(2)}, u32[]{:S(2)}) collective-permute-start(bf16[512,256]{1,0:T(8,128)(2,1)S(1)} %compact.1.refs_0_), channel_id=1, source_target_pairs={{0,2},{1,3},{2,4},{3,5},{4,6},{5,7},{6,0},{7,1},{8,10},{9,11},{10,... | collective-permute-start | bytes 786440 | tf_op jit(solution)/shard_map/ppermute | solution.py:225
  84.4 8.0 %collective-permute-start.7 = (bf16[512,256]{1,0:T(8,128)(2,1)S(1)}, bf16[512,256]{1,0:T(8,128)(2,1)S(1)}, u32[]{:S(2)}, u32[]{:S(2)}) collective-permute-start(bf16[512,256]{1,0:T(8,128)(2,1)S(1)} %compact.1.refs_0_), channel_id=1, source_target_pairs={{0,1},{1,0},{2,3},{3,2},{4,5},{5,4},{6,7},{7,6},{8,9},{9,8},{10,11... | collective-permute-start | bytes 786440 | tf_op jit(solution)/shard_map/ppermute | solution.py:225
  88.9 3.5 %collective-permute-start.10 = (bf16[512,256]{1,0:T(8,128)(2,1)S(1)}, bf16[512,256]{1,0:T(8,128)(2,1)}, u32[]{:S(2)}, u32[]{:S(2)}) collective-permute-start(bf16[512,256]{1,0:T(8,128)(2,1)S(1)} %collective-permute-done.6.refs_3_), channel_id=1, source_target_pairs={{0,1},{1,0},{2,3},{3,2},{4,5},{5,4},{6,7},{7,6},{8,9},{9,8},{10,11... | collective-permute-start | bytes 786440 | tf_op jit(solution)/shard_map/ppermute | solution.py:225
  91.5 1.7 collective-permute-start.9
  92.3 1.7 collective-permute-start.8
  94.0 21.9 %copy-start.5 = (bf16[128,1024]{1,0:T(8,128)(2,1)S(1)}, bf16[128,1024]{1,0:T(8,128)(2,1)}, u32[]{:S(2)}) copy-start(bf16[128,1024]{1,0:T(8,128)(2,1)} %param.17) | copy-start | bytes 786436
  99.0 10.2 %collective-permute-start.11 = (bf16[128,1024]{1,0:T(8,128)(2,1)S(1)}, bf16[128,1024]{1,0:T(8,128)(2,1)S(1)}, u32[]{:S(2)}, u32[]{:S(2)}) collective-permute-start(bf16[128,1024]{1,0:T(8,128)(2,1)S(1)} %get-tuple-element.24), channel_id=1, source_target_pairs={{0,8},{8,16},{16,24},{24,0},{32,40},{40,48},{48,56},{56,32},{64,72... | collective-permute-start | bytes 786440 | tf_op jit(solution)/shard_map/ppermute | solution.py:229
  100.9 13.2 %collective-permute-start.12 = (bf16[128,1024]{1,0:T(8,128)(2,1)S(1)}, bf16[128,1024]{1,0:T(8,128)(2,1)S(1)}, u32[]{:S(2)}, u32[]{:S(2)}) collective-permute-start(bf16[128,1024]{1,0:T(8,128)(2,1)S(1)} %get-tuple-element.25), channel_id=1, source_target_pairs={{0,24},{8,0},{16,8},{24,16},{32,56},{40,32},{48,40},{56,48},{64,88... | collective-permute-start | bytes 786440 | tf_op jit(solution)/shard_map/ppermute | solution.py:229
  102.6 13.3 %collective-permute-start.13 = (bf16[128,1024]{1,0:T(8,128)(2,1)S(1)}, bf16[128,1024]{1,0:T(8,128)(2,1)S(1)}, u32[]{:S(2)}, u32[]{:S(2)}) collective-permute-start(bf16[128,1024]{1,0:T(8,128)(2,1)S(1)} %get-tuple-element.26), channel_id=1, source_target_pairs={{0,16},{8,24},{16,0},{24,8},{32,48},{40,56},{48,32},{56,40},{64,80... | collective-permute-start | bytes 786440 | tf_op jit(solution)/shard_map/ppermute | solution.py:229
  133.4 11.9 %copy-start.1 = (bf16[2,8,64,1024]{3,2,1,0:T(8,128)(2,1)S(1)}, bf16[2,8,64,1024]{3,2,1,0:T(8,128)(2,1)}, u32[]{:S(2)}) copy-start(bf16[2,8,64,1024]{3,2,1,0:T(8,128)(2,1)} %param.22) | copy-start | bytes 6291460
  134.1 1.3 collective-permute-start.14
  135.4 4.2 %collective-permute-start.15 = (bf16[192,128]{1,0:T(8,128)(2,1)S(1)}, bf16[192,128]{1,0:T(8,128)(2,1)S(1)}, u32[]{:S(2)}, u32[]{:S(2)}) collective-permute-start(bf16[192,128]{1,0:T(8,128)(2,1)S(1)} %fusion.3), channel_id=1, source_target_pairs={{0,2},{1,3},{2,0},{3,1},{4,6},{5,7},{6,4},{7,5},{8,10},{9,11},{10,... | collective-permute-start | bytes 147464 | tf_op jit(solution)/shard_map/ppermute | solution.py:225
  139.6 5.7 %collective-permute-start.16 = (bf16[192,128]{1,0:T(8,128)(2,1)S(1)}, bf16[192,128]{1,0:T(8,128)(2,1)S(1)}, u32[]{:S(2)}, u32[]{:S(2)}) collective-permute-start(bf16[192,128]{1,0:T(8,128)(2,1)S(1)} %get-tuple-element.31), channel_id=1, source_target_pairs={{0,4},{1,5},{2,6},{3,7},{4,0},{5,1},{6,2},{7,3},{8,12},{9,13},{10,... | collective-permute-start | bytes 147464 | tf_op jit(solution)/shard_map/ppermute | solution.py:225
  (3 other events, 6.5 us)
Sparse Core Ops, SparseCore 0:
  24.3 62.5 all-gather.3

commit v3 on v2

--- a/solution.py
+++ b/solution.py
@@ -13,7 +13,9 @@
 HD = 128
 MOST = 3
 ROWS = 16
+COLS = 8
 RING = 4
+AROUND = (0, 3, 1, 2)
 SLOTS = 8
 RANK = 64
 PART = SLOTS * MOST
@@ -24,8 +26,6 @@
 WIDTH = 1024
 QUARTER = WIDTH // RING
 
-ALONG_Z = [[z * RING + y for z in range(RING)] for y in range(RING)]
-ALONG_Y = [[z * RING + y for y in range(RING)] for z in range(RING)]
 BF = jnp.bfloat16
 F32 = jnp.float32
 
@@ -168,8 +168,9 @@
     )(rows, mean_bank, read_bank.reshape(2, SLOTS * RANK, WIDTH))
 
 
-def erased_rows(rows_ref, sum_ref, last_ref, write_ref):
-    total = sum_ref[...] + last_ref[...].astype(F32)
+def erased_rows(rows_ref, sum_ref, sum1_ref, sum2_ref, sum3_ref, write_ref):
+    total = sum_ref[...] + sum1_ref[...].astype(F32)
+    total = total + sum2_ref[...].astype(F32) + sum3_ref[...].astype(F32)
     both = jnp.concatenate([total, pltpu.roll(total, RANK, 1)], axis=0)
     wide = jnp.concatenate([both] * (SLOTS * RANK // 128), axis=1)
     wide = jnp.where(slot_mask(PACKED), wide, 0.0).astype(BF)
@@ -177,8 +178,8 @@
     return rows_ref[...].astype(F32) - delta.astype(F32)
 
 
-def spread_body(core_ref, rows_ref, sum_ref, last_ref, write_ref, out_ref):
-    erased = erased_rows(rows_ref, sum_ref, last_ref, write_ref).astype(BF).astype(F32)
+def spread_body(core_ref, rows_ref, sum_ref, sum1_ref, sum2_ref, sum3_ref, write_ref, out_ref):
+    erased = erased_rows(rows_ref, sum_ref, sum1_ref, sum2_ref, sum3_ref, write_ref).astype(BF).astype(F32)
     first_core = core_ref[0] == 0
     for y in range(RING):
         start = QUARTER * 2 * (y % 2)
@@ -193,11 +194,11 @@
             out_ref[z * RING + y] = jnp.concatenate(pieces, axis=0).astype(BF)
 
 
-def home_body(rows_ref, sum_ref, last_ref, write_ref, out_ref):
-    out_ref[...] = erased_rows(rows_ref, sum_ref, last_ref, write_ref).astype(BF)
-
-
-def apply_eraser(body, rows, summed, last, write_bank, site, shape, extra=()):
+def home_body(rows_ref, sum_ref, sum1_ref, sum2_ref, sum3_ref, write_ref, out_ref):
+    out_ref[...] = erased_rows(rows_ref, sum_ref, sum1_ref, sum2_ref, sum3_ref, write_ref).astype(BF)
+
+
+def apply_eraser(body, rows, summed, others, write_bank, site, shape, extra=()):
     write_bank = write_bank.reshape(2, SLOTS * RANK, WIDTH)
     if site == 0:
         write_bank = in_hbm(write_bank)[0]
@@ -207,8 +208,7 @@
         in_specs=[pl.BlockSpec(memory_space=pltpu.SMEM)] * len(extra)
         + [
             whole((PACKED, WIDTH)),
-            whole((PACKED // 2, 128)),
-            whole((PACKED // 2, 128)),
+            *[whole((PACKED // 2, 128))] * RING,
             pl.BlockSpec((None, SLOTS * RANK, WIDTH), lambda i: (site, 0, 0)),
         ],
         out_specs=whole(shape),
@@ -218,7 +218,7 @@
             flops=2 * PACKED * WIDTH * SLOTS * RANK, bytes_accessed=3 << 20, transcendentals=0
         ),
         name="erase",
-    )(*extra, rows, summed, last, write_bank)
+    )(*extra, rows, summed, *others, write_bank)
 
 
 def along_col(values, move):
@@ -231,18 +231,23 @@
     )
 
 
-def sum_but_last(partial, short):
-    for bit in (1, 2):
-        partial = partial + along_col(short, lambda i: i ^ bit).astype(F32)
-        short = partial.astype(BF)
-    return partial, along_col(short, lambda i: i ^ 4)
-
-
-def compact_body(y_ref, target_ref, rows_ref, out_ref):
+def along_z(values, step):
+    return lax.ppermute(values, "row", [(i, (i + RING * step) % ROWS) for i in range(ROWS)])
+
+
+def gather_sums(partial, short):
+    partial = partial + along_col(short, lambda i: i ^ 1).astype(F32)
+    short = partial.astype(BF)
+    return partial, [along_col(short, lambda i, by=by: (i + by) % COLS) for by in (4, 2, 6)]
+
+
+def compact_body(*refs):
+    targets, rows_ref, out_ref = refs[:RING], refs[RING], refs[RING + 1]
     rows = rows_ref[...].astype(F32)
     for step in range(RING):
-        target = target_ref[pl.ds((y_ref[0] + step) & 3, 1), :]
-        table = (lax.broadcasted_iota(jnp.int32, (PACKED, BLOCK), 0) == target).astype(BF)
+        table = (
+            lax.broadcasted_iota(jnp.int32, (PACKED, BLOCK), 0) == targets[step][...]
+        ).astype(BF)
         part = rows[:, PART * step : PART * (step + 1), :].reshape(PACKED, QUARTER).astype(BF)
         picked = lax.dot_general(
             table, part, (((0,), (0,)), ((), ())), preferred_element_type=F32
@@ -250,64 +255,82 @@
         out_ref[BLOCK * step : BLOCK * (step + 1), :] = picked.astype(BF)
 
 
-def compact(y, targets, rows):
+def compact(targets, rows):
     return pl.pallas_call(
         compact_body,
-        grid_spec=pltpu.PrefetchScalarGridSpec(
-            num_scalar_prefetch=1,
-            grid=(1,),
-            in_specs=[whole((RING, BLOCK)), whole((ROWS, RING * PART, QUARTER))],
-            out_specs=whole((RING * BLOCK, QUARTER)),
-        ),
+        grid=(1,),
+        in_specs=[whole((1, BLOCK))] * RING + [whole((ROWS, RING * PART, QUARTER))],
+        out_specs=whole((RING * BLOCK, QUARTER)),
         out_shape=jax.ShapeDtypeStruct((RING * BLOCK, QUARTER), BF),
         compiler_params=params(16),
         cost_estimate=pl.CostEstimate(
             flops=2 * RING * BLOCK * PACKED * QUARTER, bytes_accessed=1 << 20, transcendentals=0
         ),
         name="compact",
-    )(y, targets, rows)
-
-
-def project_body(scalar_ref, *refs):
+    )(*targets, rows)
+
+
+def project_body(place_ref, *refs):
     same, other = refs[0:RING], refs[RING : 2 * RING]
-    weight_ref, far_ref, up_ref, down_ref, own_ref = refs[2 * RING :]
-    near = pl.multiple_of(scalar_ref[1] * QUARTER, QUARTER)
+    kept, swapped = refs[2 * RING : 3 * RING], refs[3 * RING : 4 * RING]
+    far_ref, up_ref, down_ref, own_ref, weight_ref, sems = refs[4 * RING :]
+    x, near, z = place_ref[0], place_ref[1], place_ref[2]
+    copies = {}
+    for step, offset in enumerate(AROUND):
+        block = (z + offset) & 3
+        for which, source in enumerate((kept[step], swapped[step])):
+            copies[step, which] = pltpu.make_async_copy(
+                source.at[pl.ds(0, QUARTER), :],
+                weight_ref.at[block, pl.ds(which * QUARTER, QUARTER), :],
+                sems.at[step, which],
+            )
+            copies[step, which].start()
+    for copy in copies.values():
+        copy.wait()
+    near = pl.multiple_of(near * QUARTER, QUARTER)
     away = pl.multiple_of(QUARTER - near, QUARTER)
-    product = jnp.zeros((RING * BLOCK, TILE), F32)
-    for step, offset in enumerate((0, 3, 1, 2)):
-        z = (scalar_ref[0] + offset) & 3
-        product += jnp.dot(
-            same[step][...], weight_ref[z, pl.ds(near, QUARTER), :], preferred_element_type=F32
-        )
-        product += jnp.dot(
-            other[step][...], weight_ref[z, pl.ds(away, QUARTER), :], preferred_element_type=F32
-        )
-    own_ref[...] = product[:BLOCK]
-    up_ref[...] = product[BLOCK : 2 * BLOCK].astype(BF)
-    far_ref[...] = product[2 * BLOCK : 3 * BLOCK].astype(BF)
-    down_ref[...] = product[3 * BLOCK :].astype(BF)
-
-
-def project(scalars, same, other, weight):
-    act = whole((RING * BLOCK, QUARTER))
-    out = pl.BlockSpec((BLOCK, TILE), lambda i, s: (0, i))
+    for tile in range(0, WIDTH, TILE):
+        columns = pl.ds(tile, TILE)
+        product = jnp.zeros((RING * BLOCK, TILE), F32)
+        for step, offset in enumerate(AROUND):
+            block = (x + offset) & 3
+            product += jnp.dot(
+                same[step][...],
+                weight_ref[block, pl.ds(near, QUARTER), columns],
+                preferred_element_type=F32,
+            )
+            product += jnp.dot(
+                other[step][...],
+                weight_ref[block, pl.ds(away, QUARTER), columns],
+                preferred_element_type=F32,
+            )
+        own_ref[:, columns] = product[:BLOCK]
+        up_ref[:, columns] = product[BLOCK : 2 * BLOCK].astype(BF)
+        far_ref[:, columns] = product[2 * BLOCK : 3 * BLOCK].astype(BF)
+        down_ref[:, columns] = product[3 * BLOCK :].astype(BF)
+
+
+def project(place, same, other, kept, swapped):
+    out = whole((BLOCK, WIDTH))
     sent = jax.ShapeDtypeStruct((BLOCK, WIDTH), BF)
     return pl.pallas_call(
         project_body,
-        grid_spec=pltpu.PrefetchScalarGridSpec(
-            num_scalar_prefetch=1,
-            grid=(WIDTH // TILE,),
-            in_specs=[act] * 8
-            + [pl.BlockSpec((RING, 2 * QUARTER, TILE), lambda i, s: (0, 0, i))],
-            out_specs=[out] * 4,
-        ),
+        grid=(1,),
+        in_specs=[pl.BlockSpec(memory_space=pltpu.SMEM)]
+        + [whole((RING * BLOCK, QUARTER))] * 8
+        + [pl.BlockSpec(memory_space=pltpu.HBM)] * 8,
+        out_specs=[out] * 4,
         out_shape=[sent, sent, sent, jax.ShapeDtypeStruct((BLOCK, WIDTH), F32)],
+        scratch_shapes=[
+            pltpu.VMEM((RING, 2 * QUARTER, WIDTH), BF),
+            pltpu.SemaphoreType.DMA((RING, 2)),
+        ],
         compiler_params=params(20),
         cost_estimate=pl.CostEstimate(
             flops=2 * RING * BLOCK * 8 * QUARTER * WIDTH, bytes_accessed=7 << 20, transcendentals=0
         ),
         name="project",
-    )(scalars, *same, *other, *in_hbm(weight))
+    )(place, *in_hbm(*same, *other, *kept, *swapped))
 
 
 def local(
@@ -325,9 +348,11 @@
     mean_bank,
 ):
     row, col = lax.axis_index("row"), lax.axis_index("col")
-    x, core, y, upper = col >> 1, col & 1, row & 3, (row & 3) >> 1
+    x, core, y, z = col >> 1, col & 1, row & 3, row >> 2
     half = out_weight.shape[0] // 2
-    swapped = lax.ppermute(out_weight[half:], "row", [(i, i ^ 2) for i in range(ROWS)])
+    kept0 = out_weight[:half]
+    swapped0 = lax.ppermute(out_weight[half:], "row", [(i, i ^ 2) for i in range(ROWS)])
+    kept1, kept2 = along_z(kept0, 1), along_z(kept0, 3)
     target = packed_position(tenant, tenant_slot_index)
 
     def dispatch(packed):
@@ -337,32 +362,37 @@
     packed, target = attend_and_pack(
         queries, new_keys, new_values, key_cache, value_cache, target[None]
     )
-    swapped, target = lax.optimization_barrier((swapped, target))
-    weight = jnp.concatenate([out_weight[:half], swapped], axis=0)
-    weight = lax.all_gather(weight, "row", axis_index_groups=ALONG_Z)
+    targets = [target] + [along_y(target, by) for by in (3, 2, 1)]
+    swapped0, kept1, kept2, packed = lax.optimization_barrier((swapped0, kept1, kept2, packed))
     rows = dispatch(packed)
-    targets = lax.all_gather(target[0], "row", axis_index_groups=ALONG_Y)
     table = (jnp.arange(PACKED, dtype=jnp.int32)[:, None] == target).astype(BF)
-    summed, last = sum_but_last(*partial_coefs(rows, mean_bank, read_bank, 0))
+    partial, short = partial_coefs(rows, mean_bank, read_bank, 0)
+    swapped0, short = lax.optimization_barrier((swapped0, short))
+    swapped1, swapped2 = along_z(swapped0, 1), along_z(swapped0, 3)
+    summed, others = gather_sums(partial, short)
     shape = (ROWS, RING * PART, QUARTER)
-    cleaned = apply_eraser(spread_body, rows, summed, last, write_bank, 0, shape, (core[None],))
+    cleaned = apply_eraser(spread_body, rows, summed, others, write_bank, 0, shape, (core[None],))
+    swapped1, swapped2, cleaned = lax.optimization_barrier((swapped1, swapped2, cleaned))
     cleaned = lax.all_to_all(cleaned, "row", 0, 0, tiled=True)
-    here = compact(y[None], targets, cleaned)
+    kept1, swapped2, cleaned = lax.optimization_barrier((kept1, swapped2, cleaned))
+    kept3, swapped3 = along_z(kept1, 1), along_z(swapped2, 3)
+    here = compact(targets, cleaned)
 
     after = along_col(here, lambda i: (i + 2) % 8)
     before = along_col(here, lambda i: (i - 2) % 8)
     across = along_col(here, lambda i: (i + 4) % 8)
     same = [here, after, before, across]
     other = [along_col(part, lambda i: i ^ 1) for part in same]
-    place = jnp.stack([x, core ^ upper])
-    far, up, down, own = project(place, same, other, weight)
+    place = jnp.stack([x, core ^ (y >> 1), z])
+    kept, swapped = [out_weight, kept1, kept2, kept3], [swapped0, swapped1, swapped2, swapped3]
+    far, up, down, own = project(place, same, other, kept, swapped)
     far, up, down = along_y(far, 2), along_y(up, 1), along_y(down, 3)
     projected = own + up.astype(F32) + down.astype(F32) + far.astype(F32)
     hidden = (residual.astype(F32) + projected).astype(BF)
 
     rows = dispatch(jnp.dot(table, hidden, preferred_element_type=F32).astype(BF))
-    summed, last = sum_but_last(*partial_coefs(rows, mean_bank, read_bank, 1))
-    erased = apply_eraser(home_body, rows, summed, last, write_bank, 1, (PACKED, WIDTH))
+    summed, others = gather_sums(*partial_coefs(rows, mean_bank, read_bank, 1))
+    erased = apply_eraser(home_body, rows, summed, others, write_bank, 1, (PACKED, WIDTH))
     erased = lax.all_to_all(erased.reshape(ROWS, PART, WIDTH), "row", 0, 0, tiled=True)
     return lax.dot_general(
         table,

time: 170 us -> 159 us (0.935)
  blocking collectives: 66.9 us -> 48.4 us
  between operations: 13.5 us -> 0.22 us
  starting transfers between devices: 27.9 us -> 40.4 us
  waiting for transfers between devices: 37.2 us -> 45.4 us
    all_gather x1 -> x0, blocking collectives: 13 us -> none  [local(): targets = lax.all_gather(target[0], 'row', axis_index_groups=ALONG_Y)]
    ppermute x0 -> x6, starting transfers between devices: none -> 9.37 us  [along_z(): lax.ppermute(values, 'row', [(i, (i + RING * step) % ROWS) for i in range...]
    all_to_all x2, blocking collectives: 38.7 us -> 32.2 us  [dispatch(): lax.all_to_all(packed, 'row', 0, 0, tiled=True).reshape(PACKED, WIDTH)]
    ppermute x0 -> x6, waiting for transfers between devices: none -> 6.34 us  [along_z(): lax.ppermute(values, 'row', [(i, (i + RING * step) % ROWS) for i in range...]
    all_to_all x1, waiting for transfers between devices: 1.39 us -> 7.27 us  [local(): cleaned = lax.all_to_all(cleaned, 'row', 0, 0, tiled=True)]
    ppermute x3 -> x6, starting transfers between devices: 5.8 us -> 9.37 us  [along_y(): lax.ppermute(values, 'row', [(i, i // RING * RING + (i + step) % RING) fo...]
    ppermute x1, waiting for transfers between devices: 2.44 us -> 0.01 us  [local(): lax.ppermute(out_weight[half:], 'row', [(i, i ^ 2) for i in range(ROWS)])]
    ppermute x13 -> x15, waiting for transfers between devices: 22.2 us -> 20.6 us  [along_col(): return lax.ppermute(values, 'col', [(i, move(i)) for i in range(8)])]
  transfers between devices with their start and end apart: 19 -> 29, of which waited for: 16 -> 14; matrix products, arithmetic and copies ran while one was open for 0% -> 0% of each run, Pallas kernels for 7% -> 7%
where the time goes in v3:
time: 159 us
  blocking collectives  48.4 us (30%)
  waiting for transfers between devices  45.4 us (29%)
  starting transfers between devices  40.4 us (25%)
  Pallas kernels  18.8 us (12%)
  local copies, waits for them, and re-layouts  3.8 us (2%)
    all_to_all x2, blocking collectives, dispatch(): lax.all_to_all(packed, 'row', 0, 0, tiled=True).reshape(PACKED, WIDTH)  32.2 us
    ppermute x15, waiting for transfers between devices, along_col(): return lax.ppermute(values, 'col', [(i, move(i)) for i in range(8)])  20.6 us
    all_to_all x1, blocking collectives, local(): lax.all_to_all(erased.reshape(ROWS, PART, WIDTH), 'row', 0, 0, tiled=True)  16.2 us
    ppermute x15, starting transfers between devices, along_col(): return lax.ppermute(values, 'col', [(i, move(i)) for i in range(8)])  14.2 us
    ppermute x6, waiting for transfers between devices, along_y(): lax.ppermute(values, 'row', [(i, i // RING * RING + (i + step) % RING) fo...  11.2 us
    ppermute x6, starting transfers between devices, along_y(): lax.ppermute(values, 'row', [(i, i // RING * RING + (i + step) % RING) fo...  9.37 us
    ppermute x6, starting transfers between devices, along_z(): lax.ppermute(values, 'row', [(i, (i + RING * step) % ROWS) for i in range...  9.37 us
    pallas_call x1, Pallas kernels, attend_and_pack(): pl.pallas_call(attend_body, grid=(BLOCK // CHUNK,), in_specs=[by_row(WIDT...  8.51 us
  transfers between devices with their start and end apart: 29, of which 14 were waited for; matrix products, arithmetic and copies ran while one was open for 0% of the time, Pallas kernels for 7%

profile of v3, /device:TPU:0, one launch (start us, length us, event | category | flops | bytes accessed | tf_op | source)
XLA Modules:
  0.0 158.7 jit_solution(797877985152913340)
XLA Ops:
  1.3 3.4 %collective-permute-start.3 = (bf16[256,1024]{1,0:T(8,128)(2,1)S(1)}, bf16[256,1024]{1,0:T(8,128)(2,1)}, u32[]{:S(2)}, u32[]{:S(2)}) collective-permute-start(bf16[256,1024]{1,0:T(8,128)(2,1)S(1)} %get-tuple-element.56), channel_id=1, source_target_pairs={{0,16},{8,24},{16,0},{24,8},{32,48},{40,56},{48,32},{56,40},{64,80... | collective-permute-start | bytes 1572872 | tf_op jit(solution)/shard_map/ppermute | solution.py:354
  4.7 4.0 %collective-permute-start.5 = (bf16[256,1024]{1,0:T(8,128)(2,1)S(1)}, bf16[256,1024]{1,0:T(8,128)(2,1)S(1)}, u32[]{:S(2)}, u32[]{:S(2)}) collective-permute-start(bf16[256,1024]{1,0:T(8,128)(2,1)S(1)} %get-tuple-element.55), channel_id=1, source_target_pairs={{0,96},{8,104},{16,112},{24,120},{32,0},{40,8},{48,16},{56,24},{64... | collective-permute-start | bytes 1572872 | tf_op jit(solution)/shard_map/ppermute | solution.py:235
  8.9 8.5 %attend.1 = (bf16[384,1024]{1,0:T(8,128)(2,1)S(1)}, s32[1,128]{1,0:T(1,128)S(1)}) custom-call(bf16[128,1024]{1,0:T(8,128)(2,1)} %q_ref.1, bf16[128,128]{1,0:T(8,128)(2,1)} %key_ref.1, bf16[128,128]{1,0:T(8,128)(2,1)} %value_ref.1, s32[1,128]{1,0:T(1,128)S(1)} %fusion.3.target_ref, bf16[128,256,128]{2,1,0:T(8,128)(2,1)} %keys_ref.1, ...), custom_call_target="tpu_custom_call" | custom-call | flops 134217728 | bytes 17825792 | tf_op jit(solution)/shard_map/attend/pallas_call | solution.py:91
  17.5 2.1 %collective-permute-done.5.refs_10_ = bf16[256,1024]{1,0:T(8,128)(2,1)S(1)} collective-permute-done((bf16[256,1024]{1,0:T(8,128)(2,1)S(1)}, bf16[256,1024]{1,0:T(8,128)(2,1)S(1)}, u32[]{:S(2)}, u32[]{:S(2)}) %collective-permute-start.5) | collective-permute-done | bytes 524320 | tf_op jit(solution)/shard_map/ppermute | solution.py:235
  19.6 3.4 %collective-permute-done.4.refs_9_ = bf16[256,1024]{1,0:T(8,128)(2,1)S(1)} collective-permute-done((bf16[256,1024]{1,0:T(8,128)(2,1)S(1)}, bf16[256,1024]{1,0:T(8,128)(2,1)S(1)}, u32[]{:S(2)}, u32[]{:S(2)}) %collective-permute-start.4) | collective-permute-done | bytes 524320 | tf_op jit(solution)/shard_map/ppermute | solution.py:235
  23.0 15.8 %all_to_all.20 = bf16[16,24,1024]{2,1,0:T(8,128)(2,1)S(1)} all-to-all(bf16[16,24,1024]{2,1,0:T(8,128)(2,1)S(1)} %bitcast.40), channel_id=1, replica_groups=mesh['row'=16,'col'=8] {'row'}, dimensions={0} | all-to-all | bytes 1572864 | tf_op jit(solution)/shard_map/all_to_all | solution.py:360
  42.8 2.8 %collective-permute-start.11 = (bf16[192,128]{1,0:T(8,128)(2,1)S(1)}, bf16[192,128]{1,0:T(8,128)(2,1)S(1)}, u32[]{:S(2)}, u32[]{:S(2)}) collective-permute-start(bf16[192,128]{1,0:T(8,128)(2,1)S(1)} %get-tuple-element.53), channel_id=1, source_target_pairs={{0,6},{1,7},{2,0},{3,1},{4,2},{5,3},{6,4},{7,5},{8,14},{9,15},{10,... | collective-permute-start | bytes 147464 | tf_op jit(solution)/shard_map/ppermute | solution.py:225
  45.7 2.3 %collective-permute-start.9 = (bf16[192,128]{1,0:T(8,128)(2,1)S(1)}, bf16[192,128]{1,0:T(8,128)(2,1)S(1)}, u32[]{:S(2)}, u32[]{:S(2)}) collective-permute-start(bf16[192,128]{1,0:T(8,128)(2,1)S(1)} %get-tuple-element.53), channel_id=1, source_target_pairs={{0,4},{1,5},{2,6},{3,7},{4,0},{5,1},{6,2},{7,3},{8,12},{9,13},{10,... | collective-permute-start | bytes 147464 | tf_op jit(solution)/shard_map/ppermute | solution.py:225
  48.0 3.6 %collective-permute-done.10.sum2_ref = bf16[192,128]{1,0:T(8,128)(2,1)S(1)} collective-permute-done((bf16[192,128]{1,0:T(8,128)(2,1)S(1)}, bf16[192,128]{1,0:T(8,128)(2,1)S(1)}, u32[]{:S(2)}, u32[]{:S(2)}) %collective-permute-start.10) | collective-permute-done | bytes 49184 | tf_op jit(solution)/shard_map/ppermute | solution.py:225
  54.4 4.1 %all-to-all-start.1 = ((bf16[16,96,256]{2,1,0:T(8,128)(2,1)}), bf16[16,96,256]{2,1,0:T(8,128)(2,1)S(1)}, u32[]{:S(2)}, u32[]{:S(2)}) async-start(bf16[16,96,256]{2,1,0:T(8,128)(2,1)} %copy-done.2), calls=%async_computation.1 | async-start | bytes 1572864 | tf_op jit(solution)/shard_map/all_to_all | solution.py:376
  58.5 1.9 %collective-permute-start.2 = (s32[1,128]{1,0:T(1,128)S(1)}, s32[1,128]{1,0:T(1,128)S(1)}, u32[]{:S(2)}, u32[]{:S(2)}) collective-permute-start(s32[1,128]{1,0:T(1,128)S(1)} %get-tuple-element.27.refs_0_), channel_id=1, source_target_pairs={{0,8},{8,16},{16,24},{24,0},{32,40},{40,48},{48,56},{56,32},{64,72... | collective-permute-start | bytes 1544 | tf_op jit(solution)/shard_map/ppermute | solution.py:229
  60.4 2.7 %collective-permute-start.1 = (s32[1,128]{1,0:T(1,128)S(1)}, s32[1,128]{1,0:T(1,128)S(1)}, u32[]{:S(2)}, u32[]{:S(2)}) collective-permute-start(s32[1,128]{1,0:T(1,128)S(1)} %get-tuple-element.27.refs_0_), channel_id=1, source_target_pairs={{0,16},{8,24},{16,0},{24,8},{32,48},{40,56},{48,32},{56,40},{64,80... | collective-permute-start | bytes 1544 | tf_op jit(solution)/shard_map/ppermute | solution.py:229
  64.5 7.3 %all-to-all-done.1.refs_4_ = bf16[16,96,256]{2,1,0:T(8,128)(2,1)S(1)} async-done(((bf16[16,96,256]{2,1,0:T(8,128)(2,1)}), bf16[16,96,256]{2,1,0:T(8,128)(2,1)S(1)}, u32[]{:S(2)}, u32[]{:S(2)}) %all-to-all-start.1) | async-done | bytes 786464 | tf_op jit(solution)/shard_map/all_to_all | solution.py:376
  72.3 2.1 %collective-permute-start.14 = (bf16[512,256]{1,0:T(8,128)(2,1)S(1)}, bf16[512,256]{1,0:T(8,128)(2,1)}, u32[]{:S(2)}, u32[]{:S(2)}) collective-permute-start(bf16[512,256]{1,0:T(8,128)(2,1)S(1)} %compact.1.refs_0_), channel_id=1, source_target_pairs={{0,4},{1,5},{2,6},{3,7},{4,0},{5,1},{6,2},{7,3},{8,12},{9,13},{10,... | collective-permute-start | bytes 786440 | tf_op jit(solution)/shard_map/ppermute | solution.py:225
  76.4 3.2 %collective-permute-start.20 = (bf16[256,1024]{1,0:T(8,128)(2,1)}, bf16[256,1024]{1,0:T(8,128)(2,1)S(1)}, u32[]{:S(2)}, u32[]{:S(2)}) collective-permute-start(bf16[256,1024]{1,0:T(8,128)(2,1)} %collective-permute-done.7.refs_14_), channel_id=1, source_target_pairs={{0,96},{8,104},{16,112},{24,120},{32,0},{40,8},{48,16},{56,24},{64... | collective-permute-start | bytes 1572872 | tf_op jit(solution)/shard_map/ppermute | solution.py:235
  79.7 3.5 %collective-permute-done.14.refs_3_ = bf16[512,256]{1,0:T(8,128)(2,1)} collective-permute-done((bf16[512,256]{1,0:T(8,128)(2,1)S(1)}, bf16[512,256]{1,0:T(8,128)(2,1)}, u32[]{:S(2)}, u32[]{:S(2)}) %collective-permute-start.14) | collective-permute-done | bytes 262176 | tf_op jit(solution)/shard_map/ppermute | solution.py:225
  83.1 5.1 %collective-permute-done.13.refs_2_ = bf16[512,256]{1,0:T(8,128)(2,1)} collective-permute-done((bf16[512,256]{1,0:T(8,128)(2,1)S(1)}, bf16[512,256]{1,0:T(8,128)(2,1)}, u32[]{:S(2)}, u32[]{:S(2)}) %collective-permute-start.13) | collective-permute-done | bytes 262176 | tf_op jit(solution)/shard_map/ppermute | solution.py:225
  92.8 6.1 %project.1 = (bf16[128,1024]{1,0:T(8,128)(2,1)S(1)}, bf16[128,1024]{1,0:T(8,128)(2,1)S(1)}, bf16[128,1024]{1,0:T(8,128)(2,1)S(1)}, f32[128,1024]{1,0:T(8,128)S(1)}) custom-call(s32[3]{0:T(128)S(1)} %pad_add_fusion.place_ref, bf16[512,256]{1,0:T(8,128)(2,1)} %copy-done.3, bf16[512,256]{1,0:T(8,128)(2,1)} %collective-permute-done.12.refs_1_, ...), custom_call_target="tpu_custom_call" | custom-call | flops 2147483648 | bytes 7340032 | tf_op jit(solution)/shard_map/project/pallas_call | solution.py:316
  99.5 2.7 %collective-permute-start.22 = (bf16[128,1024]{1,0:T(8,128)(2,1)S(1)}, bf16[128,1024]{1,0:T(8,128)(2,1)S(1)}, u32[]{:S(2)}, u32[]{:S(2)}) collective-permute-start(bf16[128,1024]{1,0:T(8,128)(2,1)S(1)} %get-tuple-element.45), channel_id=1, source_target_pairs={{0,24},{8,0},{16,8},{24,16},{32,56},{40,32},{48,40},{56,48},{64,88... | collective-permute-start | bytes 786440 | tf_op jit(solution)/shard_map/ppermute | solution.py:229
  102.2 11.2 %collective-permute-done.21 = bf16[128,1024]{1,0:T(8,128)(2,1)S(1)} collective-permute-done((bf16[128,1024]{1,0:T(8,128)(2,1)S(1)}, bf16[128,1024]{1,0:T(8,128)(2,1)S(1)}, u32[]{:S(2)}, u32[]{:S(2)}) %collective-permute-start.21) | collective-permute-done | bytes 262176 | tf_op jit(solution)/shard_map/ppermute | solution.py:229
  113.9 16.4 %all_to_all.21 = bf16[16,24,1024]{2,1,0:T(8,128)(2,1)S(1)} all-to-all(bf16[16,24,1024]{2,1,0:T(8,128)(2,1)S(1)} %bitcast.43), channel_id=1, replica_groups=mesh['row'=16,'col'=8] {'row'}, dimensions={0} | all-to-all | bytes 1572864 | tf_op jit(solution)/shard_map/all_to_all | solution.py:360
  132.3 2.7 %collective-permute-start.27 = (bf16[192,128]{1,0:T(8,128)(2,1)S(1)}, bf16[192,128]{1,0:T(8,128)(2,1)S(1)}, u32[]{:S(2)}, u32[]{:S(2)}) collective-permute-start(bf16[192,128]{1,0:T(8,128)(2,1)S(1)} %get-tuple-element.51), channel_id=1, source_target_pairs={{0,6},{1,7},{2,0},{3,1},{4,2},{5,3},{6,4},{7,5},{8,14},{9,15},{10,... | collective-permute-start | bytes 147464 | tf_op jit(solution)/shard_map/ppermute | solution.py:225
  136.7 4.1 %collective-permute-done.26.sum2_ref = bf16[192,128]{1,0:T(8,128)(2,1)S(1)} collective-permute-done((bf16[192,128]{1,0:T(8,128)(2,1)S(1)}, bf16[192,128]{1,0:T(8,128)(2,1)S(1)}, u32[]{:S(2)}, u32[]{:S(2)}) %collective-permute-start.26) | collective-permute-done | bytes 49184 | tf_op jit(solution)/shard_map/ppermute | solution.py:225
  141.4 16.2 %all_to_all.22 = bf16[16,24,1024]{2,1,0:T(8,128)(2,1)S(1)} all-to-all(bf16[16,24,1024]{2,1,0:T(8,128)(2,1)S(1)} %bitcast.39), channel_id=1, replica_groups=mesh['row'=16,'col'=8] {'row'}, dimensions={0} | all-to-all | bytes 1572864 | tf_op jit(solution)/shard_map/all_to_all | solution.py:396
  (78 shorter events, 23.3 us)
Async XLA Ops:
  1.3 16.1 %collective-permute-start.3 = (bf16[256,1024]{1,0:T(8,128)(2,1)S(1)}, bf16[256,1024]{1,0:T(8,128)(2,1)}, u32[]{:S(2)}, u32[]{:S(2)}) collective-permute-start(bf16[256,1024]{1,0:T(8,128)(2,1)S(1)} %get-tuple-element.56), channel_id=1, source_target_pairs={{0,16},{8,24},{16,0},{24,8},{32,48},{40,56},{48,32},{56,40},{64,80... | collective-permute-start | bytes 1572872 | tf_op jit(solution)/shard_map/ppermute | solution.py:354
  4.7 14.9 %collective-permute-start.5 = (bf16[256,1024]{1,0:T(8,128)(2,1)S(1)}, bf16[256,1024]{1,0:T(8,128)(2,1)S(1)}, u32[]{:S(2)}, u32[]{:S(2)}) collective-permute-start(bf16[256,1024]{1,0:T(8,128)(2,1)S(1)} %get-tuple-element.55), channel_id=1, source_target_pairs={{0,96},{8,104},{16,112},{24,120},{32,0},{40,8},{48,16},{56,24},{64... | collective-permute-start | bytes 1572872 | tf_op jit(solution)/shard_map/ppermute | solution.py:235
  8.7 14.3 %collective-permute-start.4 = (bf16[256,1024]{1,0:T(8,128)(2,1)S(1)}, bf16[256,1024]{1,0:T(8,128)(2,1)S(1)}, u32[]{:S(2)}, u32[]{:S(2)}) collective-permute-start(bf16[256,1024]{1,0:T(8,128)(2,1)S(1)} %get-tuple-element.55), channel_id=1, source_target_pairs={{0,32},{8,40},{16,48},{24,56},{32,64},{40,72},{48,80},{56,88},{64,... | collective-permute-start | bytes 1572872 | tf_op jit(solution)/shard_map/ppermute | solution.py:235
  39.5 14.9 %collective-permute-start.7 = (bf16[256,1024]{1,0:T(8,128)(2,1)}, bf16[256,1024]{1,0:T(8,128)(2,1)}, u32[]{:S(2)}, u32[]{:S(2)}) collective-permute-start(bf16[256,1024]{1,0:T(8,128)(2,1)} %collective-permute-done.3.refs_12_), channel_id=1, source_target_pairs={{0,96},{8,104},{16,112},{24,120},{32,0},{40,8},{48,16},{56,24},{64... | collective-permute-start | bytes 1572872 | tf_op jit(solution)/shard_map/ppermute | solution.py:235
  40.4 14.0 %collective-permute-start.6 = (bf16[256,1024]{1,0:T(8,128)(2,1)}, bf16[256,1024]{1,0:T(8,128)(2,1)}, u32[]{:S(2)}, u32[]{:S(2)}) collective-permute-start(bf16[256,1024]{1,0:T(8,128)(2,1)} %collective-permute-done.3.refs_12_), channel_id=1, source_target_pairs={{0,32},{8,40},{16,48},{24,56},{32,64},{40,72},{48,80},{56,88},{64,... | collective-permute-start | bytes 1572872 | tf_op jit(solution)/shard_map/ppermute | solution.py:235
  42.8 5.1 %collective-permute-start.11 = (bf16[192,128]{1,0:T(8,128)(2,1)S(1)}, bf16[192,128]{1,0:T(8,128)(2,1)S(1)}, u32[]{:S(2)}, u32[]{:S(2)}) collective-permute-start(bf16[192,128]{1,0:T(8,128)(2,1)S(1)} %get-tuple-element.53), channel_id=1, source_target_pairs={{0,6},{1,7},{2,0},{3,1},{4,2},{5,3},{6,4},{7,5},{8,14},{9,15},{10,... | collective-permute-start | bytes 147464 | tf_op jit(solution)/shard_map/ppermute | solution.py:225
  45.7 5.9 %collective-permute-start.10 = (bf16[192,128]{1,0:T(8,128)(2,1)S(1)}, bf16[192,128]{1,0:T(8,128)(2,1)S(1)}, u32[]{:S(2)}, u32[]{:S(2)}) collective-permute-start(bf16[192,128]{1,0:T(8,128)(2,1)S(1)} %get-tuple-element.53), channel_id=1, source_target_pairs={{0,2},{1,3},{2,4},{3,5},{4,6},{5,7},{6,0},{7,1},{8,10},{9,11},{10,... | collective-permute-start | bytes 147464 | tf_op jit(solution)/shard_map/ppermute | solution.py:225
  45.7 5.9 %collective-permute-start.9 = (bf16[192,128]{1,0:T(8,128)(2,1)S(1)}, bf16[192,128]{1,0:T(8,128)(2,1)S(1)}, u32[]{:S(2)}, u32[]{:S(2)}) collective-permute-start(bf16[192,128]{1,0:T(8,128)(2,1)S(1)} %get-tuple-element.53), channel_id=1, source_target_pairs={{0,4},{1,5},{2,6},{3,7},{4,0},{5,1},{6,2},{7,3},{8,12},{9,13},{10,... | collective-permute-start | bytes 147464 | tf_op jit(solution)/shard_map/ppermute | solution.py:225
  54.4 17.4 %all-to-all-start.1 = ((bf16[16,96,256]{2,1,0:T(8,128)(2,1)}), bf16[16,96,256]{2,1,0:T(8,128)(2,1)S(1)}, u32[]{:S(2)}, u32[]{:S(2)}) async-start(bf16[16,96,256]{2,1,0:T(8,128)(2,1)} %copy-done.2), calls=%async_computation.1 | async-start | bytes 1572864 | tf_op jit(solution)/shard_map/all_to_all | solution.py:376
  58.5 13.3 %collective-permute-start.2 = (s32[1,128]{1,0:T(1,128)S(1)}, s32[1,128]{1,0:T(1,128)S(1)}, u32[]{:S(2)}, u32[]{:S(2)}) collective-permute-start(s32[1,128]{1,0:T(1,128)S(1)} %get-tuple-element.27.refs_0_), channel_id=1, source_target_pairs={{0,8},{8,16},{16,24},{24,0},{32,40},{40,48},{48,56},{56,32},{64,72... | collective-permute-start | bytes 1544 | tf_op jit(solution)/shard_map/ppermute | solution.py:229
  60.4 11.4 %collective-permute-start.1 = (s32[1,128]{1,0:T(1,128)S(1)}, s32[1,128]{1,0:T(1,128)S(1)}, u32[]{:S(2)}, u32[]{:S(2)}) collective-permute-start(s32[1,128]{1,0:T(1,128)S(1)} %get-tuple-element.27.refs_0_), channel_id=1, source_target_pairs={{0,16},{8,24},{16,0},{24,8},{32,48},{40,56},{48,32},{56,40},{64,80... | collective-permute-start | bytes 1544 | tf_op jit(solution)/shard_map/ppermute | solution.py:229
  63.1 8.7 %collective-permute-start = (s32[1,128]{1,0:T(1,128)S(1)}, s32[1,128]{1,0:T(1,128)S(1)}, u32[]{:S(2)}, u32[]{:S(2)}) collective-permute-start(s32[1,128]{1,0:T(1,128)S(1)} %get-tuple-element.27.refs_0_), channel_id=1, source_target_pairs={{0,24},{8,0},{16,8},{24,16},{32,56},{40,32},{48,40},{56,48},{64,88... | collective-permute-start | bytes 1544 | tf_op jit(solution)/shard_map/ppermute | solution.py:229
  72.3 10.8 %collective-permute-start.14 = (bf16[512,256]{1,0:T(8,128)(2,1)S(1)}, bf16[512,256]{1,0:T(8,128)(2,1)}, u32[]{:S(2)}, u32[]{:S(2)}) collective-permute-start(bf16[512,256]{1,0:T(8,128)(2,1)S(1)} %compact.1.refs_0_), channel_id=1, source_target_pairs={{0,4},{1,5},{2,6},{3,7},{4,0},{5,1},{6,2},{7,3},{8,12},{9,13},{10,... | collective-permute-start | bytes 786440 | tf_op jit(solution)/shard_map/ppermute | solution.py:225
  74.4 13.8 %collective-permute-start.13 = (bf16[512,256]{1,0:T(8,128)(2,1)S(1)}, bf16[512,256]{1,0:T(8,128)(2,1)}, u32[]{:S(2)}, u32[]{:S(2)}) collective-permute-start(bf16[512,256]{1,0:T(8,128)(2,1)S(1)} %compact.1.refs_0_), channel_id=1, source_target_pairs={{0,6},{1,7},{2,0},{3,1},{4,2},{5,3},{6,4},{7,5},{8,14},{9,15},{10,... | collective-permute-start | bytes 786440 | tf_op jit(solution)/shard_map/ppermute | solution.py:225
  75.6 12.6 %collective-permute-start.12 = (bf16[512,256]{1,0:T(8,128)(2,1)S(1)}, bf16[512,256]{1,0:T(8,128)(2,1)}, u32[]{:S(2)}, u32[]{:S(2)}) collective-permute-start(bf16[512,256]{1,0:T(8,128)(2,1)S(1)} %compact.1.refs_0_), channel_id=1, source_target_pairs={{0,2},{1,3},{2,4},{3,5},{4,6},{5,7},{6,0},{7,1},{8,10},{9,11},{10,... | collective-permute-start | bytes 786440 | tf_op jit(solution)/shard_map/ppermute | solution.py:225
  76.4 14.8 %collective-permute-start.19 = (bf16[256,1024]{1,0:T(8,128)(2,1)}, bf16[256,1024]{1,0:T(8,128)(2,1)S(1)}, u32[]{:S(2)}, u32[]{:S(2)}) collective-permute-start(bf16[256,1024]{1,0:T(8,128)(2,1)} %copy-done.9), channel_id=1, source_target_pairs={{0,32},{8,40},{16,48},{24,56},{32,64},{40,72},{48,80},{56,88},{64,... | collective-permute-start | bytes 1572872 | tf_op jit(solution)/shard_map/ppermute | solution.py:235
  76.4 14.8 %collective-permute-start.20 = (bf16[256,1024]{1,0:T(8,128)(2,1)}, bf16[256,1024]{1,0:T(8,128)(2,1)S(1)}, u32[]{:S(2)}, u32[]{:S(2)}) collective-permute-start(bf16[256,1024]{1,0:T(8,128)(2,1)} %collective-permute-done.7.refs_14_), channel_id=1, source_target_pairs={{0,96},{8,104},{16,112},{24,120},{32,0},{40,8},{48,16},{56,24},{64... | collective-permute-start | bytes 1572872 | tf_op jit(solution)/shard_map/ppermute | solution.py:235
  83.1 5.7 %collective-permute-start.18 = (bf16[512,256]{1,0:T(8,128)(2,1)}, bf16[512,256]{1,0:T(8,128)(2,1)}, u32[]{:S(2)}, u32[]{:S(2)}) collective-permute-start(bf16[512,256]{1,0:T(8,128)(2,1)} %collective-permute-done.14.refs_3_), channel_id=1, source_target_pairs={{0,1},{1,0},{2,3},{3,2},{4,5},{5,4},{6,7},{7,6},{8,9},{9,8},{10,11... | collective-permute-start | bytes 786440 | tf_op jit(solution)/shard_map/ppermute | solution.py:225
  98.9 14.5 %collective-permute-start.21 = (bf16[128,1024]{1,0:T(8,128)(2,1)S(1)}, bf16[128,1024]{1,0:T(8,128)(2,1)S(1)}, u32[]{:S(2)}, u32[]{:S(2)}) collective-permute-start(bf16[128,1024]{1,0:T(8,128)(2,1)S(1)} %get-tuple-element.44), channel_id=1, source_target_pairs={{0,8},{8,16},{16,24},{24,0},{32,40},{40,48},{48,56},{56,32},{64,72... | collective-permute-start | bytes 786440 | tf_op jit(solution)/shard_map/ppermute | solution.py:229
  99.5 13.9 %collective-permute-start.22 = (bf16[128,1024]{1,0:T(8,128)(2,1)S(1)}, bf16[128,1024]{1,0:T(8,128)(2,1)S(1)}, u32[]{:S(2)}, u32[]{:S(2)}) collective-permute-start(bf16[128,1024]{1,0:T(8,128)(2,1)S(1)} %get-tuple-element.45), channel_id=1, source_target_pairs={{0,24},{8,0},{16,8},{24,16},{32,56},{40,32},{48,40},{56,48},{64,88... | collective-permute-start | bytes 786440 | tf_op jit(solution)/shard_map/ppermute | solution.py:229
  102.2 11.2 %collective-permute-start.23 = (bf16[128,1024]{1,0:T(8,128)(2,1)S(1)}, bf16[128,1024]{1,0:T(8,128)(2,1)S(1)}, u32[]{:S(2)}, u32[]{:S(2)}) collective-permute-start(bf16[128,1024]{1,0:T(8,128)(2,1)S(1)} %get-tuple-element.46), channel_id=1, source_target_pairs={{0,16},{8,24},{16,0},{24,8},{32,48},{40,56},{48,32},{56,40},{64,80... | collective-permute-start | bytes 786440 | tf_op jit(solution)/shard_map/ppermute | solution.py:229
  132.3 4.5 %collective-permute-start.27 = (bf16[192,128]{1,0:T(8,128)(2,1)S(1)}, bf16[192,128]{1,0:T(8,128)(2,1)S(1)}, u32[]{:S(2)}, u32[]{:S(2)}) collective-permute-start(bf16[192,128]{1,0:T(8,128)(2,1)S(1)} %get-tuple-element.51), channel_id=1, source_target_pairs={{0,6},{1,7},{2,0},{3,1},{4,2},{5,3},{6,4},{7,5},{8,14},{9,15},{10,... | collective-permute-start | bytes 147464 | tf_op jit(solution)/shard_map/ppermute | solution.py:225
  135.0 5.8 %collective-permute-start.26 = (bf16[192,128]{1,0:T(8,128)(2,1)S(1)}, bf16[192,128]{1,0:T(8,128)(2,1)S(1)}, u32[]{:S(2)}, u32[]{:S(2)}) collective-permute-start(bf16[192,128]{1,0:T(8,128)(2,1)S(1)} %get-tuple-element.51), channel_id=1, source_target_pairs={{0,2},{1,3},{2,4},{3,5},{4,6},{5,7},{6,0},{7,1},{8,10},{9,11},{10,... | collective-permute-start | bytes 147464 | tf_op jit(solution)/shard_map/ppermute | solution.py:225
  135.0 5.8 %collective-permute-start.25 = (bf16[192,128]{1,0:T(8,128)(2,1)S(1)}, bf16[192,128]{1,0:T(8,128)(2,1)S(1)}, u32[]{:S(2)}, u32[]{:S(2)}) collective-permute-start(bf16[192,128]{1,0:T(8,128)(2,1)S(1)} %get-tuple-element.51), channel_id=1, source_target_pairs={{0,4},{1,5},{2,6},{3,7},{4,0},{5,1},{6,2},{7,3},{8,12},{9,13},{10,... | collective-permute-start | bytes 147464 | tf_op jit(solution)/shard_map/ppermute | solution.py:225
  (18 other events, 209.3 us)

commit v4 on v3

--- a/solution.py
+++ b/solution.py
@@ -238,7 +238,7 @@
 def gather_sums(partial, short):
     partial = partial + along_col(short, lambda i: i ^ 1).astype(F32)
     short = partial.astype(BF)
-    return partial, [along_col(short, lambda i, by=by: (i + by) % COLS) for by in (4, 2, 6)]
+    return partial, [along_col(short, lambda i, by=by: (i + by) % COLS) for by in (2, 6, 4)]
 
 
 def compact_body(*refs):
@@ -275,18 +275,18 @@
     kept, swapped = refs[2 * RING : 3 * RING], refs[3 * RING : 4 * RING]
     far_ref, up_ref, down_ref, own_ref, weight_ref, sems = refs[4 * RING :]
     x, near, z = place_ref[0], place_ref[1], place_ref[2]
-    copies = {}
+
+    def load(step, which, block):
+        source = (kept, swapped)[which][step]
+        return pltpu.make_async_copy(
+            source.at[pl.ds(0, QUARTER), :],
+            weight_ref.at[block, pl.ds(which * QUARTER, QUARTER), :],
+            sems.at[block, which],
+        )
+
     for step, offset in enumerate(AROUND):
-        block = (z + offset) & 3
-        for which, source in enumerate((kept[step], swapped[step])):
-            copies[step, which] = pltpu.make_async_copy(
-                source.at[pl.ds(0, QUARTER), :],
-                weight_ref.at[block, pl.ds(which * QUARTER, QUARTER), :],
-                sems.at[step, which],
-            )
-            copies[step, which].start()
-    for copy in copies.values():
-        copy.wait()
+        for which in range(2):
+            load(step, which, (z + offset) & 3).start()
     near = pl.multiple_of(near * QUARTER, QUARTER)
     away = pl.multiple_of(QUARTER - near, QUARTER)
     for tile in range(0, WIDTH, TILE):
@@ -294,6 +294,9 @@
         product = jnp.zeros((RING * BLOCK, TILE), F32)
         for step, offset in enumerate(AROUND):
             block = (x + offset) & 3
+            if tile == 0:
+                for which in range(2):
+                    load(step, which, block).wait()
             product += jnp.dot(
                 same[step][...],
                 weight_ref[block, pl.ds(near, QUARTER), columns],
@@ -318,7 +321,7 @@
         grid=(1,),
         in_specs=[pl.BlockSpec(memory_space=pltpu.SMEM)]
         + [whole((RING * BLOCK, QUARTER))] * 8
-        + [pl.BlockSpec(memory_space=pltpu.HBM)] * 8,
+        + ([pl.BlockSpec(memory_space=pltpu.HBM)] * 3 + [pl.BlockSpec(memory_space=pl.ANY)]) * 2,
         out_specs=[out] * 4,
         out_shape=[sent, sent, sent, jax.ShapeDtypeStruct((BLOCK, WIDTH), F32)],
         scratch_shapes=[
@@ -330,7 +333,7 @@
             flops=2 * RING * BLOCK * 8 * QUARTER * WIDTH, bytes_accessed=7 << 20, transcendentals=0
         ),
         name="project",
-    )(place, *in_hbm(*same, *other, *kept, *swapped))
+    )(place, *in_hbm(*same, *other, *kept[:3]), kept[3], *in_hbm(*swapped[:3]), swapped[3])
 
 
 def local(

time: 159 us -> 158 us (level)
  waiting for transfers between devices: 45.4 us -> 47.5 us
    ppermute x15, waiting for transfers between devices: 20.6 us -> 22.8 us  [along_col(): return lax.ppermute(values, 'col', [(i, move(i)) for i in range(8)])]
  transfers between devices with their start and end apart: 29 -> 29, of which waited for: 14 -> 18; matrix products, arithmetic and copies ran while one was open for 0% -> 0% of each run, Pallas kernels for 7% -> 7%
where the time goes in v4:
time: 158 us
  blocking collectives  48.9 us (31%)
  waiting for transfers between devices  47.5 us (30%)
  starting transfers between devices  39.1 us (25%)
  Pallas kernels  18 us (11%)
  local copies, waits for them, and re-layouts  2.24 us (1%)
    all_to_all x2, blocking collectives, dispatch(): lax.all_to_all(packed, 'row', 0, 0, tiled=True).reshape(PACKED, WIDTH)  33 us
    ppermute x15, waiting for transfers between devices, along_col(): return lax.ppermute(values, 'col', [(i, move(i)) for i in range(8)])  22.8 us
    all_to_all x1, blocking collectives, local(): lax.all_to_all(erased.reshape(ROWS, PART, WIDTH), 'row', 0, 0, tiled=True)  15.9 us
    ppermute x15, starting transfers between devices, along_col(): return lax.ppermute(values, 'col', [(i, move(i)) for i in range(8)])  12.9 us
    ppermute x6, waiting for transfers between devices, along_y(): lax.ppermute(values, 'row', [(i, i // RING * RING + (i + step) % RING) fo...  11.8 us
    ppermute x6, starting transfers between devices, along_y(): lax.ppermute(values, 'row', [(i, i // RING * RING + (i + step) % RING) fo...  9.37 us
    ppermute x6, starting transfers between devices, along_z(): lax.ppermute(values, 'row', [(i, (i + RING * step) % ROWS) for i in range...  9.37 us
    pallas_call x1, Pallas kernels, attend_and_pack(): pl.pallas_call(attend_body, grid=(BLOCK // CHUNK,), in_specs=[by_row(WIDT...  8.51 us
  transfers between devices with their start and end apart: 29, of which 18 were waited for; matrix products, arithmetic and copies ran while one was open for 0% of the time, Pallas kernels for 7%

profile of v4, /device:TPU:0, one launch (start us, length us, event | category | flops | bytes accessed | tf_op | source)
XLA Modules:
  0.0 157.8 jit_solution(15591140849998393285)
XLA Ops:
  1.3 3.4 %collective-permute-start.3 = (bf16[256,1024]{1,0:T(8,128)(2,1)S(1)}, bf16[256,1024]{1,0:T(8,128)(2,1)}, u32[]{:S(2)}, u32[]{:S(2)}) collective-permute-start(bf16[256,1024]{1,0:T(8,128)(2,1)S(1)} %get-tuple-element.56), channel_id=1, source_target_pairs={{0,16},{8,24},{16,0},{24,8},{32,48},{40,56},{48,32},{56,40},{64,80... | collective-permute-start | bytes 1572872 | tf_op jit(solution)/shard_map/ppermute | solution.py:357
  4.7 4.0 %collective-permute-start.5 = (bf16[256,1024]{1,0:T(8,128)(2,1)S(1)}, bf16[256,1024]{1,0:T(8,128)(2,1)S(1)}, u32[]{:S(2)}, u32[]{:S(2)}) collective-permute-start(bf16[256,1024]{1,0:T(8,128)(2,1)S(1)} %get-tuple-element.55), channel_id=1, source_target_pairs={{0,96},{8,104},{16,112},{24,120},{32,0},{40,8},{48,16},{56,24},{64... | collective-permute-start | bytes 1572872 | tf_op jit(solution)/shard_map/ppermute | solution.py:235
  8.9 8.5 %attend.1 = (bf16[384,1024]{1,0:T(8,128)(2,1)S(1)}, s32[1,128]{1,0:T(1,128)S(1)}) custom-call(bf16[128,1024]{1,0:T(8,128)(2,1)} %q_ref.1, bf16[128,128]{1,0:T(8,128)(2,1)} %key_ref.1, bf16[128,128]{1,0:T(8,128)(2,1)} %value_ref.1, s32[1,128]{1,0:T(1,128)S(1)} %fusion.3.target_ref, bf16[128,256,128]{2,1,0:T(8,128)(2,1)} %keys_ref.1, ...), custom_call_target="tpu_custom_call" | custom-call | flops 134217728 | bytes 17825792 | tf_op jit(solution)/shard_map/attend/pallas_call | solution.py:91
  17.5 2.1 %collective-permute-done.5.refs_10_ = bf16[256,1024]{1,0:T(8,128)(2,1)S(1)} collective-permute-done((bf16[256,1024]{1,0:T(8,128)(2,1)S(1)}, bf16[256,1024]{1,0:T(8,128)(2,1)S(1)}, u32[]{:S(2)}, u32[]{:S(2)}) %collective-permute-start.5) | collective-permute-done | bytes 524320 | tf_op jit(solution)/shard_map/ppermute | solution.py:235
  19.6 3.4 %collective-permute-done.4.refs_9_ = bf16[256,1024]{1,0:T(8,128)(2,1)S(1)} collective-permute-done((bf16[256,1024]{1,0:T(8,128)(2,1)S(1)}, bf16[256,1024]{1,0:T(8,128)(2,1)S(1)}, u32[]{:S(2)}, u32[]{:S(2)}) %collective-permute-start.4) | collective-permute-done | bytes 524320 | tf_op jit(solution)/shard_map/ppermute | solution.py:235
  23.0 15.8 %all_to_all.20 = bf16[16,24,1024]{2,1,0:T(8,128)(2,1)S(1)} all-to-all(bf16[16,24,1024]{2,1,0:T(8,128)(2,1)S(1)} %bitcast.40), channel_id=1, replica_groups=mesh['row'=16,'col'=8] {'row'}, dimensions={0} | all-to-all | bytes 1572864 | tf_op jit(solution)/shard_map/all_to_all | solution.py:363
  42.8 3.1 %collective-permute-start.11 = (bf16[192,128]{1,0:T(8,128)(2,1)S(1)}, bf16[192,128]{1,0:T(8,128)(2,1)S(1)}, u32[]{:S(2)}, u32[]{:S(2)}) collective-permute-start(bf16[192,128]{1,0:T(8,128)(2,1)S(1)} %get-tuple-element.53), channel_id=1, source_target_pairs={{0,4},{1,5},{2,6},{3,7},{4,0},{5,1},{6,2},{7,3},{8,12},{9,13},{10,... | collective-permute-start | bytes 147464 | tf_op jit(solution)/shard_map/ppermute | solution.py:225
  50.0 2.3 %collective-permute-done.9.sum1_ref = bf16[192,128]{1,0:T(8,128)(2,1)S(1)} collective-permute-done((bf16[192,128]{1,0:T(8,128)(2,1)S(1)}, bf16[192,128]{1,0:T(8,128)(2,1)S(1)}, u32[]{:S(2)}, u32[]{:S(2)}) %collective-permute-start.9) | collective-permute-done | bytes 49184 | tf_op jit(solution)/shard_map/ppermute | solution.py:225
  52.4 1.9 %erase.2 = bf16[16,96,256]{2,1,0:T(8,128)(2,1)S(1)} custom-call(s32[1]{0:T(128)} %bitcast.9.core_ref, bf16[384,1024]{1,0:T(8,128)(2,1)S(1)} %bitcast.36, f32[192,128]{1,0:T(8,128)S(1)} %get-tuple-element.54.sum_ref, bf16[192,128]{1,0:T(8,128)(2,1)S(1)} %collective-permute-done.9.sum1_ref, bf16[192,128]{1,0:T(8,128)(2,1)S(1)} %collective-permute-done.10.sum2_ref, ...), custom_call_target="tpu_custom_call" | custom-call | flops 402653184 | bytes 3145728 | tf_op jit(solution)/shard_map/erase/pallas_call | solution.py:205
  55.2 4.1 %all-to-all-start.1 = ((bf16[16,96,256]{2,1,0:T(8,128)(2,1)}), bf16[16,96,256]{2,1,0:T(8,128)(2,1)S(1)}, u32[]{:S(2)}, u32[]{:S(2)}) async-start(bf16[16,96,256]{2,1,0:T(8,128)(2,1)} %copy-done.2), calls=%async_computation.1 | async-start | bytes 1572864 | tf_op jit(solution)/shard_map/all_to_all | solution.py:379
  59.3 1.9 %collective-permute-start.2 = (s32[1,128]{1,0:T(1,128)S(1)}, s32[1,128]{1,0:T(1,128)S(1)}, u32[]{:S(2)}, u32[]{:S(2)}) collective-permute-start(s32[1,128]{1,0:T(1,128)S(1)} %get-tuple-element.27.refs_0_), channel_id=1, source_target_pairs={{0,8},{8,16},{16,24},{24,0},{32,40},{40,48},{48,56},{56,32},{64,72... | collective-permute-start | bytes 1544 | tf_op jit(solution)/shard_map/ppermute | solution.py:229
  61.2 2.7 %collective-permute-start.1 = (s32[1,128]{1,0:T(1,128)S(1)}, s32[1,128]{1,0:T(1,128)S(1)}, u32[]{:S(2)}, u32[]{:S(2)}) collective-permute-start(s32[1,128]{1,0:T(1,128)S(1)} %get-tuple-element.27.refs_0_), channel_id=1, source_target_pairs={{0,16},{8,24},{16,0},{24,8},{32,48},{40,56},{48,32},{56,40},{64,80... | collective-permute-start | bytes 1544 | tf_op jit(solution)/shard_map/ppermute | solution.py:229
  65.3 7.1 %all-to-all-done.1.refs_4_ = bf16[16,96,256]{2,1,0:T(8,128)(2,1)S(1)} async-done(((bf16[16,96,256]{2,1,0:T(8,128)(2,1)}), bf16[16,96,256]{2,1,0:T(8,128)(2,1)S(1)}, u32[]{:S(2)}, u32[]{:S(2)}) %all-to-all-start.1) | async-done | bytes 786464 | tf_op jit(solution)/shard_map/all_to_all | solution.py:379
  76.1 3.2 %collective-permute-start.20 = (bf16[256,1024]{1,0:T(8,128)(2,1)}, bf16[256,1024]{1,0:T(8,128)(2,1)}, u32[]{:S(2)}, u32[]{:S(2)}) collective-permute-start(bf16[256,1024]{1,0:T(8,128)(2,1)} %collective-permute-done.7.refs_14_), channel_id=1, source_target_pairs={{0,96},{8,104},{16,112},{24,120},{32,0},{40,8},{48,16},{56,24},{64... | collective-permute-start | bytes 1572872 | tf_op jit(solution)/shard_map/ppermute | solution.py:235
  79.3 4.4 %collective-permute-done.14.refs_3_ = bf16[512,256]{1,0:T(8,128)(2,1)S(1)} collective-permute-done((bf16[512,256]{1,0:T(8,128)(2,1)S(1)}, bf16[512,256]{1,0:T(8,128)(2,1)S(1)}, u32[]{:S(2)}, u32[]{:S(2)}) %collective-permute-start.14) | collective-permute-done | bytes 262176 | tf_op jit(solution)/shard_map/ppermute | solution.py:225
  83.7 3.6 %collective-permute-done.13.refs_2_ = bf16[512,256]{1,0:T(8,128)(2,1)} collective-permute-done((bf16[512,256]{1,0:T(8,128)(2,1)S(1)}, bf16[512,256]{1,0:T(8,128)(2,1)}, u32[]{:S(2)}, u32[]{:S(2)}) %collective-permute-start.13) | collective-permute-done | bytes 262176 | tf_op jit(solution)/shard_map/ppermute | solution.py:225
  89.2 1.6 %collective-permute-done.16.refs_5_ = bf16[512,256]{1,0:T(8,128)(2,1)} collective-permute-done((bf16[512,256]{1,0:T(8,128)(2,1)}, bf16[512,256]{1,0:T(8,128)(2,1)}, u32[]{:S(2)}, u32[]{:S(2)}) %collective-permute-start.16) | collective-permute-done | bytes 262176 | tf_op jit(solution)/shard_map/ppermute | solution.py:225
  90.9 5.3 %project.1 = (bf16[128,1024]{1,0:T(8,128)(2,1)S(1)}, bf16[128,1024]{1,0:T(8,128)(2,1)S(1)}, bf16[128,1024]{1,0:T(8,128)(2,1)S(1)}, f32[128,1024]{1,0:T(8,128)S(1)}) custom-call(s32[3]{0:T(128)S(1)} %pad_add_fusion.place_ref, bf16[512,256]{1,0:T(8,128)(2,1)} %copy-done.3, bf16[512,256]{1,0:T(8,128)(2,1)} %collective-permute-done.12.refs_1_, ...), custom_call_target="tpu_custom_call" | custom-call | flops 2147483648 | bytes 7340032 | tf_op jit(solution)/shard_map/project/pallas_call | solution.py:319
  96.9 2.7 %collective-permute-start.22 = (bf16[128,1024]{1,0:T(8,128)(2,1)S(1)}, bf16[128,1024]{1,0:T(8,128)(2,1)S(1)}, u32[]{:S(2)}, u32[]{:S(2)}) collective-permute-start(bf16[128,1024]{1,0:T(8,128)(2,1)S(1)} %get-tuple-element.45), channel_id=1, source_target_pairs={{0,24},{8,0},{16,8},{24,16},{32,56},{40,32},{48,40},{56,48},{64,88... | collective-permute-start | bytes 786440 | tf_op jit(solution)/shard_map/ppermute | solution.py:229
  99.5 11.8 %collective-permute-done.21 = bf16[128,1024]{1,0:T(8,128)(2,1)S(1)} collective-permute-done((bf16[128,1024]{1,0:T(8,128)(2,1)S(1)}, bf16[128,1024]{1,0:T(8,128)(2,1)S(1)}, u32[]{:S(2)}, u32[]{:S(2)}) %collective-permute-start.21) | collective-permute-done | bytes 262176 | tf_op jit(solution)/shard_map/ppermute | solution.py:229
  111.8 17.3 %all_to_all.21 = bf16[16,24,1024]{2,1,0:T(8,128)(2,1)S(1)} all-to-all(bf16[16,24,1024]{2,1,0:T(8,128)(2,1)S(1)} %bitcast.43), channel_id=1, replica_groups=mesh['row'=16,'col'=8] {'row'}, dimensions={0} | all-to-all | bytes 1572864 | tf_op jit(solution)/shard_map/all_to_all | solution.py:363
  131.1 2.5 %collective-permute-start.27 = (bf16[192,128]{1,0:T(8,128)(2,1)S(1)}, bf16[192,128]{1,0:T(8,128)(2,1)S(1)}, u32[]{:S(2)}, u32[]{:S(2)}) collective-permute-start(bf16[192,128]{1,0:T(8,128)(2,1)S(1)} %get-tuple-element.51), channel_id=1, source_target_pairs={{0,4},{1,5},{2,6},{3,7},{4,0},{5,1},{6,2},{7,3},{8,12},{9,13},{10,... | collective-permute-start | bytes 147464 | tf_op jit(solution)/shard_map/ppermute | solution.py:225
  137.7 2.6 %collective-permute-done.25.sum1_ref = bf16[192,128]{1,0:T(8,128)(2,1)S(1)} collective-permute-done((bf16[192,128]{1,0:T(8,128)(2,1)S(1)}, bf16[192,128]{1,0:T(8,128)(2,1)S(1)}, u32[]{:S(2)}, u32[]{:S(2)}) %collective-permute-start.25) | collective-permute-done | bytes 49184 | tf_op jit(solution)/shard_map/ppermute | solution.py:225
  140.8 15.9 %all_to_all.22 = bf16[16,24,1024]{2,1,0:T(8,128)(2,1)S(1)} all-to-all(bf16[16,24,1024]{2,1,0:T(8,128)(2,1)S(1)} %bitcast.39), channel_id=1, replica_groups=mesh['row'=16,'col'=8] {'row'}, dimensions={0} | all-to-all | bytes 1572864 | tf_op jit(solution)/shard_map/all_to_all | solution.py:399
  (76 shorter events, 26.4 us)
Async XLA Ops:
  1.3 16.1 %collective-permute-start.3 = (bf16[256,1024]{1,0:T(8,128)(2,1)S(1)}, bf16[256,1024]{1,0:T(8,128)(2,1)}, u32[]{:S(2)}, u32[]{:S(2)}) collective-permute-start(bf16[256,1024]{1,0:T(8,128)(2,1)S(1)} %get-tuple-element.56), channel_id=1, source_target_pairs={{0,16},{8,24},{16,0},{24,8},{32,48},{40,56},{48,32},{56,40},{64,80... | collective-permute-start | bytes 1572872 | tf_op jit(solution)/shard_map/ppermute | solution.py:357
  4.7 14.9 %collective-permute-start.5 = (bf16[256,1024]{1,0:T(8,128)(2,1)S(1)}, bf16[256,1024]{1,0:T(8,128)(2,1)S(1)}, u32[]{:S(2)}, u32[]{:S(2)}) collective-permute-start(bf16[256,1024]{1,0:T(8,128)(2,1)S(1)} %get-tuple-element.55), channel_id=1, source_target_pairs={{0,96},{8,104},{16,112},{24,120},{32,0},{40,8},{48,16},{56,24},{64... | collective-permute-start | bytes 1572872 | tf_op jit(solution)/shard_map/ppermute | solution.py:235
  8.7 14.3 %collective-permute-start.4 = (bf16[256,1024]{1,0:T(8,128)(2,1)S(1)}, bf16[256,1024]{1,0:T(8,128)(2,1)S(1)}, u32[]{:S(2)}, u32[]{:S(2)}) collective-permute-start(bf16[256,1024]{1,0:T(8,128)(2,1)S(1)} %get-tuple-element.55), channel_id=1, source_target_pairs={{0,32},{8,40},{16,48},{24,56},{32,64},{40,72},{48,80},{56,88},{64,... | collective-permute-start | bytes 1572872 | tf_op jit(solution)/shard_map/ppermute | solution.py:235
  39.5 15.7 %collective-permute-start.7 = (bf16[256,1024]{1,0:T(8,128)(2,1)}, bf16[256,1024]{1,0:T(8,128)(2,1)}, u32[]{:S(2)}, u32[]{:S(2)}) collective-permute-start(bf16[256,1024]{1,0:T(8,128)(2,1)} %collective-permute-done.3.refs_12_), channel_id=1, source_target_pairs={{0,96},{8,104},{16,112},{24,120},{32,0},{40,8},{48,16},{56,24},{64... | collective-permute-start | bytes 1572872 | tf_op jit(solution)/shard_map/ppermute | solution.py:235
  40.4 14.8 %collective-permute-start.6 = (bf16[256,1024]{1,0:T(8,128)(2,1)}, bf16[256,1024]{1,0:T(8,128)(2,1)}, u32[]{:S(2)}, u32[]{:S(2)}) collective-permute-start(bf16[256,1024]{1,0:T(8,128)(2,1)} %collective-permute-done.3.refs_12_), channel_id=1, source_target_pairs={{0,32},{8,40},{16,48},{24,56},{32,64},{40,72},{48,80},{56,88},{64,... | collective-permute-start | bytes 1572872 | tf_op jit(solution)/shard_map/ppermute | solution.py:235
  42.8 5.7 %collective-permute-start.11 = (bf16[192,128]{1,0:T(8,128)(2,1)S(1)}, bf16[192,128]{1,0:T(8,128)(2,1)S(1)}, u32[]{:S(2)}, u32[]{:S(2)}) collective-permute-start(bf16[192,128]{1,0:T(8,128)(2,1)S(1)} %get-tuple-element.53), channel_id=1, source_target_pairs={{0,4},{1,5},{2,6},{3,7},{4,0},{5,1},{6,2},{7,3},{8,12},{9,13},{10,... | collective-permute-start | bytes 147464 | tf_op jit(solution)/shard_map/ppermute | solution.py:225
  45.9 4.1 %collective-permute-start.10 = (bf16[192,128]{1,0:T(8,128)(2,1)S(1)}, bf16[192,128]{1,0:T(8,128)(2,1)S(1)}, u32[]{:S(2)}, u32[]{:S(2)}) collective-permute-start(bf16[192,128]{1,0:T(8,128)(2,1)S(1)} %get-tuple-element.53), channel_id=1, source_target_pairs={{0,6},{1,7},{2,0},{3,1},{4,2},{5,3},{6,4},{7,5},{8,14},{9,15},{10,... | collective-permute-start | bytes 147464 | tf_op jit(solution)/shard_map/ppermute | solution.py:225
  47.1 5.3 %collective-permute-start.9 = (bf16[192,128]{1,0:T(8,128)(2,1)S(1)}, bf16[192,128]{1,0:T(8,128)(2,1)S(1)}, u32[]{:S(2)}, u32[]{:S(2)}) collective-permute-start(bf16[192,128]{1,0:T(8,128)(2,1)S(1)} %get-tuple-element.53), channel_id=1, source_target_pairs={{0,2},{1,3},{2,4},{3,5},{4,6},{5,7},{6,0},{7,1},{8,10},{9,11},{10,... | collective-permute-start | bytes 147464 | tf_op jit(solution)/shard_map/ppermute | solution.py:225
  55.2 17.3 %all-to-all-start.1 = ((bf16[16,96,256]{2,1,0:T(8,128)(2,1)}), bf16[16,96,256]{2,1,0:T(8,128)(2,1)S(1)}, u32[]{:S(2)}, u32[]{:S(2)}) async-start(bf16[16,96,256]{2,1,0:T(8,128)(2,1)} %copy-done.2), calls=%async_computation.1 | async-start | bytes 1572864 | tf_op jit(solution)/shard_map/all_to_all | solution.py:379
  59.3 13.2 %collective-permute-start.2 = (s32[1,128]{1,0:T(1,128)S(1)}, s32[1,128]{1,0:T(1,128)S(1)}, u32[]{:S(2)}, u32[]{:S(2)}) collective-permute-start(s32[1,128]{1,0:T(1,128)S(1)} %get-tuple-element.27.refs_0_), channel_id=1, source_target_pairs={{0,8},{8,16},{16,24},{24,0},{32,40},{40,48},{48,56},{56,32},{64,72... | collective-permute-start | bytes 1544 | tf_op jit(solution)/shard_map/ppermute | solution.py:229
  61.2 11.3 %collective-permute-start.1 = (s32[1,128]{1,0:T(1,128)S(1)}, s32[1,128]{1,0:T(1,128)S(1)}, u32[]{:S(2)}, u32[]{:S(2)}) collective-permute-start(s32[1,128]{1,0:T(1,128)S(1)} %get-tuple-element.27.refs_0_), channel_id=1, source_target_pairs={{0,16},{8,24},{16,0},{24,8},{32,48},{40,56},{48,32},{56,40},{64,80... | collective-permute-start | bytes 1544 | tf_op jit(solution)/shard_map/ppermute | solution.py:229
  63.9 8.6 %collective-permute-start = (s32[1,128]{1,0:T(1,128)S(1)}, s32[1,128]{1,0:T(1,128)S(1)}, u32[]{:S(2)}, u32[]{:S(2)}) collective-permute-start(s32[1,128]{1,0:T(1,128)S(1)} %get-tuple-element.27.refs_0_), channel_id=1, source_target_pairs={{0,24},{8,0},{16,8},{24,16},{32,56},{40,32},{48,40},{56,48},{64,88... | collective-permute-start | bytes 1544 | tf_op jit(solution)/shard_map/ppermute | solution.py:229
  72.9 10.7 %collective-permute-start.14 = (bf16[512,256]{1,0:T(8,128)(2,1)S(1)}, bf16[512,256]{1,0:T(8,128)(2,1)S(1)}, u32[]{:S(2)}, u32[]{:S(2)}) collective-permute-start(bf16[512,256]{1,0:T(8,128)(2,1)S(1)} %compact.1.refs_0_), channel_id=1, source_target_pairs={{0,4},{1,5},{2,6},{3,7},{4,0},{5,1},{6,2},{7,3},{8,12},{9,13},{10,... | collective-permute-start | bytes 786440 | tf_op jit(solution)/shard_map/ppermute | solution.py:225
  74.0 13.3 %collective-permute-start.13 = (bf16[512,256]{1,0:T(8,128)(2,1)S(1)}, bf16[512,256]{1,0:T(8,128)(2,1)}, u32[]{:S(2)}, u32[]{:S(2)}) collective-permute-start(bf16[512,256]{1,0:T(8,128)(2,1)S(1)} %compact.1.refs_0_), channel_id=1, source_target_pairs={{0,6},{1,7},{2,0},{3,1},{4,2},{5,3},{6,4},{7,5},{8,14},{9,15},{10,... | collective-permute-start | bytes 786440 | tf_op jit(solution)/shard_map/ppermute | solution.py:225
  75.6 13.3 %collective-permute-start.12 = (bf16[512,256]{1,0:T(8,128)(2,1)S(1)}, bf16[512,256]{1,0:T(8,128)(2,1)}, u32[]{:S(2)}, u32[]{:S(2)}) collective-permute-start(bf16[512,256]{1,0:T(8,128)(2,1)S(1)} %compact.1.refs_0_), channel_id=1, source_target_pairs={{0,2},{1,3},{2,4},{3,5},{4,6},{5,7},{6,0},{7,1},{8,10},{9,11},{10,... | collective-permute-start | bytes 786440 | tf_op jit(solution)/shard_map/ppermute | solution.py:225
  76.0 14.8 %collective-permute-start.19 = (bf16[256,1024]{1,0:T(8,128)(2,1)}, bf16[256,1024]{1,0:T(8,128)(2,1)S(1)}, u32[]{:S(2)}, u32[]{:S(2)}) collective-permute-start(bf16[256,1024]{1,0:T(8,128)(2,1)} %copy-done.9), channel_id=1, source_target_pairs={{0,32},{8,40},{16,48},{24,56},{32,64},{40,72},{48,80},{56,88},{64,... | collective-permute-start | bytes 1572872 | tf_op jit(solution)/shard_map/ppermute | solution.py:235
  76.1 14.8 %collective-permute-start.20 = (bf16[256,1024]{1,0:T(8,128)(2,1)}, bf16[256,1024]{1,0:T(8,128)(2,1)}, u32[]{:S(2)}, u32[]{:S(2)}) collective-permute-start(bf16[256,1024]{1,0:T(8,128)(2,1)} %collective-permute-done.7.refs_14_), channel_id=1, source_target_pairs={{0,96},{8,104},{16,112},{24,120},{32,0},{40,8},{48,16},{56,24},{64... | collective-permute-start | bytes 1572872 | tf_op jit(solution)/shard_map/ppermute | solution.py:235
  83.7 5.3 %collective-permute-start.18 = (bf16[512,256]{1,0:T(8,128)(2,1)S(1)}, bf16[512,256]{1,0:T(8,128)(2,1)}, u32[]{:S(2)}, u32[]{:S(2)}) collective-permute-start(bf16[512,256]{1,0:T(8,128)(2,1)S(1)} %collective-permute-done.14.refs_3_), channel_id=1, source_target_pairs={{0,1},{1,0},{2,3},{3,2},{4,5},{5,4},{6,7},{7,6},{8,9},{9,8},{10,11... | collective-permute-start | bytes 786440 | tf_op jit(solution)/shard_map/ppermute | solution.py:225
  96.2 15.1 %collective-permute-start.21 = (bf16[128,1024]{1,0:T(8,128)(2,1)S(1)}, bf16[128,1024]{1,0:T(8,128)(2,1)S(1)}, u32[]{:S(2)}, u32[]{:S(2)}) collective-permute-start(bf16[128,1024]{1,0:T(8,128)(2,1)S(1)} %get-tuple-element.44), channel_id=1, source_target_pairs={{0,8},{8,16},{16,24},{24,0},{32,40},{40,48},{48,56},{56,32},{64,72... | collective-permute-start | bytes 786440 | tf_op jit(solution)/shard_map/ppermute | solution.py:229
  96.9 14.5 %collective-permute-start.22 = (bf16[128,1024]{1,0:T(8,128)(2,1)S(1)}, bf16[128,1024]{1,0:T(8,128)(2,1)S(1)}, u32[]{:S(2)}, u32[]{:S(2)}) collective-permute-start(bf16[128,1024]{1,0:T(8,128)(2,1)S(1)} %get-tuple-element.45), channel_id=1, source_target_pairs={{0,24},{8,0},{16,8},{24,16},{32,56},{40,32},{48,40},{56,48},{64,88... | collective-permute-start | bytes 786440 | tf_op jit(solution)/shard_map/ppermute | solution.py:229
  99.5 11.8 %collective-permute-start.23 = (bf16[128,1024]{1,0:T(8,128)(2,1)S(1)}, bf16[128,1024]{1,0:T(8,128)(2,1)S(1)}, u32[]{:S(2)}, u32[]{:S(2)}) collective-permute-start(bf16[128,1024]{1,0:T(8,128)(2,1)S(1)} %get-tuple-element.46), channel_id=1, source_target_pairs={{0,16},{8,24},{16,0},{24,8},{32,48},{40,56},{48,32},{56,40},{64,80... | collective-permute-start | bytes 786440 | tf_op jit(solution)/shard_map/ppermute | solution.py:229
  131.1 5.7 %collective-permute-start.27 = (bf16[192,128]{1,0:T(8,128)(2,1)S(1)}, bf16[192,128]{1,0:T(8,128)(2,1)S(1)}, u32[]{:S(2)}, u32[]{:S(2)}) collective-permute-start(bf16[192,128]{1,0:T(8,128)(2,1)S(1)} %get-tuple-element.51), channel_id=1, source_target_pairs={{0,4},{1,5},{2,6},{3,7},{4,0},{5,1},{6,2},{7,3},{8,12},{9,13},{10,... | collective-permute-start | bytes 147464 | tf_op jit(solution)/shard_map/ppermute | solution.py:225
  133.6 4.1 %collective-permute-start.26 = (bf16[192,128]{1,0:T(8,128)(2,1)S(1)}, bf16[192,128]{1,0:T(8,128)(2,1)S(1)}, u32[]{:S(2)}, u32[]{:S(2)}) collective-permute-start(bf16[192,128]{1,0:T(8,128)(2,1)S(1)} %get-tuple-element.51), channel_id=1, source_target_pairs={{0,6},{1,7},{2,0},{3,1},{4,2},{5,3},{6,4},{7,5},{8,14},{9,15},{10,... | collective-permute-start | bytes 147464 | tf_op jit(solution)/shard_map/ppermute | solution.py:225
  134.9 5.3 %collective-permute-start.25 = (bf16[192,128]{1,0:T(8,128)(2,1)S(1)}, bf16[192,128]{1,0:T(8,128)(2,1)S(1)}, u32[]{:S(2)}, u32[]{:S(2)}) collective-permute-start(bf16[192,128]{1,0:T(8,128)(2,1)S(1)} %get-tuple-element.51), channel_id=1, source_target_pairs={{0,2},{1,3},{2,4},{3,5},{4,6},{5,7},{6,0},{7,1},{8,10},{9,11},{10,... | collective-permute-start | bytes 147464 | tf_op jit(solution)/shard_map/ppermute | solution.py:225
  (17 other events, 214.9 us)

commit v5 on v4

--- a/solution.py
+++ b/solution.py
@@ -273,7 +273,7 @@
 def project_body(place_ref, *refs):
     same, other = refs[0:RING], refs[RING : 2 * RING]
     kept, swapped = refs[2 * RING : 3 * RING], refs[3 * RING : 4 * RING]
-    far_ref, up_ref, down_ref, own_ref, weight_ref, sems = refs[4 * RING :]
+    far_ref, up_ref, down_ref, own_ref, weight_ref, act_ref, sems, act_sems = refs[4 * RING :]
     x, near, z = place_ref[0], place_ref[1], place_ref[2]
 
     def load(step, which, block):
@@ -284,9 +284,14 @@
             sems.at[block, which],
         )
 
+    def fetch(step, which):
+        source = (same, other)[which][step]
+        return pltpu.make_async_copy(source, act_ref.at[step, which], act_sems.at[step, which])
+
     for step, offset in enumerate(AROUND):
         for which in range(2):
             load(step, which, (z + offset) & 3).start()
+            fetch(step, which).start()
     near = pl.multiple_of(near * QUARTER, QUARTER)
     away = pl.multiple_of(QUARTER - near, QUARTER)
     for tile in range(0, WIDTH, TILE):
@@ -297,13 +302,14 @@
             if tile == 0:
                 for which in range(2):
                     load(step, which, block).wait()
+                    fetch(step, which).wait()
             product += jnp.dot(
-                same[step][...],
+                act_ref[step, 0],
                 weight_ref[block, pl.ds(near, QUARTER), columns],
                 preferred_element_type=F32,
             )
             product += jnp.dot(
-                other[step][...],
+                act_ref[step, 1],
                 weight_ref[block, pl.ds(away, QUARTER), columns],
                 preferred_element_type=F32,
             )
@@ -320,12 +326,14 @@
         project_body,
         grid=(1,),
         in_specs=[pl.BlockSpec(memory_space=pltpu.SMEM)]
-        + [whole((RING * BLOCK, QUARTER))] * 8
+        + [pl.BlockSpec(memory_space=pl.ANY)] * 8
         + ([pl.BlockSpec(memory_space=pltpu.HBM)] * 3 + [pl.BlockSpec(memory_space=pl.ANY)]) * 2,
         out_specs=[out] * 4,
         out_shape=[sent, sent, sent, jax.ShapeDtypeStruct((BLOCK, WIDTH), F32)],
         scratch_shapes=[
             pltpu.VMEM((RING, 2 * QUARTER, WIDTH), BF),
+            pltpu.VMEM((RING, 2, RING * BLOCK, QUARTER), BF),
+            pltpu.SemaphoreType.DMA((RING, 2)),
             pltpu.SemaphoreType.DMA((RING, 2)),
         ],
         compiler_params=params(20),
@@ -333,7 +341,7 @@
             flops=2 * RING * BLOCK * 8 * QUARTER * WIDTH, bytes_accessed=7 << 20, transcendentals=0
         ),
         name="project",
-    )(place, *in_hbm(*same, *other, *kept[:3]), kept[3], *in_hbm(*swapped[:3]), swapped[3])
+    )(place, *same, *other, *in_hbm(*kept[:3]), kept[3], *in_hbm(*swapped[:3]), swapped[3])
 
 
 def local(

time: 158 us -> 158 us (level)
  no operation moved by 1% of the time
where the time goes in v5:
time: 158 us; the launch traced here: 157 us
  blocking collectives  48.8 us (31%)
  waiting for transfers between devices  47.5 us (30%)
  starting transfers between devices  39.5 us (25%)
  Pallas kernels  17.4 us (11%)
  local copies, waits for them, and re-layouts  2.22 us (1%)
    all_to_all x2, blocking collectives, dispatch(): lax.all_to_all(packed, 'row', 0, 0, tiled=True).reshape(PACKED, WIDTH)  32.9 us
    ppermute x15, waiting for transfers between devices, along_col(): return lax.ppermute(values, 'col', [(i, move(i)) for i in range(8)])  22.8 us
    all_to_all x1, blocking collectives, local(): lax.all_to_all(erased.reshape(ROWS, PART, WIDTH), 'row', 0, 0, tiled=True)  15.9 us
    ppermute x15, starting transfers between devices, along_col(): return lax.ppermute(values, 'col', [(i, move(i)) for i in range(8)])  13.1 us
    ppermute x6, waiting for transfers between devices, along_y(): lax.ppermute(values, 'row', [(i, i // RING * RING + (i + step) % RING) fo...  11.8 us
    ppermute x6, starting transfers between devices, along_y(): lax.ppermute(values, 'row', [(i, i // RING * RING + (i + step) % RING) fo...  9.55 us
    ppermute x6, starting transfers between devices, along_z(): lax.ppermute(values, 'row', [(i, (i + RING * step) % ROWS) for i in range...  9.37 us
    pallas_call x1, Pallas kernels, attend_and_pack(): pl.pallas_call(attend_body, grid=(BLOCK // CHUNK,), in_specs=[by_row(WIDT...  8.51 us
  transfers between devices with their start and end apart: 29, of which 18 were waited for; matrix products, arithmetic and copies ran while one was open for 0% of the time, Pallas kernels for 7%

profile of v5, /device:TPU:0, one launch (start us, length us, event | category | flops | bytes accessed | tf_op | source)
XLA Modules:
  0.0 157.4 jit_solution(18231154537287705703)
XLA Ops:
  1.3 3.4 %collective-permute-start.3 = (bf16[256,1024]{1,0:T(8,128)(2,1)S(1)}, bf16[256,1024]{1,0:T(8,128)(2,1)}, u32[]{:S(2)}, u32[]{:S(2)}) collective-permute-start(bf16[256,1024]{1,0:T(8,128)(2,1)S(1)} %get-tuple-element.56), channel_id=1, source_target_pairs={{0,16},{8,24},{16,0},{24,8},{32,48},{40,56},{48,32},{56,40},{64,80... | collective-permute-start | bytes 1572872 | tf_op jit(solution)/shard_map/ppermute | solution.py:365
  4.7 4.0 %collective-permute-start.5 = (bf16[256,1024]{1,0:T(8,128)(2,1)S(1)}, bf16[256,1024]{1,0:T(8,128)(2,1)S(1)}, u32[]{:S(2)}, u32[]{:S(2)}) collective-permute-start(bf16[256,1024]{1,0:T(8,128)(2,1)S(1)} %get-tuple-element.55), channel_id=1, source_target_pairs={{0,96},{8,104},{16,112},{24,120},{32,0},{40,8},{48,16},{56,24},{64... | collective-permute-start | bytes 1572872 | tf_op jit(solution)/shard_map/ppermute | solution.py:235
  8.9 8.5 %attend.1 = (bf16[384,1024]{1,0:T(8,128)(2,1)S(1)}, s32[1,128]{1,0:T(1,128)S(1)}) custom-call(bf16[128,1024]{1,0:T(8,128)(2,1)} %q_ref.1, bf16[128,128]{1,0:T(8,128)(2,1)} %key_ref.1, bf16[128,128]{1,0:T(8,128)(2,1)} %value_ref.1, s32[1,128]{1,0:T(1,128)S(1)} %fusion.3.target_ref, bf16[128,256,128]{2,1,0:T(8,128)(2,1)} %keys_ref.1, ...), custom_call_target="tpu_custom_call" | custom-call | flops 134217728 | bytes 17825792 | tf_op jit(solution)/shard_map/attend/pallas_call | solution.py:91
  17.5 2.1 %collective-permute-done.5.refs_10_ = bf16[256,1024]{1,0:T(8,128)(2,1)S(1)} collective-permute-done((bf16[256,1024]{1,0:T(8,128)(2,1)S(1)}, bf16[256,1024]{1,0:T(8,128)(2,1)S(1)}, u32[]{:S(2)}, u32[]{:S(2)}) %collective-permute-start.5) | collective-permute-done | bytes 524320 | tf_op jit(solution)/shard_map/ppermute | solution.py:235
  19.6 3.4 %collective-permute-done.4.refs_9_ = bf16[256,1024]{1,0:T(8,128)(2,1)S(1)} collective-permute-done((bf16[256,1024]{1,0:T(8,128)(2,1)S(1)}, bf16[256,1024]{1,0:T(8,128)(2,1)S(1)}, u32[]{:S(2)}, u32[]{:S(2)}) %collective-permute-start.4) | collective-permute-done | bytes 524320 | tf_op jit(solution)/shard_map/ppermute | solution.py:235
  23.0 15.8 %all_to_all.20 = bf16[16,24,1024]{2,1,0:T(8,128)(2,1)S(1)} all-to-all(bf16[16,24,1024]{2,1,0:T(8,128)(2,1)S(1)} %bitcast.40), channel_id=1, replica_groups=mesh['row'=16,'col'=8] {'row'}, dimensions={0} | all-to-all | bytes 1572864 | tf_op jit(solution)/shard_map/all_to_all | solution.py:371
  42.8 3.1 %collective-permute-start.11 = (bf16[192,128]{1,0:T(8,128)(2,1)S(1)}, bf16[192,128]{1,0:T(8,128)(2,1)S(1)}, u32[]{:S(2)}, u32[]{:S(2)}) collective-permute-start(bf16[192,128]{1,0:T(8,128)(2,1)S(1)} %get-tuple-element.53), channel_id=1, source_target_pairs={{0,4},{1,5},{2,6},{3,7},{4,0},{5,1},{6,2},{7,3},{8,12},{9,13},{10,... | collective-permute-start | bytes 147464 | tf_op jit(solution)/shard_map/ppermute | solution.py:225
  50.0 2.3 %collective-permute-done.9.sum1_ref = bf16[192,128]{1,0:T(8,128)(2,1)S(1)} collective-permute-done((bf16[192,128]{1,0:T(8,128)(2,1)S(1)}, bf16[192,128]{1,0:T(8,128)(2,1)S(1)}, u32[]{:S(2)}, u32[]{:S(2)}) %collective-permute-start.9) | collective-permute-done | bytes 49184 | tf_op jit(solution)/shard_map/ppermute | solution.py:225
  52.4 1.9 %erase.2 = bf16[16,96,256]{2,1,0:T(8,128)(2,1)S(1)} custom-call(s32[1]{0:T(128)} %bitcast.9.core_ref, bf16[384,1024]{1,0:T(8,128)(2,1)S(1)} %bitcast.36, f32[192,128]{1,0:T(8,128)S(1)} %get-tuple-element.54.sum_ref, bf16[192,128]{1,0:T(8,128)(2,1)S(1)} %collective-permute-done.9.sum1_ref, bf16[192,128]{1,0:T(8,128)(2,1)S(1)} %collective-permute-done.10.sum2_ref, ...), custom_call_target="tpu_custom_call" | custom-call | flops 402653184 | bytes 3145728 | tf_op jit(solution)/shard_map/erase/pallas_call | solution.py:205
  55.2 4.1 %all-to-all-start.1 = ((bf16[16,96,256]{2,1,0:T(8,128)(2,1)}), bf16[16,96,256]{2,1,0:T(8,128)(2,1)S(1)}, u32[]{:S(2)}, u32[]{:S(2)}) async-start(bf16[16,96,256]{2,1,0:T(8,128)(2,1)} %copy-done.2), calls=%async_computation.1 | async-start | bytes 1572864 | tf_op jit(solution)/shard_map/all_to_all | solution.py:387
  59.3 1.9 %collective-permute-start.2 = (s32[1,128]{1,0:T(1,128)S(1)}, s32[1,128]{1,0:T(1,128)S(1)}, u32[]{:S(2)}, u32[]{:S(2)}) collective-permute-start(s32[1,128]{1,0:T(1,128)S(1)} %get-tuple-element.27.refs_0_), channel_id=1, source_target_pairs={{0,8},{8,16},{16,24},{24,0},{32,40},{40,48},{48,56},{56,32},{64,72... | collective-permute-start | bytes 1544 | tf_op jit(solution)/shard_map/ppermute | solution.py:229
  61.2 2.7 %collective-permute-start.1 = (s32[1,128]{1,0:T(1,128)S(1)}, s32[1,128]{1,0:T(1,128)S(1)}, u32[]{:S(2)}, u32[]{:S(2)}) collective-permute-start(s32[1,128]{1,0:T(1,128)S(1)} %get-tuple-element.27.refs_0_), channel_id=1, source_target_pairs={{0,16},{8,24},{16,0},{24,8},{32,48},{40,56},{48,32},{56,40},{64,80... | collective-permute-start | bytes 1544 | tf_op jit(solution)/shard_map/ppermute | solution.py:229
  65.3 7.1 %all-to-all-done.1.refs_4_ = bf16[16,96,256]{2,1,0:T(8,128)(2,1)S(1)} async-done(((bf16[16,96,256]{2,1,0:T(8,128)(2,1)}), bf16[16,96,256]{2,1,0:T(8,128)(2,1)S(1)}, u32[]{:S(2)}, u32[]{:S(2)}) %all-to-all-start.1) | async-done | bytes 786464 | tf_op jit(solution)/shard_map/all_to_all | solution.py:387
  76.0 3.2 %collective-permute-start.20 = (bf16[256,1024]{1,0:T(8,128)(2,1)}, bf16[256,1024]{1,0:T(8,128)(2,1)}, u32[]{:S(2)}, u32[]{:S(2)}) collective-permute-start(bf16[256,1024]{1,0:T(8,128)(2,1)} %collective-permute-done.7.refs_14_), channel_id=1, source_target_pairs={{0,96},{8,104},{16,112},{24,120},{32,0},{40,8},{48,16},{56,24},{64... | collective-permute-start | bytes 1572872 | tf_op jit(solution)/shard_map/ppermute | solution.py:235
  79.3 4.4 %collective-permute-done.14.refs_3_ = bf16[512,256]{1,0:T(8,128)(2,1)S(1)} collective-permute-done((bf16[512,256]{1,0:T(8,128)(2,1)S(1)}, bf16[512,256]{1,0:T(8,128)(2,1)S(1)}, u32[]{:S(2)}, u32[]{:S(2)}) %collective-permute-start.14) | collective-permute-done | bytes 262176 | tf_op jit(solution)/shard_map/ppermute | solution.py:225
  83.6 3.6 %collective-permute-done.13.refs_2_ = bf16[512,256]{1,0:T(8,128)(2,1)} collective-permute-done((bf16[512,256]{1,0:T(8,128)(2,1)S(1)}, bf16[512,256]{1,0:T(8,128)(2,1)}, u32[]{:S(2)}, u32[]{:S(2)}) %collective-permute-start.13) | collective-permute-done | bytes 262176 | tf_op jit(solution)/shard_map/ppermute | solution.py:225
  89.1 1.6 %collective-permute-done.16.refs_5_ = bf16[512,256]{1,0:T(8,128)(2,1)} collective-permute-done((bf16[512,256]{1,0:T(8,128)(2,1)}, bf16[512,256]{1,0:T(8,128)(2,1)}, u32[]{:S(2)}, u32[]{:S(2)}) %collective-permute-start.16) | collective-permute-done | bytes 262176 | tf_op jit(solution)/shard_map/ppermute | solution.py:225
  90.9 4.7 %project.1 = (bf16[128,1024]{1,0:T(8,128)(2,1)S(1)}, bf16[128,1024]{1,0:T(8,128)(2,1)S(1)}, bf16[128,1024]{1,0:T(8,128)(2,1)S(1)}, f32[128,1024]{1,0:T(8,128)S(1)}) custom-call(s32[3]{0:T(128)S(1)} %pad_add_fusion.place_ref, bf16[512,256]{1,0:T(8,128)(2,1)S(1)} %compact.1.refs_0_, bf16[512,256]{1,0:T(8,128)(2,1)} %collective-permute-done.12.refs_1_, ...), custom_call_target="tpu_custom_call" | custom-call | flops 2147483648 | bytes 7340032 | tf_op jit(solution)/shard_map/project/pallas_call | solution.py:325
  96.4 2.7 %collective-permute-start.22 = (bf16[128,1024]{1,0:T(8,128)(2,1)S(1)}, bf16[128,1024]{1,0:T(8,128)(2,1)S(1)}, u32[]{:S(2)}, u32[]{:S(2)}) collective-permute-start(bf16[128,1024]{1,0:T(8,128)(2,1)S(1)} %get-tuple-element.45), channel_id=1, source_target_pairs={{0,24},{8,0},{16,8},{24,16},{32,56},{40,32},{48,40},{56,48},{64,88... | collective-permute-start | bytes 786440 | tf_op jit(solution)/shard_map/ppermute | solution.py:229
  99.1 11.8 %collective-permute-done.21 = bf16[128,1024]{1,0:T(8,128)(2,1)S(1)} collective-permute-done((bf16[128,1024]{1,0:T(8,128)(2,1)S(1)}, bf16[128,1024]{1,0:T(8,128)(2,1)S(1)}, u32[]{:S(2)}, u32[]{:S(2)}) %collective-permute-start.21) | collective-permute-done | bytes 262176 | tf_op jit(solution)/shard_map/ppermute | solution.py:229
  111.3 17.2 %all_to_all.21 = bf16[16,24,1024]{2,1,0:T(8,128)(2,1)S(1)} all-to-all(bf16[16,24,1024]{2,1,0:T(8,128)(2,1)S(1)} %bitcast.43), channel_id=1, replica_groups=mesh['row'=16,'col'=8] {'row'}, dimensions={0} | all-to-all | bytes 1572864 | tf_op jit(solution)/shard_map/all_to_all | solution.py:371
  130.5 2.6 %collective-permute-start.27 = (bf16[192,128]{1,0:T(8,128)(2,1)S(1)}, bf16[192,128]{1,0:T(8,128)(2,1)S(1)}, u32[]{:S(2)}, u32[]{:S(2)}) collective-permute-start(bf16[192,128]{1,0:T(8,128)(2,1)S(1)} %get-tuple-element.51), channel_id=1, source_target_pairs={{0,4},{1,5},{2,6},{3,7},{4,0},{5,1},{6,2},{7,3},{8,12},{9,13},{10,... | collective-permute-start | bytes 147464 | tf_op jit(solution)/shard_map/ppermute | solution.py:225
  137.2 2.6 %collective-permute-done.25.sum1_ref = bf16[192,128]{1,0:T(8,128)(2,1)S(1)} collective-permute-done((bf16[192,128]{1,0:T(8,128)(2,1)S(1)}, bf16[192,128]{1,0:T(8,128)(2,1)S(1)}, u32[]{:S(2)}, u32[]{:S(2)}) %collective-permute-start.25) | collective-permute-done | bytes 49184 | tf_op jit(solution)/shard_map/ppermute | solution.py:225
  140.4 15.9 %all_to_all.22 = bf16[16,24,1024]{2,1,0:T(8,128)(2,1)S(1)} all-to-all(bf16[16,24,1024]{2,1,0:T(8,128)(2,1)S(1)} %bitcast.39), channel_id=1, replica_groups=mesh['row'=16,'col'=8] {'row'}, dimensions={0} | all-to-all | bytes 1572864 | tf_op jit(solution)/shard_map/all_to_all | solution.py:407
  (70 shorter events, 26.6 us)
Async XLA Ops:
  1.3 16.1 %collective-permute-start.3 = (bf16[256,1024]{1,0:T(8,128)(2,1)S(1)}, bf16[256,1024]{1,0:T(8,128)(2,1)}, u32[]{:S(2)}, u32[]{:S(2)}) collective-permute-start(bf16[256,1024]{1,0:T(8,128)(2,1)S(1)} %get-tuple-element.56), channel_id=1, source_target_pairs={{0,16},{8,24},{16,0},{24,8},{32,48},{40,56},{48,32},{56,40},{64,80... | collective-permute-start | bytes 1572872 | tf_op jit(solution)/shard_map/ppermute | solution.py:365
  4.7 14.9 %collective-permute-start.5 = (bf16[256,1024]{1,0:T(8,128)(2,1)S(1)}, bf16[256,1024]{1,0:T(8,128)(2,1)S(1)}, u32[]{:S(2)}, u32[]{:S(2)}) collective-permute-start(bf16[256,1024]{1,0:T(8,128)(2,1)S(1)} %get-tuple-element.55), channel_id=1, source_target_pairs={{0,96},{8,104},{16,112},{24,120},{32,0},{40,8},{48,16},{56,24},{64... | collective-permute-start | bytes 1572872 | tf_op jit(solution)/shard_map/ppermute | solution.py:235
  8.7 14.3 %collective-permute-start.4 = (bf16[256,1024]{1,0:T(8,128)(2,1)S(1)}, bf16[256,1024]{1,0:T(8,128)(2,1)S(1)}, u32[]{:S(2)}, u32[]{:S(2)}) collective-permute-start(bf16[256,1024]{1,0:T(8,128)(2,1)S(1)} %get-tuple-element.55), channel_id=1, source_target_pairs={{0,32},{8,40},{16,48},{24,56},{32,64},{40,72},{48,80},{56,88},{64,... | collective-permute-start | bytes 1572872 | tf_op jit(solution)/shard_map/ppermute | solution.py:235
  39.5 15.7 %collective-permute-start.7 = (bf16[256,1024]{1,0:T(8,128)(2,1)}, bf16[256,1024]{1,0:T(8,128)(2,1)}, u32[]{:S(2)}, u32[]{:S(2)}) collective-permute-start(bf16[256,1024]{1,0:T(8,128)(2,1)} %collective-permute-done.3.refs_12_), channel_id=1, source_target_pairs={{0,96},{8,104},{16,112},{24,120},{32,0},{40,8},{48,16},{56,24},{64... | collective-permute-start | bytes 1572872 | tf_op jit(solution)/shard_map/ppermute | solution.py:235
  40.4 14.8 %collective-permute-start.6 = (bf16[256,1024]{1,0:T(8,128)(2,1)}, bf16[256,1024]{1,0:T(8,128)(2,1)}, u32[]{:S(2)}, u32[]{:S(2)}) collective-permute-start(bf16[256,1024]{1,0:T(8,128)(2,1)} %collective-permute-done.3.refs_12_), channel_id=1, source_target_pairs={{0,32},{8,40},{16,48},{24,56},{32,64},{40,72},{48,80},{56,88},{64,... | collective-permute-start | bytes 1572872 | tf_op jit(solution)/shard_map/ppermute | solution.py:235
  42.8 5.7 %collective-permute-start.11 = (bf16[192,128]{1,0:T(8,128)(2,1)S(1)}, bf16[192,128]{1,0:T(8,128)(2,1)S(1)}, u32[]{:S(2)}, u32[]{:S(2)}) collective-permute-start(bf16[192,128]{1,0:T(8,128)(2,1)S(1)} %get-tuple-element.53), channel_id=1, source_target_pairs={{0,4},{1,5},{2,6},{3,7},{4,0},{5,1},{6,2},{7,3},{8,12},{9,13},{10,... | collective-permute-start | bytes 147464 | tf_op jit(solution)/shard_map/ppermute | solution.py:225
  45.9 4.1 %collective-permute-start.10 = (bf16[192,128]{1,0:T(8,128)(2,1)S(1)}, bf16[192,128]{1,0:T(8,128)(2,1)S(1)}, u32[]{:S(2)}, u32[]{:S(2)}) collective-permute-start(bf16[192,128]{1,0:T(8,128)(2,1)S(1)} %get-tuple-element.53), channel_id=1, source_target_pairs={{0,6},{1,7},{2,0},{3,1},{4,2},{5,3},{6,4},{7,5},{8,14},{9,15},{10,... | collective-permute-start | bytes 147464 | tf_op jit(solution)/shard_map/ppermute | solution.py:225
  47.1 5.3 %collective-permute-start.9 = (bf16[192,128]{1,0:T(8,128)(2,1)S(1)}, bf16[192,128]{1,0:T(8,128)(2,1)S(1)}, u32[]{:S(2)}, u32[]{:S(2)}) collective-permute-start(bf16[192,128]{1,0:T(8,128)(2,1)S(1)} %get-tuple-element.53), channel_id=1, source_target_pairs={{0,2},{1,3},{2,4},{3,5},{4,6},{5,7},{6,0},{7,1},{8,10},{9,11},{10,... | collective-permute-start | bytes 147464 | tf_op jit(solution)/shard_map/ppermute | solution.py:225
  55.2 17.3 %all-to-all-start.1 = ((bf16[16,96,256]{2,1,0:T(8,128)(2,1)}), bf16[16,96,256]{2,1,0:T(8,128)(2,1)S(1)}, u32[]{:S(2)}, u32[]{:S(2)}) async-start(bf16[16,96,256]{2,1,0:T(8,128)(2,1)} %copy-done.2), calls=%async_computation.1 | async-start | bytes 1572864 | tf_op jit(solution)/shard_map/all_to_all | solution.py:387
  59.3 13.2 %collective-permute-start.2 = (s32[1,128]{1,0:T(1,128)S(1)}, s32[1,128]{1,0:T(1,128)S(1)}, u32[]{:S(2)}, u32[]{:S(2)}) collective-permute-start(s32[1,128]{1,0:T(1,128)S(1)} %get-tuple-element.27.refs_0_), channel_id=1, source_target_pairs={{0,8},{8,16},{16,24},{24,0},{32,40},{40,48},{48,56},{56,32},{64,72... | collective-permute-start | bytes 1544 | tf_op jit(solution)/shard_map/ppermute | solution.py:229
  61.2 11.3 %collective-permute-start.1 = (s32[1,128]{1,0:T(1,128)S(1)}, s32[1,128]{1,0:T(1,128)S(1)}, u32[]{:S(2)}, u32[]{:S(2)}) collective-permute-start(s32[1,128]{1,0:T(1,128)S(1)} %get-tuple-element.27.refs_0_), channel_id=1, source_target_pairs={{0,16},{8,24},{16,0},{24,8},{32,48},{40,56},{48,32},{56,40},{64,80... | collective-permute-start | bytes 1544 | tf_op jit(solution)/shard_map/ppermute | solution.py:229
  63.9 8.6 %collective-permute-start = (s32[1,128]{1,0:T(1,128)S(1)}, s32[1,128]{1,0:T(1,128)S(1)}, u32[]{:S(2)}, u32[]{:S(2)}) collective-permute-start(s32[1,128]{1,0:T(1,128)S(1)} %get-tuple-element.27.refs_0_), channel_id=1, source_target_pairs={{0,24},{8,0},{16,8},{24,16},{32,56},{40,32},{48,40},{56,48},{64,88... | collective-permute-start | bytes 1544 | tf_op jit(solution)/shard_map/ppermute | solution.py:229
  72.9 10.7 %collective-permute-start.14 = (bf16[512,256]{1,0:T(8,128)(2,1)S(1)}, bf16[512,256]{1,0:T(8,128)(2,1)S(1)}, u32[]{:S(2)}, u32[]{:S(2)}) collective-permute-start(bf16[512,256]{1,0:T(8,128)(2,1)S(1)} %compact.1.refs_0_), channel_id=1, source_target_pairs={{0,4},{1,5},{2,6},{3,7},{4,0},{5,1},{6,2},{7,3},{8,12},{9,13},{10,... | collective-permute-start | bytes 786440 | tf_op jit(solution)/shard_map/ppermute | solution.py:225
  74.0 13.2 %collective-permute-start.13 = (bf16[512,256]{1,0:T(8,128)(2,1)S(1)}, bf16[512,256]{1,0:T(8,128)(2,1)}, u32[]{:S(2)}, u32[]{:S(2)}) collective-permute-start(bf16[512,256]{1,0:T(8,128)(2,1)S(1)} %compact.1.refs_0_), channel_id=1, source_target_pairs={{0,6},{1,7},{2,0},{3,1},{4,2},{5,3},{6,4},{7,5},{8,14},{9,15},{10,... | collective-permute-start | bytes 786440 | tf_op jit(solution)/shard_map/ppermute | solution.py:225
  75.6 13.3 %collective-permute-start.12 = (bf16[512,256]{1,0:T(8,128)(2,1)S(1)}, bf16[512,256]{1,0:T(8,128)(2,1)}, u32[]{:S(2)}, u32[]{:S(2)}) collective-permute-start(bf16[512,256]{1,0:T(8,128)(2,1)S(1)} %compact.1.refs_0_), channel_id=1, source_target_pairs={{0,2},{1,3},{2,4},{3,5},{4,6},{5,7},{6,0},{7,1},{8,10},{9,11},{10,... | collective-permute-start | bytes 786440 | tf_op jit(solution)/shard_map/ppermute | solution.py:225
  76.0 14.8 %collective-permute-start.19 = (bf16[256,1024]{1,0:T(8,128)(2,1)}, bf16[256,1024]{1,0:T(8,128)(2,1)S(1)}, u32[]{:S(2)}, u32[]{:S(2)}) collective-permute-start(bf16[256,1024]{1,0:T(8,128)(2,1)} %copy-done.8), channel_id=1, source_target_pairs={{0,32},{8,40},{16,48},{24,56},{32,64},{40,72},{48,80},{56,88},{64,... | collective-permute-start | bytes 1572872 | tf_op jit(solution)/shard_map/ppermute | solution.py:235
  76.0 14.8 %collective-permute-start.20 = (bf16[256,1024]{1,0:T(8,128)(2,1)}, bf16[256,1024]{1,0:T(8,128)(2,1)}, u32[]{:S(2)}, u32[]{:S(2)}) collective-permute-start(bf16[256,1024]{1,0:T(8,128)(2,1)} %collective-permute-done.7.refs_14_), channel_id=1, source_target_pairs={{0,96},{8,104},{16,112},{24,120},{32,0},{40,8},{48,16},{56,24},{64... | collective-permute-start | bytes 1572872 | tf_op jit(solution)/shard_map/ppermute | solution.py:235
  83.6 5.3 %collective-permute-start.18 = (bf16[512,256]{1,0:T(8,128)(2,1)S(1)}, bf16[512,256]{1,0:T(8,128)(2,1)}, u32[]{:S(2)}, u32[]{:S(2)}) collective-permute-start(bf16[512,256]{1,0:T(8,128)(2,1)S(1)} %collective-permute-done.14.refs_3_), channel_id=1, source_target_pairs={{0,1},{1,0},{2,3},{3,2},{4,5},{5,4},{6,7},{7,6},{8,9},{9,8},{10,11... | collective-permute-start | bytes 786440 | tf_op jit(solution)/shard_map/ppermute | solution.py:225
  95.6 15.3 %collective-permute-start.21 = (bf16[128,1024]{1,0:T(8,128)(2,1)S(1)}, bf16[128,1024]{1,0:T(8,128)(2,1)S(1)}, u32[]{:S(2)}, u32[]{:S(2)}) collective-permute-start(bf16[128,1024]{1,0:T(8,128)(2,1)S(1)} %get-tuple-element.44), channel_id=1, source_target_pairs={{0,8},{8,16},{16,24},{24,0},{32,40},{40,48},{48,56},{56,32},{64,72... | collective-permute-start | bytes 786440 | tf_op jit(solution)/shard_map/ppermute | solution.py:229
  96.4 14.5 %collective-permute-start.22 = (bf16[128,1024]{1,0:T(8,128)(2,1)S(1)}, bf16[128,1024]{1,0:T(8,128)(2,1)S(1)}, u32[]{:S(2)}, u32[]{:S(2)}) collective-permute-start(bf16[128,1024]{1,0:T(8,128)(2,1)S(1)} %get-tuple-element.45), channel_id=1, source_target_pairs={{0,24},{8,0},{16,8},{24,16},{32,56},{40,32},{48,40},{56,48},{64,88... | collective-permute-start | bytes 786440 | tf_op jit(solution)/shard_map/ppermute | solution.py:229
  99.1 11.8 %collective-permute-start.23 = (bf16[128,1024]{1,0:T(8,128)(2,1)S(1)}, bf16[128,1024]{1,0:T(8,128)(2,1)S(1)}, u32[]{:S(2)}, u32[]{:S(2)}) collective-permute-start(bf16[128,1024]{1,0:T(8,128)(2,1)S(1)} %get-tuple-element.46), channel_id=1, source_target_pairs={{0,16},{8,24},{16,0},{24,8},{32,48},{40,56},{48,32},{56,40},{64,80... | collective-permute-start | bytes 786440 | tf_op jit(solution)/shard_map/ppermute | solution.py:229
  130.5 5.7 %collective-permute-start.27 = (bf16[192,128]{1,0:T(8,128)(2,1)S(1)}, bf16[192,128]{1,0:T(8,128)(2,1)S(1)}, u32[]{:S(2)}, u32[]{:S(2)}) collective-permute-start(bf16[192,128]{1,0:T(8,128)(2,1)S(1)} %get-tuple-element.51), channel_id=1, source_target_pairs={{0,4},{1,5},{2,6},{3,7},{4,0},{5,1},{6,2},{7,3},{8,12},{9,13},{10,... | collective-permute-start | bytes 147464 | tf_op jit(solution)/shard_map/ppermute | solution.py:225
  133.1 4.1 %collective-permute-start.26 = (bf16[192,128]{1,0:T(8,128)(2,1)S(1)}, bf16[192,128]{1,0:T(8,128)(2,1)S(1)}, u32[]{:S(2)}, u32[]{:S(2)}) collective-permute-start(bf16[192,128]{1,0:T(8,128)(2,1)S(1)} %get-tuple-element.51), channel_id=1, source_target_pairs={{0,6},{1,7},{2,0},{3,1},{4,2},{5,3},{6,4},{7,5},{8,14},{9,15},{10,... | collective-permute-start | bytes 147464 | tf_op jit(solution)/shard_map/ppermute | solution.py:225
  134.5 5.3 %collective-permute-start.25 = (bf16[192,128]{1,0:T(8,128)(2,1)S(1)}, bf16[192,128]{1,0:T(8,128)(2,1)S(1)}, u32[]{:S(2)}, u32[]{:S(2)}) collective-permute-start(bf16[192,128]{1,0:T(8,128)(2,1)S(1)} %get-tuple-element.51), channel_id=1, source_target_pairs={{0,2},{1,3},{2,4},{3,5},{4,6},{5,7},{6,0},{7,1},{8,10},{9,11},{10,... | collective-permute-start | bytes 147464 | tf_op jit(solution)/shard_map/ppermute | solution.py:225
  (14 other events, 174.3 us)

commit v6 on v5

--- a/solution.py
+++ b/solution.py
@@ -21,7 +21,7 @@
 PART = SLOTS * MOST
 PACKED = ROWS * PART
 BLOCK = 128
-TILE = 512
+TILE = 1024
 CHUNK = 32
 WIDTH = 1024
 QUARTER = WIDTH // RING

time: 158 us -> 158 us (level)
  no operation moved by 1% of the time
where the time goes in v6:
time: 158 us; the launch traced here: 157 us
  blocking collectives  49.1 us (31%)
  waiting for transfers between devices  47.7 us (30%)
  starting transfers between devices  39.2 us (25%)
  Pallas kernels  17.1 us (11%)
  local copies, waits for them, and re-layouts  2.22 us (1%)
    all_to_all x2, blocking collectives, dispatch(): lax.all_to_all(packed, 'row', 0, 0, tiled=True).reshape(PACKED, WIDTH)  33.2 us
    ppermute x15, waiting for transfers between devices, along_col(): return lax.ppermute(values, 'col', [(i, move(i)) for i in range(8)])  23.1 us
    all_to_all x1, blocking collectives, local(): lax.all_to_all(erased.reshape(ROWS, PART, WIDTH), 'row', 0, 0, tiled=True)  15.9 us
    ppermute x15, starting transfers between devices, along_col(): return lax.ppermute(values, 'col', [(i, move(i)) for i in range(8)])  12.8 us
    ppermute x6, waiting for transfers between devices, along_y(): lax.ppermute(values, 'row', [(i, i // RING * RING + (i + step) % RING) fo...  11.8 us
    ppermute x6, starting transfers between devices, along_y(): lax.ppermute(values, 'row', [(i, i // RING * RING + (i + step) % RING) fo...  9.55 us
    ppermute x6, starting transfers between devices, along_z(): lax.ppermute(values, 'row', [(i, (i + RING * step) % ROWS) for i in range...  9.37 us
    pallas_call x1, Pallas kernels, attend_and_pack(): pl.pallas_call(attend_body, grid=(BLOCK // CHUNK,), in_specs=[by_row(WIDT...  8.51 us
  transfers between devices with their start and end apart: 29, of which 18 were waited for; matrix products, arithmetic and copies ran while one was open for 0% of the time, Pallas kernels for 7%

profile of v6, /device:TPU:0, one launch (start us, length us, event | category | flops | bytes accessed | tf_op | source)
XLA Modules:
  0.0 157.4 jit_solution(3615369381044000694)
XLA Ops:
  1.3 3.4 %collective-permute-start.3 = (bf16[256,1024]{1,0:T(8,128)(2,1)S(1)}, bf16[256,1024]{1,0:T(8,128)(2,1)}, u32[]{:S(2)}, u32[]{:S(2)}) collective-permute-start(bf16[256,1024]{1,0:T(8,128)(2,1)S(1)} %get-tuple-element.56), channel_id=1, source_target_pairs={{0,16},{8,24},{16,0},{24,8},{32,48},{40,56},{48,32},{56,40},{64,80... | collective-permute-start | bytes 1572872 | tf_op jit(solution)/shard_map/ppermute | solution.py:365
  4.7 4.0 %collective-permute-start.5 = (bf16[256,1024]{1,0:T(8,128)(2,1)S(1)}, bf16[256,1024]{1,0:T(8,128)(2,1)S(1)}, u32[]{:S(2)}, u32[]{:S(2)}) collective-permute-start(bf16[256,1024]{1,0:T(8,128)(2,1)S(1)} %get-tuple-element.55), channel_id=1, source_target_pairs={{0,96},{8,104},{16,112},{24,120},{32,0},{40,8},{48,16},{56,24},{64... | collective-permute-start | bytes 1572872 | tf_op jit(solution)/shard_map/ppermute | solution.py:235
  8.9 8.5 %attend.1 = (bf16[384,1024]{1,0:T(8,128)(2,1)S(1)}, s32[1,128]{1,0:T(1,128)S(1)}) custom-call(bf16[128,1024]{1,0:T(8,128)(2,1)} %q_ref.1, bf16[128,128]{1,0:T(8,128)(2,1)} %key_ref.1, bf16[128,128]{1,0:T(8,128)(2,1)} %value_ref.1, s32[1,128]{1,0:T(1,128)S(1)} %fusion.3.target_ref, bf16[128,256,128]{2,1,0:T(8,128)(2,1)} %keys_ref.1, ...), custom_call_target="tpu_custom_call" | custom-call | flops 134217728 | bytes 17825792 | tf_op jit(solution)/shard_map/attend/pallas_call | solution.py:91
  17.5 2.1 %collective-permute-done.5.refs_10_ = bf16[256,1024]{1,0:T(8,128)(2,1)S(1)} collective-permute-done((bf16[256,1024]{1,0:T(8,128)(2,1)S(1)}, bf16[256,1024]{1,0:T(8,128)(2,1)S(1)}, u32[]{:S(2)}, u32[]{:S(2)}) %collective-permute-start.5) | collective-permute-done | bytes 524320 | tf_op jit(solution)/shard_map/ppermute | solution.py:235
  19.6 3.4 %collective-permute-done.4.refs_9_ = bf16[256,1024]{1,0:T(8,128)(2,1)S(1)} collective-permute-done((bf16[256,1024]{1,0:T(8,128)(2,1)S(1)}, bf16[256,1024]{1,0:T(8,128)(2,1)S(1)}, u32[]{:S(2)}, u32[]{:S(2)}) %collective-permute-start.4) | collective-permute-done | bytes 524320 | tf_op jit(solution)/shard_map/ppermute | solution.py:235
  23.0 15.8 %all_to_all.20 = bf16[16,24,1024]{2,1,0:T(8,128)(2,1)S(1)} all-to-all(bf16[16,24,1024]{2,1,0:T(8,128)(2,1)S(1)} %bitcast.40), channel_id=1, replica_groups=mesh['row'=16,'col'=8] {'row'}, dimensions={0} | all-to-all | bytes 1572864 | tf_op jit(solution)/shard_map/all_to_all | solution.py:371
  42.8 3.1 %collective-permute-start.11 = (bf16[192,128]{1,0:T(8,128)(2,1)S(1)}, bf16[192,128]{1,0:T(8,128)(2,1)S(1)}, u32[]{:S(2)}, u32[]{:S(2)}) collective-permute-start(bf16[192,128]{1,0:T(8,128)(2,1)S(1)} %get-tuple-element.53), channel_id=1, source_target_pairs={{0,4},{1,5},{2,6},{3,7},{4,0},{5,1},{6,2},{7,3},{8,12},{9,13},{10,... | collective-permute-start | bytes 147464 | tf_op jit(solution)/shard_map/ppermute | solution.py:225
  50.0 2.3 %collective-permute-done.9.sum1_ref = bf16[192,128]{1,0:T(8,128)(2,1)S(1)} collective-permute-done((bf16[192,128]{1,0:T(8,128)(2,1)S(1)}, bf16[192,128]{1,0:T(8,128)(2,1)S(1)}, u32[]{:S(2)}, u32[]{:S(2)}) %collective-permute-start.9) | collective-permute-done | bytes 49184 | tf_op jit(solution)/shard_map/ppermute | solution.py:225
  52.4 1.9 %erase.2 = bf16[16,96,256]{2,1,0:T(8,128)(2,1)S(1)} custom-call(s32[1]{0:T(128)} %bitcast.9.core_ref, bf16[384,1024]{1,0:T(8,128)(2,1)S(1)} %bitcast.36, f32[192,128]{1,0:T(8,128)S(1)} %get-tuple-element.54.sum_ref, bf16[192,128]{1,0:T(8,128)(2,1)S(1)} %collective-permute-done.9.sum1_ref, bf16[192,128]{1,0:T(8,128)(2,1)S(1)} %collective-permute-done.10.sum2_ref, ...), custom_call_target="tpu_custom_call" | custom-call | flops 402653184 | bytes 3145728 | tf_op jit(solution)/shard_map/erase/pallas_call | solution.py:205
  55.2 4.1 %all-to-all-start.1 = ((bf16[16,96,256]{2,1,0:T(8,128)(2,1)}), bf16[16,96,256]{2,1,0:T(8,128)(2,1)S(1)}, u32[]{:S(2)}, u32[]{:S(2)}) async-start(bf16[16,96,256]{2,1,0:T(8,128)(2,1)} %copy-done.2), calls=%async_computation.1 | async-start | bytes 1572864 | tf_op jit(solution)/shard_map/all_to_all | solution.py:387
  59.3 1.9 %collective-permute-start.2 = (s32[1,128]{1,0:T(1,128)S(1)}, s32[1,128]{1,0:T(1,128)S(1)}, u32[]{:S(2)}, u32[]{:S(2)}) collective-permute-start(s32[1,128]{1,0:T(1,128)S(1)} %get-tuple-element.27.refs_0_), channel_id=1, source_target_pairs={{0,8},{8,16},{16,24},{24,0},{32,40},{40,48},{48,56},{56,32},{64,72... | collective-permute-start | bytes 1544 | tf_op jit(solution)/shard_map/ppermute | solution.py:229
  61.2 2.7 %collective-permute-start.1 = (s32[1,128]{1,0:T(1,128)S(1)}, s32[1,128]{1,0:T(1,128)S(1)}, u32[]{:S(2)}, u32[]{:S(2)}) collective-permute-start(s32[1,128]{1,0:T(1,128)S(1)} %get-tuple-element.27.refs_0_), channel_id=1, source_target_pairs={{0,16},{8,24},{16,0},{24,8},{32,48},{40,56},{48,32},{56,40},{64,80... | collective-permute-start | bytes 1544 | tf_op jit(solution)/shard_map/ppermute | solution.py:229
  65.3 7.1 %all-to-all-done.1.refs_4_ = bf16[16,96,256]{2,1,0:T(8,128)(2,1)S(1)} async-done(((bf16[16,96,256]{2,1,0:T(8,128)(2,1)}), bf16[16,96,256]{2,1,0:T(8,128)(2,1)S(1)}, u32[]{:S(2)}, u32[]{:S(2)}) %all-to-all-start.1) | async-done | bytes 786464 | tf_op jit(solution)/shard_map/all_to_all | solution.py:387
  76.0 3.2 %collective-permute-start.20 = (bf16[256,1024]{1,0:T(8,128)(2,1)}, bf16[256,1024]{1,0:T(8,128)(2,1)}, u32[]{:S(2)}, u32[]{:S(2)}) collective-permute-start(bf16[256,1024]{1,0:T(8,128)(2,1)} %collective-permute-done.7.refs_14_), channel_id=1, source_target_pairs={{0,96},{8,104},{16,112},{24,120},{32,0},{40,8},{48,16},{56,24},{64... | collective-permute-start | bytes 1572872 | tf_op jit(solution)/shard_map/ppermute | solution.py:235
  79.3 4.4 %collective-permute-done.14.refs_3_ = bf16[512,256]{1,0:T(8,128)(2,1)S(1)} collective-permute-done((bf16[512,256]{1,0:T(8,128)(2,1)S(1)}, bf16[512,256]{1,0:T(8,128)(2,1)S(1)}, u32[]{:S(2)}, u32[]{:S(2)}) %collective-permute-start.14) | collective-permute-done | bytes 262176 | tf_op jit(solution)/shard_map/ppermute | solution.py:225
  83.6 3.6 %collective-permute-done.13.refs_2_ = bf16[512,256]{1,0:T(8,128)(2,1)} collective-permute-done((bf16[512,256]{1,0:T(8,128)(2,1)S(1)}, bf16[512,256]{1,0:T(8,128)(2,1)}, u32[]{:S(2)}, u32[]{:S(2)}) %collective-permute-start.13) | collective-permute-done | bytes 262176 | tf_op jit(solution)/shard_map/ppermute | solution.py:225
  90.9 4.4 %project.1 = (bf16[128,1024]{1,0:T(8,128)(2,1)S(1)}, bf16[128,1024]{1,0:T(8,128)(2,1)S(1)}, bf16[128,1024]{1,0:T(8,128)(2,1)S(1)}, f32[128,1024]{1,0:T(8,128)S(1)}) custom-call(s32[3]{0:T(128)S(1)} %pad_add_fusion.place_ref, bf16[512,256]{1,0:T(8,128)(2,1)S(1)} %compact.1.refs_0_, bf16[512,256]{1,0:T(8,128)(2,1)} %collective-permute-done.12.refs_1_, ...), custom_call_target="tpu_custom_call" | custom-call | flops 2147483648 | bytes 7340032 | tf_op jit(solution)/shard_map/project/pallas_call | solution.py:325
  96.1 2.7 %collective-permute-start.22 = (bf16[128,1024]{1,0:T(8,128)(2,1)S(1)}, bf16[128,1024]{1,0:T(8,128)(2,1)S(1)}, u32[]{:S(2)}, u32[]{:S(2)}) collective-permute-start(bf16[128,1024]{1,0:T(8,128)(2,1)S(1)} %get-tuple-element.45), channel_id=1, source_target_pairs={{0,24},{8,0},{16,8},{24,16},{32,56},{40,32},{48,40},{56,48},{64,88... | collective-permute-start | bytes 786440 | tf_op jit(solution)/shard_map/ppermute | solution.py:229
  98.8 11.8 %collective-permute-done.21 = bf16[128,1024]{1,0:T(8,128)(2,1)S(1)} collective-permute-done((bf16[128,1024]{1,0:T(8,128)(2,1)S(1)}, bf16[128,1024]{1,0:T(8,128)(2,1)S(1)}, u32[]{:S(2)}, u32[]{:S(2)}) %collective-permute-start.21) | collective-permute-done | bytes 262176 | tf_op jit(solution)/shard_map/ppermute | solution.py:229
  111.0 17.4 %all_to_all.21 = bf16[16,24,1024]{2,1,0:T(8,128)(2,1)S(1)} all-to-all(bf16[16,24,1024]{2,1,0:T(8,128)(2,1)S(1)} %bitcast.43), channel_id=1, replica_groups=mesh['row'=16,'col'=8] {'row'}, dimensions={0} | all-to-all | bytes 1572864 | tf_op jit(solution)/shard_map/all_to_all | solution.py:371
  130.5 2.4 %collective-permute-start.27 = (bf16[192,128]{1,0:T(8,128)(2,1)S(1)}, bf16[192,128]{1,0:T(8,128)(2,1)S(1)}, u32[]{:S(2)}, u32[]{:S(2)}) collective-permute-start(bf16[192,128]{1,0:T(8,128)(2,1)S(1)} %get-tuple-element.51), channel_id=1, source_target_pairs={{0,4},{1,5},{2,6},{3,7},{4,0},{5,1},{6,2},{7,3},{8,12},{9,13},{10,... | collective-permute-start | bytes 147464 | tf_op jit(solution)/shard_map/ppermute | solution.py:225
  132.9 1.6 %collective-permute-start.26 = (bf16[192,128]{1,0:T(8,128)(2,1)S(1)}, bf16[192,128]{1,0:T(8,128)(2,1)S(1)}, u32[]{:S(2)}, u32[]{:S(2)}) collective-permute-start(bf16[192,128]{1,0:T(8,128)(2,1)S(1)} %get-tuple-element.51), channel_id=1, source_target_pairs={{0,6},{1,7},{2,0},{3,1},{4,2},{5,3},{6,4},{7,5},{8,14},{9,15},{10,... | collective-permute-start | bytes 147464 | tf_op jit(solution)/shard_map/ppermute | solution.py:225
  137.0 2.8 %collective-permute-done.25.sum1_ref = bf16[192,128]{1,0:T(8,128)(2,1)S(1)} collective-permute-done((bf16[192,128]{1,0:T(8,128)(2,1)S(1)}, bf16[192,128]{1,0:T(8,128)(2,1)S(1)}, u32[]{:S(2)}, u32[]{:S(2)}) %collective-permute-start.25) | collective-permute-done | bytes 49184 | tf_op jit(solution)/shard_map/ppermute | solution.py:225
  140.4 15.9 %all_to_all.22 = bf16[16,24,1024]{2,1,0:T(8,128)(2,1)S(1)} all-to-all(bf16[16,24,1024]{2,1,0:T(8,128)(2,1)S(1)} %bitcast.39), channel_id=1, replica_groups=mesh['row'=16,'col'=8] {'row'}, dimensions={0} | all-to-all | bytes 1572864 | tf_op jit(solution)/shard_map/all_to_all | solution.py:407
  (70 shorter events, 26.6 us)
Async XLA Ops:
  1.3 16.1 %collective-permute-start.3 = (bf16[256,1024]{1,0:T(8,128)(2,1)S(1)}, bf16[256,1024]{1,0:T(8,128)(2,1)}, u32[]{:S(2)}, u32[]{:S(2)}) collective-permute-start(bf16[256,1024]{1,0:T(8,128)(2,1)S(1)} %get-tuple-element.56), channel_id=1, source_target_pairs={{0,16},{8,24},{16,0},{24,8},{32,48},{40,56},{48,32},{56,40},{64,80... | collective-permute-start | bytes 1572872 | tf_op jit(solution)/shard_map/ppermute | solution.py:365
  4.7 14.9 %collective-permute-start.5 = (bf16[256,1024]{1,0:T(8,128)(2,1)S(1)}, bf16[256,1024]{1,0:T(8,128)(2,1)S(1)}, u32[]{:S(2)}, u32[]{:S(2)}) collective-permute-start(bf16[256,1024]{1,0:T(8,128)(2,1)S(1)} %get-tuple-element.55), channel_id=1, source_target_pairs={{0,96},{8,104},{16,112},{24,120},{32,0},{40,8},{48,16},{56,24},{64... | collective-permute-start | bytes 1572872 | tf_op jit(solution)/shard_map/ppermute | solution.py:235
  8.7 14.3 %collective-permute-start.4 = (bf16[256,1024]{1,0:T(8,128)(2,1)S(1)}, bf16[256,1024]{1,0:T(8,128)(2,1)S(1)}, u32[]{:S(2)}, u32[]{:S(2)}) collective-permute-start(bf16[256,1024]{1,0:T(8,128)(2,1)S(1)} %get-tuple-element.55), channel_id=1, source_target_pairs={{0,32},{8,40},{16,48},{24,56},{32,64},{40,72},{48,80},{56,88},{64,... | collective-permute-start | bytes 1572872 | tf_op jit(solution)/shard_map/ppermute | solution.py:235
  39.5 15.7 %collective-permute-start.7 = (bf16[256,1024]{1,0:T(8,128)(2,1)}, bf16[256,1024]{1,0:T(8,128)(2,1)}, u32[]{:S(2)}, u32[]{:S(2)}) collective-permute-start(bf16[256,1024]{1,0:T(8,128)(2,1)} %collective-permute-done.3.refs_12_), channel_id=1, source_target_pairs={{0,96},{8,104},{16,112},{24,120},{32,0},{40,8},{48,16},{56,24},{64... | collective-permute-start | bytes 1572872 | tf_op jit(solution)/shard_map/ppermute | solution.py:235
  40.4 14.8 %collective-permute-start.6 = (bf16[256,1024]{1,0:T(8,128)(2,1)}, bf16[256,1024]{1,0:T(8,128)(2,1)}, u32[]{:S(2)}, u32[]{:S(2)}) collective-permute-start(bf16[256,1024]{1,0:T(8,128)(2,1)} %collective-permute-done.3.refs_12_), channel_id=1, source_target_pairs={{0,32},{8,40},{16,48},{24,56},{32,64},{40,72},{48,80},{56,88},{64,... | collective-permute-start | bytes 1572872 | tf_op jit(solution)/shard_map/ppermute | solution.py:235
  42.8 5.7 %collective-permute-start.11 = (bf16[192,128]{1,0:T(8,128)(2,1)S(1)}, bf16[192,128]{1,0:T(8,128)(2,1)S(1)}, u32[]{:S(2)}, u32[]{:S(2)}) collective-permute-start(bf16[192,128]{1,0:T(8,128)(2,1)S(1)} %get-tuple-element.53), channel_id=1, source_target_pairs={{0,4},{1,5},{2,6},{3,7},{4,0},{5,1},{6,2},{7,3},{8,12},{9,13},{10,... | collective-permute-start | bytes 147464 | tf_op jit(solution)/shard_map/ppermute | solution.py:225
  45.9 4.1 %collective-permute-start.10 = (bf16[192,128]{1,0:T(8,128)(2,1)S(1)}, bf16[192,128]{1,0:T(8,128)(2,1)S(1)}, u32[]{:S(2)}, u32[]{:S(2)}) collective-permute-start(bf16[192,128]{1,0:T(8,128)(2,1)S(1)} %get-tuple-element.53), channel_id=1, source_target_pairs={{0,6},{1,7},{2,0},{3,1},{4,2},{5,3},{6,4},{7,5},{8,14},{9,15},{10,... | collective-permute-start | bytes 147464 | tf_op jit(solution)/shard_map/ppermute | solution.py:225
  47.1 5.3 %collective-permute-start.9 = (bf16[192,128]{1,0:T(8,128)(2,1)S(1)}, bf16[192,128]{1,0:T(8,128)(2,1)S(1)}, u32[]{:S(2)}, u32[]{:S(2)}) collective-permute-start(bf16[192,128]{1,0:T(8,128)(2,1)S(1)} %get-tuple-element.53), channel_id=1, source_target_pairs={{0,2},{1,3},{2,4},{3,5},{4,6},{5,7},{6,0},{7,1},{8,10},{9,11},{10,... | collective-permute-start | bytes 147464 | tf_op jit(solution)/shard_map/ppermute | solution.py:225
  55.2 17.3 %all-to-all-start.1 = ((bf16[16,96,256]{2,1,0:T(8,128)(2,1)}), bf16[16,96,256]{2,1,0:T(8,128)(2,1)S(1)}, u32[]{:S(2)}, u32[]{:S(2)}) async-start(bf16[16,96,256]{2,1,0:T(8,128)(2,1)} %copy-done.2), calls=%async_computation.1 | async-start | bytes 1572864 | tf_op jit(solution)/shard_map/all_to_all | solution.py:387
  59.3 13.2 %collective-permute-start.2 = (s32[1,128]{1,0:T(1,128)S(1)}, s32[1,128]{1,0:T(1,128)S(1)}, u32[]{:S(2)}, u32[]{:S(2)}) collective-permute-start(s32[1,128]{1,0:T(1,128)S(1)} %get-tuple-element.27.refs_0_), channel_id=1, source_target_pairs={{0,8},{8,16},{16,24},{24,0},{32,40},{40,48},{48,56},{56,32},{64,72... | collective-permute-start | bytes 1544 | tf_op jit(solution)/shard_map/ppermute | solution.py:229
  61.2 11.3 %collective-permute-start.1 = (s32[1,128]{1,0:T(1,128)S(1)}, s32[1,128]{1,0:T(1,128)S(1)}, u32[]{:S(2)}, u32[]{:S(2)}) collective-permute-start(s32[1,128]{1,0:T(1,128)S(1)} %get-tuple-element.27.refs_0_), channel_id=1, source_target_pairs={{0,16},{8,24},{16,0},{24,8},{32,48},{40,56},{48,32},{56,40},{64,80... | collective-permute-start | bytes 1544 | tf_op jit(solution)/shard_map/ppermute | solution.py:229
  63.9 8.6 %collective-permute-start = (s32[1,128]{1,0:T(1,128)S(1)}, s32[1,128]{1,0:T(1,128)S(1)}, u32[]{:S(2)}, u32[]{:S(2)}) collective-permute-start(s32[1,128]{1,0:T(1,128)S(1)} %get-tuple-element.27.refs_0_), channel_id=1, source_target_pairs={{0,24},{8,0},{16,8},{24,16},{32,56},{40,32},{48,40},{56,48},{64,88... | collective-permute-start | bytes 1544 | tf_op jit(solution)/shard_map/ppermute | solution.py:229
  72.9 10.7 %collective-permute-start.14 = (bf16[512,256]{1,0:T(8,128)(2,1)S(1)}, bf16[512,256]{1,0:T(8,128)(2,1)S(1)}, u32[]{:S(2)}, u32[]{:S(2)}) collective-permute-start(bf16[512,256]{1,0:T(8,128)(2,1)S(1)} %compact.1.refs_0_), channel_id=1, source_target_pairs={{0,4},{1,5},{2,6},{3,7},{4,0},{5,1},{6,2},{7,3},{8,12},{9,13},{10,... | collective-permute-start | bytes 786440 | tf_op jit(solution)/shard_map/ppermute | solution.py:225
  74.0 13.2 %collective-permute-start.13 = (bf16[512,256]{1,0:T(8,128)(2,1)S(1)}, bf16[512,256]{1,0:T(8,128)(2,1)}, u32[]{:S(2)}, u32[]{:S(2)}) collective-permute-start(bf16[512,256]{1,0:T(8,128)(2,1)S(1)} %compact.1.refs_0_), channel_id=1, source_target_pairs={{0,6},{1,7},{2,0},{3,1},{4,2},{5,3},{6,4},{7,5},{8,14},{9,15},{10,... | collective-permute-start | bytes 786440 | tf_op jit(solution)/shard_map/ppermute | solution.py:225
  75.6 13.3 %collective-permute-start.12 = (bf16[512,256]{1,0:T(8,128)(2,1)S(1)}, bf16[512,256]{1,0:T(8,128)(2,1)}, u32[]{:S(2)}, u32[]{:S(2)}) collective-permute-start(bf16[512,256]{1,0:T(8,128)(2,1)S(1)} %compact.1.refs_0_), channel_id=1, source_target_pairs={{0,2},{1,3},{2,4},{3,5},{4,6},{5,7},{6,0},{7,1},{8,10},{9,11},{10,... | collective-permute-start | bytes 786440 | tf_op jit(solution)/shard_map/ppermute | solution.py:225
  76.0 14.8 %collective-permute-start.19 = (bf16[256,1024]{1,0:T(8,128)(2,1)}, bf16[256,1024]{1,0:T(8,128)(2,1)S(1)}, u32[]{:S(2)}, u32[]{:S(2)}) collective-permute-start(bf16[256,1024]{1,0:T(8,128)(2,1)} %copy-done.8), channel_id=1, source_target_pairs={{0,32},{8,40},{16,48},{24,56},{32,64},{40,72},{48,80},{56,88},{64,... | collective-permute-start | bytes 1572872 | tf_op jit(solution)/shard_map/ppermute | solution.py:235
  76.0 14.8 %collective-permute-start.20 = (bf16[256,1024]{1,0:T(8,128)(2,1)}, bf16[256,1024]{1,0:T(8,128)(2,1)}, u32[]{:S(2)}, u32[]{:S(2)}) collective-permute-start(bf16[256,1024]{1,0:T(8,128)(2,1)} %collective-permute-done.7.refs_14_), channel_id=1, source_target_pairs={{0,96},{8,104},{16,112},{24,120},{32,0},{40,8},{48,16},{56,24},{64... | collective-permute-start | bytes 1572872 | tf_op jit(solution)/shard_map/ppermute | solution.py:235
  83.6 5.3 %collective-permute-start.18 = (bf16[512,256]{1,0:T(8,128)(2,1)S(1)}, bf16[512,256]{1,0:T(8,128)(2,1)}, u32[]{:S(2)}, u32[]{:S(2)}) collective-permute-start(bf16[512,256]{1,0:T(8,128)(2,1)S(1)} %collective-permute-done.14.refs_3_), channel_id=1, source_target_pairs={{0,1},{1,0},{2,3},{3,2},{4,5},{5,4},{6,7},{7,6},{8,9},{9,8},{10,11... | collective-permute-start | bytes 786440 | tf_op jit(solution)/shard_map/ppermute | solution.py:225
  95.3 15.3 %collective-permute-start.21 = (bf16[128,1024]{1,0:T(8,128)(2,1)S(1)}, bf16[128,1024]{1,0:T(8,128)(2,1)S(1)}, u32[]{:S(2)}, u32[]{:S(2)}) collective-permute-start(bf16[128,1024]{1,0:T(8,128)(2,1)S(1)} %get-tuple-element.44), channel_id=1, source_target_pairs={{0,8},{8,16},{16,24},{24,0},{32,40},{40,48},{48,56},{56,32},{64,72... | collective-permute-start | bytes 786440 | tf_op jit(solution)/shard_map/ppermute | solution.py:229
  96.1 14.5 %collective-permute-start.22 = (bf16[128,1024]{1,0:T(8,128)(2,1)S(1)}, bf16[128,1024]{1,0:T(8,128)(2,1)S(1)}, u32[]{:S(2)}, u32[]{:S(2)}) collective-permute-start(bf16[128,1024]{1,0:T(8,128)(2,1)S(1)} %get-tuple-element.45), channel_id=1, source_target_pairs={{0,24},{8,0},{16,8},{24,16},{32,56},{40,32},{48,40},{56,48},{64,88... | collective-permute-start | bytes 786440 | tf_op jit(solution)/shard_map/ppermute | solution.py:229
  98.8 11.8 %collective-permute-start.23 = (bf16[128,1024]{1,0:T(8,128)(2,1)S(1)}, bf16[128,1024]{1,0:T(8,128)(2,1)S(1)}, u32[]{:S(2)}, u32[]{:S(2)}) collective-permute-start(bf16[128,1024]{1,0:T(8,128)(2,1)S(1)} %get-tuple-element.46), channel_id=1, source_target_pairs={{0,16},{8,24},{16,0},{24,8},{32,48},{40,56},{48,32},{56,40},{64,80... | collective-permute-start | bytes 786440 | tf_op jit(solution)/shard_map/ppermute | solution.py:229
  130.5 5.7 %collective-permute-start.27 = (bf16[192,128]{1,0:T(8,128)(2,1)S(1)}, bf16[192,128]{1,0:T(8,128)(2,1)S(1)}, u32[]{:S(2)}, u32[]{:S(2)}) collective-permute-start(bf16[192,128]{1,0:T(8,128)(2,1)S(1)} %get-tuple-element.51), channel_id=1, source_target_pairs={{0,4},{1,5},{2,6},{3,7},{4,0},{5,1},{6,2},{7,3},{8,12},{9,13},{10,... | collective-permute-start | bytes 147464 | tf_op jit(solution)/shard_map/ppermute | solution.py:225
  132.9 4.1 %collective-permute-start.26 = (bf16[192,128]{1,0:T(8,128)(2,1)S(1)}, bf16[192,128]{1,0:T(8,128)(2,1)S(1)}, u32[]{:S(2)}, u32[]{:S(2)}) collective-permute-start(bf16[192,128]{1,0:T(8,128)(2,1)S(1)} %get-tuple-element.51), channel_id=1, source_target_pairs={{0,6},{1,7},{2,0},{3,1},{4,2},{5,3},{6,4},{7,5},{8,14},{9,15},{10,... | collective-permute-start | bytes 147464 | tf_op jit(solution)/shard_map/ppermute | solution.py:225
  134.5 5.3 %collective-permute-start.25 = (bf16[192,128]{1,0:T(8,128)(2,1)S(1)}, bf16[192,128]{1,0:T(8,128)(2,1)S(1)}, u32[]{:S(2)}, u32[]{:S(2)}) collective-permute-start(bf16[192,128]{1,0:T(8,128)(2,1)S(1)} %get-tuple-element.51), channel_id=1, source_target_pairs={{0,2},{1,3},{2,4},{3,5},{4,6},{5,7},{6,0},{7,1},{8,10},{9,11},{10,... | collective-permute-start | bytes 147464 | tf_op jit(solution)/shard_map/ppermute | solution.py:225
  (14 other events, 174.3 us)
